TPU v7x, 32 devices: a whole 2x2x4 slice. The times are simulated.
32 devices in a mesh: grp: 4 (over x, core), row: 8 (over z, y).
Axes of the slice: x: 2, y: 2, z: 4, core: 2. Of those that a mesh axis runs over, the one named last changes fastest.
Arguments:
- rhs: float32 [64, 4096], P(None, ('grp', 'row')), may hold values from -120 to 120
- guess: float32 [64, 4096], P(None, ('grp', 'row')), may hold values from -6 to 6
- diag_blocks: bfloat16 [64, 64, 4096], P(None, None, ('grp', 'row'))
- diag_inverse: bfloat16 [64, 64, 4096], P(None, None, ('grp', 'row'))
- coupling: bfloat16 [64, 64, 4096], P(None, None, ('grp', 'row'))
- prolong: bfloat16 [64, 64, 4096], P(None, None, ('grp', 'row')), may hold values from -0.75 to 0.75
- coarse_inverse: bfloat16 [64, 64, 512], P(None, None, ('grp', 'row'))
- aggregate: int32 [4096], P(('grp', 'row')), may hold values from 0 to 511, as said below
Outputs:
- solution: float32 [64, 4096], P(None, ('grp', 'row'))
- residual: float32 [64, 4096], P(None, ('grp', 'row'))
Inputs may be any that keep to these rules, and one draw needn't show every extreme that they name: The fine blocks held by index g of grp name only the aggregates g * 128 to (g + 1) * 128 - 1, and each aggregate is named by exactly 8 fine blocks.
All inputs are finite; a program needn't handle non-finite values.
Results may differ from a plain program's by a relative error of at most 0.0003.
Values may be sent and summed in bfloat16 or wider, within the bound.
No kernel may reach another device: no remote copies, remote signals or barrier semaphores. Data moves between devices by JAX's collectives and lax.ppermute only.
A program may use at most 64 MiB of HBM per device.

v0:
```python
import jax
import jax.numpy as jnp
from jax import lax
from jax.sharding import PartitionSpec as P

AGG = 8
SWEEPS = 2


def from_behind(block, axis, distance):
    devices = range(lax.axis_size(axis))
    route = [(i - distance, i) for i in devices if i - distance in devices]
    return lax.ppermute(block, axis, route)


def apply_blocks(blocks, vector):
    return jnp.einsum(
        "ijn,jn->in",
        blocks,
        vector,
        precision=lax.Precision.HIGHEST,
        preferred_element_type=jnp.float32,
    )


def apply_transposed(blocks, vector):
    return jnp.einsum(
        "jin,jn->in",
        blocks,
        vector,
        precision=lax.Precision.HIGHEST,
        preferred_element_type=jnp.float32,
    )


def local(rhs, guess, diag_blocks, diag_inverse, coupling, prolong, coarse_inverse, aggregate):
    count = rhs.shape[1]

    def operate(vector):
        before = from_behind(vector[:, -1:], ("grp", "row"), 1)
        lower = jnp.concatenate([before, vector[:, :-1]], axis=1)
        upward = apply_transposed(coupling, vector)
        after = from_behind(upward[:, :1], ("grp", "row"), -1)
        upper = jnp.concatenate([upward[:, 1:], after], axis=1)
        return apply_blocks(diag_blocks, vector) + apply_blocks(coupling, lower) + upper

    def sweep(iterate):
        return iterate + apply_blocks(diag_inverse, rhs - operate(iterate))

    iterate = guess
    for number in range(SWEEPS):
        iterate = sweep(iterate)
    fine_residual = rhs - operate(iterate)
    group_count = count * lax.axis_size("row") // AGG
    first_coarse = lax.axis_index("grp") * group_count
    local_index = aggregate - first_coarse
    selector = (local_index[:, None] == jnp.arange(group_count, dtype=jnp.int32)[None, :]).astype(
        jnp.float32
    )
    pieces = apply_transposed(prolong, fine_residual)
    partial_coarse = jnp.dot(pieces, selector, precision=lax.Precision.HIGHEST)
    share = lax.psum_scatter(partial_coarse, "row", scatter_dimension=1, tiled=True)
    corrected = apply_blocks(coarse_inverse, share)
    spread = jnp.einsum(
        "ic,nc->in",
        lax.all_gather(corrected, "row", axis=1, tiled=True),
        selector,
        precision=lax.Precision.HIGHEST,
    )
    iterate = iterate + apply_blocks(prolong, spread)
    for number in range(SWEEPS):
        iterate = sweep(iterate)
    return (iterate, rhs - operate(iterate))


def solution(mesh):
    return jax.shard_map(
        local,
        mesh=mesh,
        in_specs=(
            P(None, ("grp", "row")),
            P(None, ("grp", "row")),
            P(None, None, ("grp", "row")),
            P(None, None, ("grp", "row")),
            P(None, None, ("grp", "row")),
            P(None, None, ("grp", "row")),
            P(None, None, ("grp", "row")),
            P(("grp", "row")),
        ),
        out_specs=(P(None, ("grp", "row")), P(None, ("grp", "row"))),
        check_vma=False,
    )
```

profile of v0, /device:TPU:29, one launch (start us, length us, event | category | flops | bytes accessed | tf_op | source)
XLA Modules:
  0.0 189.8 jit_solution(13991179022347229462)
XLA Ops:
  7.2 1.6 fusion.16
  8.9 2.1 %collective-permute-start.1 = (f32[64,1]{1,0:T(8,128)S(1)}, f32[64,1]{1,0:T(8,128)S(1)}, u32[]{:S(2)}, u32[]{:S(2)}) collective-permute-start(f32[64,1]{1,0:T(8,128)S(1)} %bitcast.153), channel_id=1, source_target_pairs={{1,0},{2,1},{3,2},{4,3},{5,4},{6,5},{7,6},{8,7},{9,8},{10,9},{11,1... | collective-permute-start | bytes 776 | tf_op jit(solution)/shard_map/ppermute | solution.py:13
  11.1 7.0 %collective-permute-start = (f32[64,1]{1,0:T(8,128)S(1)}, f32[64,1]{1,0:T(8,128)S(1)}, u32[]{:S(2)}, u32[]{:S(2)}) collective-permute-start(f32[64,1]{1,0:T(8,128)S(1)} %slice.72), channel_id=1, source_target_pairs={{0,1},{1,2},{2,3},{3,4},{4,5},{5,6},{6,7},{7,8},{8,9},{9,10},{10,1... | collective-permute-start | bytes 776 | tf_op jit(solution)/shard_map/ppermute | solution.py:13
  18.2 0.3 fusion.4
  18.6 0.7 collective-permute-done
  19.4 0.3 fusion.10
  19.9 0.3 fusion
  20.3 8.0 %collective-permute-start.2 = (f32[64,1]{1,0:T(8,128)S(1)}, f32[64,1]{1,0:T(8,128)S(1)}, u32[]{:S(2)}, u32[]{:S(2)}) collective-permute-start(f32[64,1]{1,0:T(8,128)S(1)} %slice.98), channel_id=1, source_target_pairs={{0,1},{1,2},{2,3},{3,4},{4,5},{5,6},{6,7},{7,8},{8,9},{9,10},{10,1... | collective-permute-start | bytes 776 | tf_op jit(solution)/shard_map/ppermute | solution.py:13
  28.9 1.9 %collective-permute-start.3 = (f32[64,1]{1,0:T(8,128)S(1)}, f32[64,1]{1,0:T(8,128)S(1)}, u32[]{:S(2)}, u32[]{:S(2)}) collective-permute-start(f32[64,1]{1,0:T(8,128)S(1)} %bitcast.156), channel_id=1, source_target_pairs={{1,0},{2,1},{3,2},{4,3},{5,4},{6,5},{7,6},{8,7},{9,8},{10,9},{11,1... | collective-permute-start | bytes 776 | tf_op jit(solution)/shard_map/ppermute | solution.py:13
  31.3 6.5 %collective-permute-done.3 = f32[64,1]{1,0:T(8,128)S(1)} collective-permute-done((f32[64,1]{1,0:T(8,128)S(1)}, f32[64,1]{1,0:T(8,128)S(1)}, u32[]{:S(2)}, u32[]{:S(2)}) %collective-permute-start.3) | collective-permute-done | bytes 288 | tf_op jit(solution)/shard_map/ppermute | solution.py:13
  38.3 1.9 %collective-permute-start.4 = (f32[64,1]{1,0:T(8,128)S(1)}, f32[64,1]{1,0:T(8,128)S(1)}, u32[]{:S(2)}, u32[]{:S(2)}) collective-permute-start(f32[64,1]{1,0:T(8,128)S(1)} %slice.102), channel_id=1, source_target_pairs={{0,1},{1,2},{2,3},{3,4},{4,5},{5,6},{6,7},{7,8},{8,9},{9,10},{10,1... | collective-permute-start | bytes 776 | tf_op jit(solution)/shard_map/ppermute | solution.py:13
  40.5 0.3 fusion.6
  40.9 3.4 %collective-permute-start.5 = (f32[64,1]{1,0:T(8,128)S(1)}, f32[64,1]{1,0:T(8,128)S(1)}, u32[]{:S(2)}, u32[]{:S(2)}) collective-permute-start(f32[64,1]{1,0:T(8,128)S(1)} %bitcast.158), channel_id=1, source_target_pairs={{1,0},{2,1},{3,2},{4,3},{5,4},{6,5},{7,6},{8,7},{9,8},{10,9},{11,1... | collective-permute-start | bytes 776 | tf_op jit(solution)/shard_map/ppermute | solution.py:13
  44.3 0.3 fusion.12
  44.7 5.0 %collective-permute-done.5 = f32[64,1]{1,0:T(8,128)S(1)} collective-permute-done((f32[64,1]{1,0:T(8,128)S(1)}, f32[64,1]{1,0:T(8,128)S(1)}, u32[]{:S(2)}, u32[]{:S(2)}) %collective-permute-start.5) | collective-permute-done | bytes 288 | tf_op jit(solution)/shard_map/ppermute | solution.py:13
  50.0 0.9 convolution_bitcast_fusion
  51.0 57.1 %reduce-scatter.4.cloned.1.call-done = f32[16,64]{1,0:T(8,128)} async-done(((f32[128,64]{1,0:T(8,128)}), f32[16,64]{1,0:T(8,128)}) %reduce-scatter.4.cloned.1.call-update) | async-done | bytes 4112
  108.1 0.9 multiply_reduce_fusion.2
  109.1 24.7 %all_gather.3 = f32[64,128]{0,1:T(8,128)S(1)} all-gather(f32[64,16]{0,1:T(8,128)S(1)} %bitcast.165), channel_id=1, replica_groups=mesh['grp'=4,'row'=8] {'row'}, dimensions={1}, use_global_device_ids=true | all-gather | bytes 36864 | tf_op jit(solution)/shard_map/all_gather | solution.py:66
  134.1 1.6 multiply_reduce_fusion
  135.7 13.2 %collective-permute-start.6 = (f32[64,1]{1,0:T(8,128)S(1)}, f32[64,1]{1,0:T(8,128)S(1)}, u32[]{:S(2)}, u32[]{:S(2)}) collective-permute-start(f32[64,1]{1,0:T(8,128)S(1)} %slice.106), channel_id=1, source_target_pairs={{0,1},{1,2},{2,3},{3,4},{4,5},{5,6},{6,7},{7,8},{8,9},{9,10},{10,1... | collective-permute-start | bytes 776 | tf_op jit(solution)/shard_map/ppermute | solution.py:13
  149.2 0.3 fusion.7
  149.6 1.9 %collective-permute-start.7 = (f32[64,1]{1,0:T(8,128)S(1)}, f32[64,1]{1,0:T(8,128)S(1)}, u32[]{:S(2)}, u32[]{:S(2)}) collective-permute-start(f32[64,1]{1,0:T(8,128)S(1)} %bitcast.160), channel_id=1, source_target_pairs={{1,0},{2,1},{3,2},{4,3},{5,4},{6,5},{7,6},{8,7},{9,8},{10,9},{11,1... | collective-permute-start | bytes 776 | tf_op jit(solution)/shard_map/ppermute | solution.py:13
  151.9 6.5 %collective-permute-done.7 = f32[64,1]{1,0:T(8,128)S(1)} collective-permute-done((f32[64,1]{1,0:T(8,128)S(1)}, f32[64,1]{1,0:T(8,128)S(1)}, u32[]{:S(2)}, u32[]{:S(2)}) %collective-permute-start.7) | collective-permute-done | bytes 288 | tf_op jit(solution)/shard_map/ppermute | solution.py:13
  158.5 0.3 fusion.2
  158.9 1.9 %collective-permute-start.8 = (f32[64,1]{1,0:T(8,128)S(1)}, f32[64,1]{1,0:T(8,128)S(1)}, u32[]{:S(2)}, u32[]{:S(2)}) collective-permute-start(f32[64,1]{1,0:T(8,128)S(1)} %slice.110), channel_id=1, source_target_pairs={{0,1},{1,2},{2,3},{3,4},{4,5},{5,6},{6,7},{7,8},{8,9},{9,10},{10,1... | collective-permute-start | bytes 776 | tf_op jit(solution)/shard_map/ppermute | solution.py:13
  161.5 3.4 %collective-permute-start.9 = (f32[64,1]{1,0:T(8,128)S(1)}, f32[64,1]{1,0:T(8,128)S(1)}, u32[]{:S(2)}, u32[]{:S(2)}) collective-permute-start(f32[64,1]{1,0:T(8,128)S(1)} %bitcast.162), channel_id=1, source_target_pairs={{1,0},{2,1},{3,2},{4,3},{5,4},{6,5},{7,6},{8,7},{9,8},{10,9},{11,1... | collective-permute-start | bytes 776 | tf_op jit(solution)/shard_map/ppermute | solution.py:13
  165.3 5.0 %collective-permute-done.9 = f32[64,1]{1,0:T(8,128)S(1)} collective-permute-done((f32[64,1]{1,0:T(8,128)S(1)}, f32[64,1]{1,0:T(8,128)S(1)}, u32[]{:S(2)}, u32[]{:S(2)}) %collective-permute-start.9) | collective-permute-done | bytes 288 | tf_op jit(solution)/shard_map/ppermute | solution.py:13
  170.9 1.9 %collective-permute-start.10 = (f32[64,1]{1,0:T(8,128)S(1)}, f32[64,1]{1,0:T(8,128)S(1)}, u32[]{:S(2)}, u32[]{:S(2)}) collective-permute-start(f32[64,1]{1,0:T(8,128)S(1)} %slice.114), channel_id=1, source_target_pairs={{0,1},{1,2},{2,3},{3,4},{4,5},{5,6},{6,7},{7,8},{8,9},{9,10},{10,1... | collective-permute-start | bytes 776 | tf_op jit(solution)/shard_map/ppermute | solution.py:13
  173.4 3.4 %collective-permute-start.11 = (f32[64,1]{1,0:T(8,128)S(1)}, f32[64,1]{1,0:T(8,128)S(1)}, u32[]{:S(2)}, u32[]{:S(2)}) collective-permute-start(f32[64,1]{1,0:T(8,128)S(1)} %bitcast.164), channel_id=1, source_target_pairs={{1,0},{2,1},{3,2},{4,3},{5,4},{6,5},{7,6},{8,7},{9,8},{10,9},{11,1... | collective-permute-start | bytes 776 | tf_op jit(solution)/shard_map/ppermute | solution.py:13
  177.3 5.0 %collective-permute-done.11 = f32[64,1]{1,0:T(8,128)S(1)} collective-permute-done((f32[64,1]{1,0:T(8,128)S(1)}, f32[64,1]{1,0:T(8,128)S(1)}, u32[]{:S(2)}, u32[]{:S(2)}) %collective-permute-start.11) | collective-permute-done | bytes 288 | tf_op jit(solution)/shard_map/ppermute | solution.py:13
  182.3 0.7 fusion.32
  (72 shorter events, 6.8 us)
Async XLA Ops:
  7.2 3.9 %copy-start.5 = (f32[64,128]{1,0:T(8,128)S(1)}, f32[64,128]{1,0:T(8,128)}, u32[]{:S(2)}) copy-start(f32[64,128]{1,0:T(8,128)} %param.9) | copy-start | bytes 98308
  7.2 11.0 %copy-start.8 = (s32[128]{0:T(128)S(1)}, s32[128]{0:T(128)}, u32[]{:S(2)}) copy-start(s32[128]{0:T(128)} %param.15) | copy-start | bytes 1540
  7.2 11.0 %copy-start.1 = (bf16[64,64,128]{2,1,0:T(8,128)(2,1)S(1)}, bf16[64,64,128]{2,1,0:T(8,128)(2,1)}, u32[]{:S(2)}) copy-start(bf16[64,64,128]{2,1,0:T(8,128)(2,1)} %param.10) | copy-start | bytes 3145732
  7.2 100.9 %reduce-scatter.4.cloned.1.call-start = ((), (), s32[]{:S(2)}) async-start(), calls=%async_computation.1 | async-start | bytes 73728
  7.2 12.2 %copy-start = (bf16[64,64,128]{2,1,0:T(8,128)(2,1)S(1)}, bf16[64,64,128]{2,1,0:T(8,128)(2,1)}, u32[]{:S(2)}) copy-start(bf16[64,64,128]{2,1,0:T(8,128)(2,1)} %param.12) | copy-start | bytes 3145732
  8.9 10.9 %collective-permute-start.1 = (f32[64,1]{1,0:T(8,128)S(1)}, f32[64,1]{1,0:T(8,128)S(1)}, u32[]{:S(2)}, u32[]{:S(2)}) collective-permute-start(f32[64,1]{1,0:T(8,128)S(1)} %bitcast.153), channel_id=1, source_target_pairs={{1,0},{2,1},{3,2},{4,3},{5,4},{6,5},{7,6},{8,7},{9,8},{10,9},{11,1... | collective-permute-start | bytes 776 | tf_op jit(solution)/shard_map/ppermute | solution.py:13
  11.1 8.2 %collective-permute-start = (f32[64,1]{1,0:T(8,128)S(1)}, f32[64,1]{1,0:T(8,128)S(1)}, u32[]{:S(2)}, u32[]{:S(2)}) collective-permute-start(f32[64,1]{1,0:T(8,128)S(1)} %slice.72), channel_id=1, source_target_pairs={{0,1},{1,2},{2,3},{3,4},{4,5},{5,6},{6,7},{7,8},{8,9},{9,10},{10,1... | collective-permute-start | bytes 776 | tf_op jit(solution)/shard_map/ppermute | solution.py:13
  18.2 1.6 copy-start.4
  18.2 1.7 copy-start.2
  20.3 10.6 %collective-permute-start.2 = (f32[64,1]{1,0:T(8,128)S(1)}, f32[64,1]{1,0:T(8,128)S(1)}, u32[]{:S(2)}, u32[]{:S(2)}) collective-permute-start(f32[64,1]{1,0:T(8,128)S(1)} %slice.98), channel_id=1, source_target_pairs={{0,1},{1,2},{2,3},{3,4},{4,5},{5,6},{6,7},{7,8},{8,9},{9,10},{10,1... | collective-permute-start | bytes 776 | tf_op jit(solution)/shard_map/ppermute | solution.py:13
  28.9 8.8 %collective-permute-start.3 = (f32[64,1]{1,0:T(8,128)S(1)}, f32[64,1]{1,0:T(8,128)S(1)}, u32[]{:S(2)}, u32[]{:S(2)}) collective-permute-start(f32[64,1]{1,0:T(8,128)S(1)} %bitcast.156), channel_id=1, source_target_pairs={{1,0},{2,1},{3,2},{4,3},{5,4},{6,5},{7,6},{8,7},{9,8},{10,9},{11,1... | collective-permute-start | bytes 776 | tf_op jit(solution)/shard_map/ppermute | solution.py:13
  38.3 6.0 %collective-permute-start.4 = (f32[64,1]{1,0:T(8,128)S(1)}, f32[64,1]{1,0:T(8,128)S(1)}, u32[]{:S(2)}, u32[]{:S(2)}) collective-permute-start(f32[64,1]{1,0:T(8,128)S(1)} %slice.102), channel_id=1, source_target_pairs={{0,1},{1,2},{2,3},{3,4},{4,5},{5,6},{6,7},{7,8},{8,9},{9,10},{10,1... | collective-permute-start | bytes 776 | tf_op jit(solution)/shard_map/ppermute | solution.py:13
  40.5 9.3 %copy-start.3 = (bf16[64,64,128]{2,1,0:T(8,128)(2,1)S(1)}, bf16[64,64,128]{2,1,0:T(8,128)(2,1)}, u32[]{:S(2)}) copy-start(bf16[64,64,128]{2,1,0:T(8,128)(2,1)} %param.13) | copy-start | bytes 3145732
  40.9 8.8 %collective-permute-start.5 = (f32[64,1]{1,0:T(8,128)S(1)}, f32[64,1]{1,0:T(8,128)S(1)}, u32[]{:S(2)}, u32[]{:S(2)}) collective-permute-start(f32[64,1]{1,0:T(8,128)S(1)} %bitcast.158), channel_id=1, source_target_pairs={{1,0},{2,1},{3,2},{4,3},{5,4},{6,5},{7,6},{8,7},{9,8},{10,9},{11,1... | collective-permute-start | bytes 776 | tf_op jit(solution)/shard_map/ppermute | solution.py:13
  44.3 63.8 %copy-start.7 = (bf16[64,64,16]{1,2,0:T(8,128)(2,1)S(1)}, bf16[64,64,16]{1,2,0:T(8,128)(2,1)}, u32[]{:S(2)}) copy-start(bf16[64,64,16]{1,2,0:T(8,128)(2,1)} %param.14) | copy-start | bytes 393220
  135.7 15.8 %collective-permute-start.6 = (f32[64,1]{1,0:T(8,128)S(1)}, f32[64,1]{1,0:T(8,128)S(1)}, u32[]{:S(2)}, u32[]{:S(2)}) collective-permute-start(f32[64,1]{1,0:T(8,128)S(1)} %slice.106), channel_id=1, source_target_pairs={{0,1},{1,2},{2,3},{3,4},{4,5},{5,6},{6,7},{7,8},{8,9},{9,10},{10,1... | collective-permute-start | bytes 776 | tf_op jit(solution)/shard_map/ppermute | solution.py:13
  149.6 8.8 %collective-permute-start.7 = (f32[64,1]{1,0:T(8,128)S(1)}, f32[64,1]{1,0:T(8,128)S(1)}, u32[]{:S(2)}, u32[]{:S(2)}) collective-permute-start(f32[64,1]{1,0:T(8,128)S(1)} %bitcast.160), channel_id=1, source_target_pairs={{1,0},{2,1},{3,2},{4,3},{5,4},{6,5},{7,6},{8,7},{9,8},{10,9},{11,1... | collective-permute-start | bytes 776 | tf_op jit(solution)/shard_map/ppermute | solution.py:13
  158.9 6.0 %collective-permute-start.8 = (f32[64,1]{1,0:T(8,128)S(1)}, f32[64,1]{1,0:T(8,128)S(1)}, u32[]{:S(2)}, u32[]{:S(2)}) collective-permute-start(f32[64,1]{1,0:T(8,128)S(1)} %slice.110), channel_id=1, source_target_pairs={{0,1},{1,2},{2,3},{3,4},{4,5},{5,6},{6,7},{7,8},{8,9},{9,10},{10,1... | collective-permute-start | bytes 776 | tf_op jit(solution)/shard_map/ppermute | solution.py:13
  161.5 8.8 %collective-permute-start.9 = (f32[64,1]{1,0:T(8,128)S(1)}, f32[64,1]{1,0:T(8,128)S(1)}, u32[]{:S(2)}, u32[]{:S(2)}) collective-permute-start(f32[64,1]{1,0:T(8,128)S(1)} %bitcast.162), channel_id=1, source_target_pairs={{1,0},{2,1},{3,2},{4,3},{5,4},{6,5},{7,6},{8,7},{9,8},{10,9},{11,1... | collective-permute-start | bytes 776 | tf_op jit(solution)/shard_map/ppermute | solution.py:13
  170.8 6.1 %copy-start.6 = (f32[64,128]{1,0:T(8,128)}, f32[64,128]{1,0:T(8,128)S(1)}, u32[]{:S(2)}) copy-start(f32[64,128]{1,0:T(8,128)S(1)} %bitcast_add_fusion) | copy-start | bytes 98308
  170.9 6.0 %collective-permute-start.10 = (f32[64,1]{1,0:T(8,128)S(1)}, f32[64,1]{1,0:T(8,128)S(1)}, u32[]{:S(2)}, u32[]{:S(2)}) collective-permute-start(f32[64,1]{1,0:T(8,128)S(1)} %slice.114), channel_id=1, source_target_pairs={{0,1},{1,2},{2,3},{3,4},{4,5},{5,6},{6,7},{7,8},{8,9},{9,10},{10,1... | collective-permute-start | bytes 776 | tf_op jit(solution)/shard_map/ppermute | solution.py:13
  173.4 8.8 %collective-permute-start.11 = (f32[64,1]{1,0:T(8,128)S(1)}, f32[64,1]{1,0:T(8,128)S(1)}, u32[]{:S(2)}, u32[]{:S(2)}) collective-permute-start(f32[64,1]{1,0:T(8,128)S(1)} %bitcast.164), channel_id=1, source_target_pairs={{1,0},{2,1},{3,2},{4,3},{5,4},{6,5},{7,6},{8,7},{9,8},{10,9},{11,1... | collective-permute-start | bytes 776 | tf_op jit(solution)/shard_map/ppermute | solution.py:13
Sparse Core Ops, SparseCore 0:
  51.1 56.9 reduce-scatter.3
where the time goes:
time: 190 us
  waiting for transfers between devices  85.8 us (45%)
  starting transfers between devices  50 us (26%)
  blocking collectives  24.7 us (13%)
  between operations  14.5 us (8%)
  other arithmetic  12.7 us (7%)
    unnamed x2, waiting for transfers between devices  57.1 us
    ppermute x12, starting transfers between devices, from_behind(): return lax.ppermute(block, axis, route)  49.9 us
    ppermute x12, waiting for transfers between devices, from_behind(): return lax.ppermute(block, axis, route)  28.7 us
    all_gather x1, blocking collectives, local(): lax.all_gather(corrected, 'row', axis=1, tiled=True)  24.7 us
    dot_general x17, other arithmetic, apply_blocks(): jnp.einsum('ijn,jn->in', blocks, vector, precision=lax.Precision.HIGHEST,...  6.99 us
  transfers between devices with their start and end apart: 13, of which 7 were waited for; matrix products, arithmetic and copies ran while one was open for 3% of the time, Pallas kernels for 0%

commit v1 on v0

v1 whole, which is shorter than its diff:
```python
import functools

import jax
import jax.numpy as jnp
from jax import lax
from jax.experimental import pallas as pl
from jax.experimental.pallas import tpu as pltpu
from jax.sharding import PartitionSpec as P

AGG = 8
BOTH = ("grp", "row")
F32 = jnp.float32
BF16 = jnp.bfloat16
ROWS = 8


def from_behind(block, distance):
    devices = range(lax.axis_size(BOTH))
    route = [(i - distance, i) for i in devices if i - distance in devices]
    return lax.ppermute(block, BOTH, route)


def lanes(like):
    return lax.broadcasted_iota(jnp.int32, like.shape, 1)


def turn(tile, shift):
    return pltpu.roll(tile, shift % tile.shape[1], 1)


def three(tile):
    high = tile.astype(BF16)
    rest = tile - high.astype(F32)
    middle = rest.astype(BF16)
    return high, middle, (rest - middle.astype(F32)).astype(BF16)


def product(left, right, dims):
    left = left.astype(BF16)
    parts = [
        lax.dot_general(left, part, (dims, ((), ())), preferred_element_type=F32)
        for part in three(right)
    ]
    return parts[0] + (parts[1] + parts[2])


def times(block, columns):
    return product(block, columns, ((1,), (0,)))


def times_transposed(block, columns):
    return product(block, columns, ((0,), (0,)))


def operate(diag, coupling, vector_ref, out_ref, lower):
    vector = vector_ref[...]

    def step(chunk, upward):
        start = pl.multiple_of(chunk * ROWS, ROWS)
        own = vector_ref[pl.ds(start, ROWS), :]
        sums = []
        for s in range(ROWS):
            pair = coupling[start + s].astype(F32)
            terms = diag[start + s].astype(F32) * vector + pair * lower
            sums.append(jnp.sum(terms, axis=0, keepdims=True))
            upward = upward + pair * own[s : s + 1, :]
        out_ref[pl.ds(start, ROWS), :] = jnp.concatenate(sums, axis=0)
        return upward

    return lax.fori_loop(0, vector.shape[0] // ROWS, step, jnp.zeros_like(vector))


def apply_blocks(blocks, vector, base_ref, out_ref):
    def step(chunk, carry):
        start = pl.multiple_of(chunk * ROWS, ROWS)
        sums = [
            jnp.sum(blocks[start + s].astype(F32) * vector, axis=0, keepdims=True)
            for s in range(ROWS)
        ]
        base = base_ref[pl.ds(start, ROWS), :]
        out_ref[pl.ds(start, ROWS), :] = base + jnp.concatenate(sums, axis=0)
        return carry

    lax.fori_loop(0, vector.shape[0] // ROWS, step, 0)


def apply_transposed(blocks, vector_ref):
    def step(chunk, total):
        start = pl.multiple_of(chunk * ROWS, ROWS)
        own = vector_ref[pl.ds(start, ROWS), :]
        for s in range(ROWS):
            total = total + blocks[start + s].astype(F32) * own[s : s + 1, :]
        return total

    zero = jnp.zeros(vector_ref.shape, F32)
    return lax.fori_loop(0, vector_ref.shape[0] // ROWS, step, zero)


def edges(blocks, scratch):
    size, count = blocks.shape[0], blocks.shape[2]
    lane = lax.broadcasted_iota(jnp.int32, (size, count), 1)

    def step(chunk, tile):
        start = chunk * ROWS
        for s in range(ROWS):
            turned = pltpu.roll(blocks[start + s].astype(F32), 2 * (start + s) + 1, 1)
            tile = jnp.where(lax.shift_right_logical(lane, 1) == start + s, turned, tile)
        return tile

    tile = lax.fori_loop(0, size // ROWS, step, jnp.zeros((size, count), F32))
    scratch[...] = jnp.transpose(tile)
    return scratch[pl.ds(1, size, stride=2), :], scratch[pl.ds(0, size, stride=2), :]


def trial_sweep(rhs_ref, start_ref, diag, inverse, coupling, last_coupling, trial_ref, work_ref):
    start = start_ref[...]
    lane = lanes(start)
    end = start.shape[1] - 1
    lower = jnp.where(lane == 0, 0.0, turn(start, 1))
    upward = operate(diag, coupling, start_ref, work_ref, lower)
    upper = jnp.where(lane == end, 0.0, turn(upward, -1))
    defect = rhs_ref[...] - (work_ref[...] + upper)
    apply_blocks(inverse, defect, start_ref, trial_ref)
    trial = trial_ref[...]
    upward = apply_transposed(coupling, trial_ref)
    to_left = rhs_ref[...] - turn(upward, -1)
    to_right = rhs_ref[...] - times(last_coupling, turn(trial, 1))
    right = jnp.where(
        lane == 0, turn(start, 1), jnp.where(lane == 1, turn(trial, 2), turn(to_right, 3))
    )
    left = jnp.where(
        lane == end, turn(start, -1), jnp.where(lane == end - 1, turn(trial, -2), turn(to_left, -3))
    )
    return right, left


def first_kernel(
    rhs, guess, diag, inverse, coupling, trial, to_right, to_left, own, work, scratch
):
    size = guess.shape[0]
    first_diag, last_diag = edges(diag, scratch)
    first_inverse, last_inverse = edges(inverse, scratch)
    first_coupling, last_coupling = edges(coupling, scratch)
    to_right[1] = jnp.concatenate([last_diag, last_inverse], axis=1)
    to_left[1] = jnp.concatenate([first_diag, first_inverse], axis=1)
    to_left[2] = jnp.concatenate([first_coupling, first_coupling], axis=1)
    own[0] = first_coupling.astype(BF16)
    own[1] = first_inverse.astype(BF16)
    own[2] = last_coupling.astype(BF16)
    own[3] = last_inverse.astype(BF16)
    right, left = trial_sweep(rhs, guess, diag, inverse, coupling, last_coupling, trial, work)
    to_right[0] = right
    to_left[0] = left


def finish(
    rhs, start_ref, trial_ref, diag, inverse, coupling, own, left, right,
    left_blocks, right_blocks, twice_ref, work_ref, once_ref,
):
    start, trial = start_ref[...], trial_ref[...]
    size = start.shape[0]
    lane = lanes(start)
    end = start.shape[1] - 1
    at_start, at_end = lane == 0, lane == end
    left_diag, left_inverse = left_blocks[0][:, :size], left_blocks[0][:, size:]
    right_diag, right_inverse = right_blocks[0][:, :size], right_blocks[0][:, size:]
    right_coupling = right_blocks[1][:, :size]
    first_coupling, first_inverse, last_inverse = own[0], own[1], own[3]

    up_right = times_transposed(right_coupling, right)
    down_left = times(first_coupling, left)
    once = trial - jnp.where(
        at_start,
        times(first_inverse, down_left),
        jnp.where(at_end, times(last_inverse, up_right), 0.0),
    )
    once_ref[...] = once
    left_once = turn(left, -1) - times(left_inverse, times_transposed(first_coupling, start))
    right_once = turn(right, 1) - times(right_inverse, times(right_coupling, start))
    left_twice = left_once + times(
        left_inverse,
        turn(left, -2) - times(left_diag, left_once) - times_transposed(first_coupling, once),
    )
    right_twice = right_once + times(
        right_inverse,
        turn(right, 2) - times(right_diag, right_once) - times(right_coupling, once),
    )

    upward = operate(
        diag, coupling, once_ref, work_ref, jnp.where(at_start, left_once, turn(once, 1))
    )
    upper = jnp.where(at_end, times_transposed(right_coupling, right_once), turn(upward, -1))
    defect = rhs[...] - (work_ref[...] + upper)
    apply_blocks(inverse, defect, once_ref, twice_ref)
    twice = twice_ref[...]
    upward = operate(
        diag, coupling, twice_ref, work_ref, jnp.where(at_start, left_twice, turn(twice, 1))
    )
    upper = jnp.where(at_end, times_transposed(right_coupling, right_twice), turn(upward, -1))
    return rhs[...] - (work_ref[...] + upper)


def chosen(aggregate, group_count, half):
    rows = group_count // 2
    local_index = jnp.broadcast_to(lax.rem(aggregate[...], group_count), (rows, aggregate.shape[1]))
    row = lax.broadcasted_iota(jnp.int32, local_index.shape, 0)
    named = (row // ROWS) * (2 * ROWS) + lax.rem(row, ROWS) + half * ROWS
    return jnp.where(local_index == named, 1.0, 0.0).astype(F32)


def second_kernel(
    group_count, rhs, guess, trial, diag, inverse, coupling, own, from_left, from_right,
    prolong, aggregate, twice, partial, work, once,
):
    residual = finish(
        rhs, guess, trial, diag, inverse, coupling, own, from_left[0], from_right[0],
        from_left.at[1:], from_right.at[1:], twice, work, once,
    )
    work[...] = residual
    pieces = apply_transposed(prolong, work)
    partial[...] = jnp.concatenate(
        [product(chosen(aggregate, group_count, half), pieces, ((1,), (1,))) for half in (0, 1)],
        axis=1,
    )


def coarse_kernel(shares, coarse_inverse, out, work, zero):
    size, own = coarse_inverse.shape[0], coarse_inverse.shape[2]
    rows = shares.shape[0] // ROWS
    share = shares[0:ROWS]
    for row in range(1, rows):
        share = share + shares[row * ROWS : (row + 1) * ROWS]
    flipped = jnp.transpose(share)
    vector = jnp.concatenate([flipped[:size], flipped[size:]], axis=1)
    zero[...] = jnp.zeros_like(vector)
    apply_blocks(coarse_inverse, vector, zero, work)
    value = jnp.transpose(work[...])
    value = jnp.concatenate([value[:ROWS], value[ROWS:]], axis=1)
    for row in range(rows):
        out[row * ROWS : (row + 1) * ROWS] = value


def third_kernel(
    group_count, rhs, twice, values, diag, inverse, coupling, own, prolong, aggregate,
    start, trial, to_right, to_left, work,
):
    size = twice.shape[0]
    spread = jnp.zeros(twice.shape, F32)
    packed = values[...]
    for half in (0, 1):
        picked = chosen(aggregate, group_count, half).astype(BF16)
        for part in three(packed):
            both = lax.dot_general(
                part, picked, (((0,), (0,)), ((), ())), preferred_element_type=F32
            )
            spread = spread + both[half * size : (half + 1) * size]
    apply_blocks(prolong, spread, twice, start)
    right, left = trial_sweep(rhs, start, diag, inverse, coupling, own[2], trial, work)
    to_right[...] = right
    to_left[...] = left


def fourth_kernel(
    rhs, start, trial, diag, inverse, coupling, own, from_left, from_right,
    left_blocks, right_blocks, twice, residual, work, once,
):
    residual[...] = finish(
        rhs, start, trial, diag, inverse, coupling, own, from_left[...], from_right[...],
        left_blocks.at[1:], right_blocks.at[1:], twice, work, once,
    )


def call(kernel, outs, scratch, *operands):
    inside = pl.BlockSpec(memory_space=pltpu.VMEM)
    single = not isinstance(outs, tuple)
    return pl.pallas_call(
        kernel,
        out_shape=outs,
        in_specs=[inside] * len(operands),
        out_specs=inside if single else (inside,) * len(outs),
        scratch_shapes=[pltpu.VMEM(shape, F32) for shape in scratch],
        compiler_params=pltpu.CompilerParams(vmem_limit_bytes=24 << 20),
    )(*operands)


def local(rhs, guess, diag_blocks, diag_inverse, coupling, prolong, coarse_inverse, aggregate):
    size, count = rhs.shape
    rows = lax.axis_size("row")
    group_count = count * rows // AGG
    own_coarse = coarse_inverse.shape[2]
    assert own_coarse == 2 * ROWS and 2 * size == count
    tile = jax.ShapeDtypeStruct((size, count), F32)
    aggregate = aggregate.reshape(1, count)

    def stack(n):
        return jax.ShapeDtypeStruct((n, size, count), F32)

    packed = jax.ShapeDtypeStruct((group_count // 2, count), F32)
    own_shape = jax.ShapeDtypeStruct((4, size, size), BF16)
    plain = (size, count)
    trial, to_right, to_left, own = call(
        first_kernel, (tile, stack(2), stack(3), own_shape), [plain, (count, size)],
        rhs, guess, diag_blocks, diag_inverse, coupling,
    )
    from_left = from_behind(to_right, 1)
    from_right = from_behind(to_left, -1)
    twice, partial = call(
        functools.partial(second_kernel, group_count), (tile, packed), [plain, plain],
        rhs, guess, trial, diag_blocks, diag_inverse, coupling, own, from_left, from_right,
        prolong, aggregate,
    )
    shares = lax.all_to_all(partial, "row", 0, 0, tiled=True)
    corrected = call(
        coarse_kernel, packed, [(size, own_coarse), (size, own_coarse)], shares, coarse_inverse
    )
    values = lax.all_to_all(corrected, "row", 0, 0, tiled=True)
    start, trial, to_right, to_left = call(
        functools.partial(third_kernel, group_count), (tile, tile, tile, tile), [plain],
        rhs, twice, values, diag_blocks, diag_inverse, coupling, own, prolong, aggregate,
    )
    next_left = from_behind(to_right, 1)
    next_right = from_behind(to_left, -1)
    return call(
        fourth_kernel, (tile, tile), [plain, plain],
        rhs, start, trial, diag_blocks, diag_inverse, coupling, own, next_left, next_right,
        from_left, from_right,
    )


def solution(mesh):
    vector = P(None, BOTH)
    blocks = P(None, None, BOTH)
    return jax.shard_map(
        local,
        mesh=mesh,
        in_specs=(vector, vector, blocks, blocks, blocks, blocks, blocks, P(BOTH)),
        out_specs=(vector, vector),
        check_vma=False,
    )
```

time: 190 us -> 71.8 us (0.38)
  waiting for transfers between devices: 85.8 us -> 8.78 us
  starting transfers between devices: 50 us -> 28 us
  blocking collectives: 24.7 us -> 7.85 us
  Pallas kernels: 0 us -> 15 us
  between operations: 14.5 us -> 0.73 us
  other arithmetic: 12.7 us -> 0 us
  local copies, waits for them, and re-layouts: 0.99 us -> 10.7 us
    unnamed x2 -> x0, waiting for transfers between devices: 57.1 us -> none
    ppermute x12 -> x4, starting transfers between devices: 49.9 us -> 20.2 us  [from_behind(): return lax.ppermute(block, BOTH, route)]
    all_gather x1 -> x0, blocking collectives: 24.7 us -> none  [local(): lax.all_gather(corrected, 'row', axis=1, tiled=True)]
    ppermute x12 -> x4, waiting for transfers between devices: 28.7 us -> 8.78 us  [from_behind(): return lax.ppermute(block, BOTH, route)]
    pallas_call x0 -> x5, Pallas kernels: none -> 15 us  [call(): pl.pallas_call(kernel, out_shape=outs, in_specs=[inside] * len(operands),...]
    unnamed x18 -> x27, local copies, waits for them, and re-layouts: 0.04 us -> 10.7 us
    dot_general x24 -> x0, other arithmetic: 10.2 us -> none  [the longest x17 6.99 us: apply_blocks(): jnp.einsum('ijn,jn->in', blocks, vector, precision=lax.Precision.HIGHEST,...]
    all_to_all x0 -> x1, blocking collectives: none -> 7.85 us  [local(): values = lax.all_to_all(corrected, 'row', 0, 0, tiled=True)]
  transfers between devices with their start and end apart: 13 -> 5, of which waited for: 7 -> 2; matrix products, arithmetic and copies ran while one was open for 3% -> 3% of each run, Pallas kernels for 0% -> 0%
where the time goes in v1:
time: 71.8 us; the launch traced here: 71.1 us
  starting transfers between devices  28 us (39%)
  Pallas kernels  15 us (21%)
  local copies, waits for them, and re-layouts  10.7 us (15%)
  waiting for transfers between devices  8.78 us (12%)
  blocking collectives  7.85 us (11%)
  between operations  0.73 us (1%)
    ppermute x4, starting transfers between devices, from_behind(): return lax.ppermute(block, BOTH, route)  20.2 us
    pallas_call x5, Pallas kernels, call(): pl.pallas_call(kernel, out_shape=outs, in_specs=[inside] * len(operands),...  15 us
    unnamed x27, local copies, waits for them, and re-layouts  10.7 us
    ppermute x4, waiting for transfers between devices, from_behind(): return lax.ppermute(block, BOTH, route)  8.78 us
    all_to_all x1, blocking collectives, local(): values = lax.all_to_all(corrected, 'row', 0, 0, tiled=True)  7.85 us
    all_to_all x1, starting transfers between devices, local(): shares = lax.all_to_all(partial, 'row', 0, 0, tiled=True)  7.81 us
  transfers between devices with their start and end apart: 5, of which 2 were waited for; matrix products, arithmetic and copies ran while one was open for 3% of the time, Pallas kernels for 0%

profile of v1, /device:TPU:29, one launch (start us, length us, event | category | flops | bytes accessed | tf_op | source)
XLA Modules:
  0.0 71.1 jit_solution(959732227690480561)
XLA Ops:
  0.6 0.0 copy-start
  0.6 1.2 %copy-done = bf16[64,64,128]{2,1,0:T(8,128)(2,1)S(1)} copy-done((bf16[64,64,128]{2,1,0:T(8,128)(2,1)S(1)}, bf16[64,64,128]{2,1,0:T(8,128)(2,1)}, u32[]{:S(2)}) %copy-start) | copy-done | bytes 1048600
  1.9 1.2 %copy-done.2 = bf16[64,64,128]{2,1,0:T(8,128)(2,1)S(1)} copy-done((bf16[64,64,128]{2,1,0:T(8,128)(2,1)S(1)}, bf16[64,64,128]{2,1,0:T(8,128)(2,1)}, u32[]{:S(2)}) %copy-start.2) | copy-done | bytes 1048600
  3.1 1.2 %copy-done.4 = bf16[64,64,128]{2,1,0:T(8,128)(2,1)S(1)} copy-done((bf16[64,64,128]{2,1,0:T(8,128)(2,1)S(1)}, bf16[64,64,128]{2,1,0:T(8,128)(2,1)}, u32[]{:S(2)}) %copy-start.4) | copy-done | bytes 1048600
  4.3 0.8 %copy-done.9 = f32[64,128]{1,0:T(8,128)S(1)} copy-done((f32[64,128]{1,0:T(8,128)S(1)}, f32[64,128]{1,0:T(8,128)}, u32[]{:S(2)}) %copy-start.9) | copy-done | bytes 32792
  5.1 0.8 %copy-done.11 = f32[64,128]{1,0:T(8,128)S(1)} copy-done((f32[64,128]{1,0:T(8,128)S(1)}, f32[64,128]{1,0:T(8,128)}, u32[]{:S(2)}) %copy-start.11) | copy-done | bytes 32792
  5.8 4.4 %shard_map.95 = (f32[64,128]{1,0:T(8,128)S(1)}, f32[2,64,128]{2,1,0:T(8,128)S(1)}, f32[3,64,128]{2,1,0:T(8,128)S(1)}, bf16[4,64,64]{2,1,0:T(8,128)(2,1)S(1)}) custom-call(f32[64,128]{1,0:T(8,128)S(1)} %copy-done.9, f32[64,128]{1,0:T(8,128)S(1)} %copy-done.11, bf16[64,64,128]{2,1,0:T(8,128)(2,1)S(1)} %copy-done, bf16[64,64,128]{2,1,0:T(8,128)(2,1)S(1)} %copy-done.2, ...), custom_call_target="tpu_custom_call" | custom-call | tf_op jit(solution)/shard_map/pallas_call | solution.py:276
  10.3 2.1 %collective-permute-start.1 = (f32[3,64,128]{2,1,0:T(8,128)S(1)}, f32[3,64,128]{2,1,0:T(8,128)S(1)}, u32[]{:S(2)}, u32[]{:S(2)}) collective-permute-start(f32[3,64,128]{2,1,0:T(8,128)S(1)} %get-tuple-element.15), channel_id=1, source_target_pairs={{1,0},{2,1},{3,2},{4,3},{5,4},{6,5},{7,6},{8,7},{9,8},{10,9},{11,1... | collective-permute-start | bytes 294920 | tf_op jit(solution)/shard_map/ppermute | solution.py:20
  12.4 7.0 %collective-permute-start = (f32[2,64,128]{2,1,0:T(8,128)S(1)}, f32[2,64,128]{2,1,0:T(8,128)S(1)}, u32[]{:S(2)}, u32[]{:S(2)}) collective-permute-start(f32[2,64,128]{2,1,0:T(8,128)S(1)} %get-tuple-element.14), channel_id=1, source_target_pairs={{0,1},{1,2},{2,3},{3,4},{4,5},{5,6},{6,7},{7,8},{8,9},{9,10},{10,1... | collective-permute-start | bytes 196616 | tf_op jit(solution)/shard_map/ppermute | solution.py:20
  19.4 1.9 %collective-permute-done.from_left.left_blocks = f32[2,64,128]{2,1,0:T(8,128)S(1)} collective-permute-done((f32[2,64,128]{2,1,0:T(8,128)S(1)}, f32[2,64,128]{2,1,0:T(8,128)S(1)}, u32[]{:S(2)}, u32[]{:S(2)}) %collective-permute-start) | collective-permute-done | bytes 65568 | tf_op jit(solution)/shard_map/ppermute | solution.py:20
  21.3 0.0 collective-permute-done.1.from_right.right_blocks
  21.3 0.0 copy-done.6
  21.3 0.7 copy-done.12
  22.0 4.1 %shard_map.96 = (f32[64,128]{1,0:T(8,128)S(1)}, f32[64,128]{1,0:T(8,128)}) custom-call(f32[64,128]{1,0:T(8,128)S(1)} %copy-done.9, f32[64,128]{1,0:T(8,128)S(1)} %copy-done.11, f32[64,128]{1,0:T(8,128)S(1)} %get-tuple-element.12.trial, bf16[64,64,128]{2,1,0:T(8,128)(2,1)S(1)} %copy-done, bf16[64,64,128]{2,1,0:T(8,128)(2,1)S(1)} %copy-done.2, ...), custom_call_target="tpu_custom_call" | custom-call | tf_op jit(solution)/shard_map/pallas_call | solution.py:276
  26.1 7.8 %all-to-all-start = ((f32[8,8,128]{2,1,0:T(8,128)}), f32[8,8,128]{2,1,0:T(8,128)S(1)}, u32[]{:S(2)}, u32[]{:S(2)}) async-start(f32[8,8,128]{2,1,0:T(8,128)} %bitcast.1), calls=%async_computation | async-start | bytes 65536 | tf_op jit(solution)/shard_map/all_to_all | solution.py:312
  33.9 2.4 %copy.10.coarse_inverse = bf16[64,64,16]{2,1,0:T(8,128)(2,1)} copy(bf16[64,64,16]{1,2,0:T(8,128)(2,1)} %param.14) | data formatting | bytes 262144 | tf_op args[6]
  36.3 0.0 all-to-all-done
  36.3 1.2 %copy-done.8 = bf16[64,64,16]{2,1,0:T(8,128)(2,1)S(1)} copy-done((bf16[64,64,16]{2,1,0:T(8,128)(2,1)S(1)}, bf16[64,64,16]{2,1,0:T(8,128)(2,1)}, u32[]{:S(2)}) %copy-start.8) | copy-done | bytes 131096
  37.6 0.7 shard_map.97
  38.2 7.8 %all_to_all.22 = f32[8,8,128]{2,1,0:T(8,128)S(1)} all-to-all(f32[8,8,128]{2,1,0:T(8,128)S(1)} %bitcast.7), channel_id=1, replica_groups=mesh['grp'=4,'row'=8] {'row'}, dimensions={0} | all-to-all | bytes 65536 | tf_op jit(solution)/shard_map/all_to_all | solution.py:316
  46.1 0.0 copy-done.5
  46.1 0.0 copy-done.1
  46.1 0.0 copy-done.3
  46.1 0.0 copy-done.10
  46.1 0.0 copy-start.7
  46.1 1.2 %copy-done.7 = bf16[64,64,128]{2,1,0:T(8,128)(2,1)S(1)} copy-done((bf16[64,64,128]{2,1,0:T(8,128)(2,1)S(1)}, bf16[64,64,128]{2,1,0:T(8,128)(2,1)}, u32[]{:S(2)}) %copy-start.7) | copy-done | bytes 1048600
  47.3 2.2 %shard_map.98 = (f32[64,128]{1,0:T(8,128)S(1)}, f32[64,128]{1,0:T(8,128)S(1)}, f32[64,128]{1,0:T(8,128)S(1)}, f32[64,128]{1,0:T(8,128)S(1)}) custom-call(f32[64,128]{1,0:T(8,128)S(1)} %copy-done.10, f32[64,128]{1,0:T(8,128)S(1)} %get-tuple-element.16.twice, f32[64,128]{1,0:T(8,128)S(1)} %bitcast.5, bf16[64,64,128]{2,1,0:T(8,128)(2,1)S(1)} %copy-done.1, ...), custom_call_target="tpu_custom_call" | custom-call | tf_op jit(solution)/shard_map/pallas_call | solution.py:276
  49.5 9.1 %collective-permute-start.2 = (f32[64,128]{1,0:T(8,128)S(1)}, f32[64,128]{1,0:T(8,128)S(1)}, u32[]{:S(2)}, u32[]{:S(2)}) collective-permute-start(f32[64,128]{1,0:T(8,128)S(1)} %get-tuple-element.20), channel_id=1, source_target_pairs={{0,1},{1,2},{2,3},{3,4},{4,5},{5,6},{6,7},{7,8},{8,9},{9,10},{10,1... | collective-permute-start | bytes 98312 | tf_op jit(solution)/shard_map/ppermute | solution.py:20
  58.6 1.9 %collective-permute-start.3 = (f32[64,128]{1,0:T(8,128)S(1)}, f32[64,128]{1,0:T(8,128)S(1)}, u32[]{:S(2)}, u32[]{:S(2)}) collective-permute-start(f32[64,128]{1,0:T(8,128)S(1)} %get-tuple-element.21), channel_id=1, source_target_pairs={{1,0},{2,1},{3,2},{4,3},{5,4},{6,5},{7,6},{8,7},{9,8},{10,9},{11,1... | collective-permute-start | bytes 98312 | tf_op jit(solution)/shard_map/ppermute | solution.py:20
  60.6 0.0 collective-permute-done.2.from_left
  60.6 6.9 %collective-permute-done.3.from_right = f32[64,128]{1,0:T(8,128)S(1)} collective-permute-done((f32[64,128]{1,0:T(8,128)S(1)}, f32[64,128]{1,0:T(8,128)S(1)}, u32[]{:S(2)}, u32[]{:S(2)}) %collective-permute-start.3) | collective-permute-done | bytes 32800 | tf_op jit(solution)/shard_map/ppermute | solution.py:20
  67.5 3.6 %shard_map.99 = (f32[64,128]{1,0:T(8,128)}, f32[64,128]{1,0:T(8,128)}) custom-call(f32[64,128]{1,0:T(8,128)S(1)} %copy-done.10, f32[64,128]{1,0:T(8,128)S(1)} %get-tuple-element.18.start, f32[64,128]{1,0:T(8,128)S(1)} %get-tuple-element.19.trial, bf16[64,64,128]{2,1,0:T(8,128)(2,1)S(1)} %copy-done.1, bf16[64,64,128]{2,1,0:T(8,128)(2,1)S(1)} %copy-done.3, ...), custom_call_target="tpu_custom_call" | custom-call | tf_op jit(solution)/shard_map/pallas_call | solution.py:276
  (11 shorter events, 0.0 us)
Async XLA Ops:
  0.6 1.2 %copy-start = (bf16[64,64,128]{2,1,0:T(8,128)(2,1)S(1)}, bf16[64,64,128]{2,1,0:T(8,128)(2,1)}, u32[]{:S(2)}) copy-start(bf16[64,64,128]{2,1,0:T(8,128)(2,1)} %diag.7) | copy-start | bytes 3145732
  1.9 1.2 %copy-start.2 = (bf16[64,64,128]{2,1,0:T(8,128)(2,1)S(1)}, bf16[64,64,128]{2,1,0:T(8,128)(2,1)}, u32[]{:S(2)}) copy-start(bf16[64,64,128]{2,1,0:T(8,128)(2,1)} %inverse.7) | copy-start | bytes 3145732
  3.1 1.2 %copy-start.4 = (bf16[64,64,128]{2,1,0:T(8,128)(2,1)S(1)}, bf16[64,64,128]{2,1,0:T(8,128)(2,1)}, u32[]{:S(2)}) copy-start(bf16[64,64,128]{2,1,0:T(8,128)(2,1)} %coupling.7) | copy-start | bytes 3145732
  4.3 0.8 %copy-start.9 = (f32[64,128]{1,0:T(8,128)S(1)}, f32[64,128]{1,0:T(8,128)}, u32[]{:S(2)}) copy-start(f32[64,128]{1,0:T(8,128)} %rhs.7) | copy-start | bytes 98308
  5.1 0.8 %copy-start.11 = (f32[64,128]{1,0:T(8,128)S(1)}, f32[64,128]{1,0:T(8,128)}, u32[]{:S(2)}) copy-start(f32[64,128]{1,0:T(8,128)} %guess.3) | copy-start | bytes 98308
  5.8 15.5 %copy-start.6 = (bf16[64,64,128]{2,1,0:T(8,128)(2,1)S(1)}, bf16[64,64,128]{2,1,0:T(8,128)(2,1)}, u32[]{:S(2)}) copy-start(bf16[64,64,128]{2,1,0:T(8,128)(2,1)} %prolong.3) | copy-start | bytes 3145732
  10.3 11.1 %collective-permute-start.1 = (f32[3,64,128]{2,1,0:T(8,128)S(1)}, f32[3,64,128]{2,1,0:T(8,128)S(1)}, u32[]{:S(2)}, u32[]{:S(2)}) collective-permute-start(f32[3,64,128]{2,1,0:T(8,128)S(1)} %get-tuple-element.15), channel_id=1, source_target_pairs={{1,0},{2,1},{3,2},{4,3},{5,4},{6,5},{7,6},{8,7},{9,8},{10,9},{11,1... | collective-permute-start | bytes 294920 | tf_op jit(solution)/shard_map/ppermute | solution.py:20
  12.4 8.9 %collective-permute-start = (f32[2,64,128]{2,1,0:T(8,128)S(1)}, f32[2,64,128]{2,1,0:T(8,128)S(1)}, u32[]{:S(2)}, u32[]{:S(2)}) collective-permute-start(f32[2,64,128]{2,1,0:T(8,128)S(1)} %get-tuple-element.14), channel_id=1, source_target_pairs={{0,1},{1,2},{2,3},{3,4},{4,5},{5,6},{6,7},{7,8},{8,9},{9,10},{10,1... | collective-permute-start | bytes 196616 | tf_op jit(solution)/shard_map/ppermute | solution.py:20
  21.3 0.7 copy-start.12
  22.0 24.1 %copy-start.5 = (bf16[64,64,128]{2,1,0:T(8,128)(2,1)S(1)}, bf16[64,64,128]{2,1,0:T(8,128)(2,1)}, u32[]{:S(2)}) copy-start(bf16[64,64,128]{2,1,0:T(8,128)(2,1)} %coupling.7) | copy-start | bytes 3145732
  26.1 10.3 %all-to-all-start = ((f32[8,8,128]{2,1,0:T(8,128)}), f32[8,8,128]{2,1,0:T(8,128)S(1)}, u32[]{:S(2)}, u32[]{:S(2)}) async-start(f32[8,8,128]{2,1,0:T(8,128)} %bitcast.1), calls=%async_computation | async-start | bytes 65536 | tf_op jit(solution)/shard_map/all_to_all | solution.py:312
  33.9 12.2 %copy-start.1 = (bf16[64,64,128]{2,1,0:T(8,128)(2,1)S(1)}, bf16[64,64,128]{2,1,0:T(8,128)(2,1)}, u32[]{:S(2)}) copy-start(bf16[64,64,128]{2,1,0:T(8,128)(2,1)} %diag.7) | copy-start | bytes 3145732
  33.9 12.2 %copy-start.3 = (bf16[64,64,128]{2,1,0:T(8,128)(2,1)S(1)}, bf16[64,64,128]{2,1,0:T(8,128)(2,1)}, u32[]{:S(2)}) copy-start(bf16[64,64,128]{2,1,0:T(8,128)(2,1)} %inverse.7) | copy-start | bytes 3145732
  36.3 1.2 %copy-start.8 = (bf16[64,64,16]{2,1,0:T(8,128)(2,1)S(1)}, bf16[64,64,16]{2,1,0:T(8,128)(2,1)}, u32[]{:S(2)}) copy-start(bf16[64,64,16]{2,1,0:T(8,128)(2,1)} %copy.10.coarse_inverse) | copy-start | bytes 393220
  38.2 7.9 %copy-start.10 = (f32[64,128]{1,0:T(8,128)S(1)}, f32[64,128]{1,0:T(8,128)}, u32[]{:S(2)}) copy-start(f32[64,128]{1,0:T(8,128)} %rhs.7) | copy-start | bytes 98308
  46.1 1.2 %copy-start.7 = (bf16[64,64,128]{2,1,0:T(8,128)(2,1)S(1)}, bf16[64,64,128]{2,1,0:T(8,128)(2,1)}, u32[]{:S(2)}) copy-start(bf16[64,64,128]{2,1,0:T(8,128)(2,1)} %prolong.3) | copy-start | bytes 3145732
  49.5 11.0 %collective-permute-start.2 = (f32[64,128]{1,0:T(8,128)S(1)}, f32[64,128]{1,0:T(8,128)S(1)}, u32[]{:S(2)}, u32[]{:S(2)}) collective-permute-start(f32[64,128]{1,0:T(8,128)S(1)} %get-tuple-element.20), channel_id=1, source_target_pairs={{0,1},{1,2},{2,3},{3,4},{4,5},{5,6},{6,7},{7,8},{8,9},{9,10},{10,1... | collective-permute-start | bytes 98312 | tf_op jit(solution)/shard_map/ppermute | solution.py:20
  58.6 8.8 %collective-permute-start.3 = (f32[64,128]{1,0:T(8,128)S(1)}, f32[64,128]{1,0:T(8,128)S(1)}, u32[]{:S(2)}, u32[]{:S(2)}) collective-permute-start(f32[64,128]{1,0:T(8,128)S(1)} %get-tuple-element.21), channel_id=1, source_target_pairs={{1,0},{2,1},{3,2},{4,3},{5,4},{6,5},{7,6},{8,7},{9,8},{10,9},{11,1... | collective-permute-start | bytes 98312 | tf_op jit(solution)/shard_map/ppermute | solution.py:20

commit v2 on v1

--- a/solution.py
+++ b/solution.py
@@ -12,6 +12,7 @@
 F32 = jnp.float32
 BF16 = jnp.bfloat16
 ROWS = 8
+LOAD = 16
 
 
 def from_behind(block, distance):
@@ -60,14 +61,14 @@
         own = vector_ref[pl.ds(start, ROWS), :]
         sums = []
         for s in range(ROWS):
-            pair = coupling[start + s].astype(F32)
-            terms = diag[start + s].astype(F32) * vector + pair * lower
+            pair = coupling[start + s]
+            terms = diag[start + s] * vector + pair * lower
             sums.append(jnp.sum(terms, axis=0, keepdims=True))
             upward = upward + pair * own[s : s + 1, :]
         out_ref[pl.ds(start, ROWS), :] = jnp.concatenate(sums, axis=0)
         return upward
 
-    return lax.fori_loop(0, vector.shape[0] // ROWS, step, jnp.zeros_like(vector))
+    return loop(vector.shape[0] // ROWS, step, jnp.zeros_like(vector))
 
 
 def apply_blocks(blocks, vector, base_ref, out_ref):
@@ -81,7 +82,7 @@
         out_ref[pl.ds(start, ROWS), :] = base + jnp.concatenate(sums, axis=0)
         return carry
 
-    lax.fori_loop(0, vector.shape[0] // ROWS, step, 0)
+    loop(vector.shape[0] // ROWS, step, 0)
 
 
 def apply_transposed(blocks, vector_ref):
@@ -93,36 +94,30 @@
         return total
 
     zero = jnp.zeros(vector_ref.shape, F32)
-    return lax.fori_loop(0, vector_ref.shape[0] // ROWS, step, zero)
-
-
-def edges(blocks, scratch):
-    size, count = blocks.shape[0], blocks.shape[2]
-    lane = lax.broadcasted_iota(jnp.int32, (size, count), 1)
-
-    def step(chunk, tile):
-        start = chunk * ROWS
-        for s in range(ROWS):
-            turned = pltpu.roll(blocks[start + s].astype(F32), 2 * (start + s) + 1, 1)
-            tile = jnp.where(lax.shift_right_logical(lane, 1) == start + s, turned, tile)
-        return tile
-
-    tile = lax.fori_loop(0, size // ROWS, step, jnp.zeros((size, count), F32))
+    return loop(vector_ref.shape[0] // ROWS, step, zero)
+
+
+def loop(count, step, carry):
+    return lax.fori_loop(0, count, step, carry, unroll=True)
+
+
+def place(tile, block, row):
+    shape = (tile.shape[0] // ROWS, ROWS, tile.shape[1])
+    lane = lax.broadcasted_iota(jnp.int32, (1,) + shape[1:], 2)
+    mine = lax.shift_right_logical(lane, 1) == row
+    turned = pltpu.roll(block, 2 * row + 1, 1).reshape(shape)
+    return jnp.where(mine, turned, tile.reshape(shape)).reshape(tile.shape)
+
+
+def split(tile, scratch):
+    size = tile.shape[0]
     scratch[...] = jnp.transpose(tile)
     return scratch[pl.ds(1, size, stride=2), :], scratch[pl.ds(0, size, stride=2), :]
 
 
-def trial_sweep(rhs_ref, start_ref, diag, inverse, coupling, last_coupling, trial_ref, work_ref):
-    start = start_ref[...]
+def messages(rhs_ref, start, trial, upward, last_coupling):
     lane = lanes(start)
     end = start.shape[1] - 1
-    lower = jnp.where(lane == 0, 0.0, turn(start, 1))
-    upward = operate(diag, coupling, start_ref, work_ref, lower)
-    upper = jnp.where(lane == end, 0.0, turn(upward, -1))
-    defect = rhs_ref[...] - (work_ref[...] + upper)
-    apply_blocks(inverse, defect, start_ref, trial_ref)
-    trial = trial_ref[...]
-    upward = apply_transposed(coupling, trial_ref)
     to_left = rhs_ref[...] - turn(upward, -1)
     to_right = rhs_ref[...] - times(last_coupling, turn(trial, 1))
     right = jnp.where(
@@ -135,12 +130,82 @@
 
 
 def first_kernel(
-    rhs, guess, diag, inverse, coupling, trial, to_right, to_left, own, work, scratch
+    rhs_in, guess_in, diag_in, inverse_in, coupling_in, prolong_in, coarse_in, aggregate_in,
+    rhs, guess, diag, inverse, coupling, prolong, coarse, aggregate,
+    trial, to_right, to_left, own, diag_half, inverse_half, coupling_half, work, scratch, sems,
 ):
-    size = guess.shape[0]
-    first_diag, last_diag = edges(diag, scratch)
-    first_inverse, last_inverse = edges(inverse, scratch)
-    first_coupling, last_coupling = edges(coupling, scratch)
+    size, count = guess.shape
+    parts = diag_half.shape[0] // LOAD
+    copies = [
+        pltpu.make_async_copy(guess_in, guess, sems.at[0]),
+        pltpu.make_async_copy(rhs_in, rhs, sems.at[1]),
+    ]
+    for p in range(parts):
+        rows = pl.ds(p * LOAD, LOAD)
+        for source, target in ((coupling_in, coupling_half), (diag_in, diag_half)):
+            copies.append(
+                pltpu.make_async_copy(source.at[rows], target.at[rows], sems.at[len(copies)])
+            )
+    for p in range(parts):
+        rows = pl.ds(p * LOAD, LOAD)
+        copies.append(
+            pltpu.make_async_copy(inverse_in.at[rows], inverse_half.at[rows], sems.at[len(copies)])
+        )
+    for source, target in ((prolong_in, prolong), (coarse_in, coarse), (aggregate_in, aggregate)):
+        copies.append(pltpu.make_async_copy(source, target, sems.at[len(copies)]))
+    for copy in copies:
+        copy.start()
+    copies[0].wait()
+
+    start = guess[...]
+    lane = lanes(start)
+    lower = jnp.where(lane == 0, 0.0, turn(start, 1))
+    upward = jnp.zeros_like(start)
+    edge = jnp.zeros_like(start)
+    for chunk in range(size // ROWS):
+        if chunk * ROWS % LOAD == 0:
+            at = 2 + 2 * (chunk * ROWS // LOAD)
+            copies[at].wait()
+            copies[at + 1].wait()
+        sums = []
+        for i in range(chunk * ROWS, chunk * ROWS + ROWS):
+            pair = coupling_half[i].astype(F32)
+            block = diag_half[i].astype(F32)
+            coupling[i] = pair
+            diag[i] = block
+            edge = place(edge, block, i)
+            sums.append(jnp.sum(block * start + pair * lower, axis=0, keepdims=True))
+            upward = upward + pair * guess[i : i + 1, :]
+        work[pl.ds(chunk * ROWS, ROWS), :] = jnp.concatenate(sums, axis=0)
+    first_diag, last_diag = split(edge, scratch.at[0])
+    upper = jnp.where(lane == count - 1, 0.0, turn(upward, -1))
+    copies[1].wait()
+    defect = rhs[...] - (work[...] + upper)
+
+    edge = jnp.zeros_like(start)
+    for chunk in range(size // ROWS):
+        if chunk * ROWS % LOAD == 0:
+            copies[2 + 2 * parts + chunk * ROWS // LOAD].wait()
+        rows = pl.ds(chunk * ROWS, ROWS)
+        sums = []
+        for i in range(chunk * ROWS, chunk * ROWS + ROWS):
+            block = inverse_half[i].astype(F32)
+            inverse[i] = block
+            edge = place(edge, block, i)
+            sums.append(jnp.sum(block * defect, axis=0, keepdims=True))
+        trial[rows, :] = guess[rows, :] + jnp.concatenate(sums, axis=0)
+    first_inverse, last_inverse = split(edge, scratch.at[1])
+
+    upward = jnp.zeros_like(start)
+    edge = jnp.zeros_like(start)
+    for i in range(size):
+        edge = place(edge, coupling[i], i)
+        upward = upward + coupling[i] * trial[i : i + 1, :]
+    first_coupling, last_coupling = split(edge, scratch.at[2])
+
+    right, left = messages(rhs, start, trial[...], upward, last_coupling)
+    to_right[0] = right
+    to_left[0] = left
     to_right[1] = jnp.concatenate([last_diag, last_inverse], axis=1)
     to_left[1] = jnp.concatenate([first_diag, first_inverse], axis=1)
     to_left[2] = jnp.concatenate([first_coupling, first_coupling], axis=1)
@@ -148,9 +213,8 @@
     own[1] = first_inverse.astype(BF16)
     own[2] = last_coupling.astype(BF16)
     own[3] = last_inverse.astype(BF16)
-    right, left = trial_sweep(rhs, guess, diag, inverse, coupling, last_coupling, trial, work)
-    to_right[0] = right
-    to_left[0] = left
+    for copy in copies[-3:]:
+        copy.wait()
 
 
 def finish(
@@ -224,17 +288,18 @@
     )
 
 
-def coarse_kernel(shares, coarse_inverse, out, work, zero):
-    size, own = coarse_inverse.shape[0], coarse_inverse.shape[2]
+def coarse_kernel(shares, coarse_inverse, out):
+    size = coarse_inverse.shape[0]
     rows = shares.shape[0] // ROWS
     share = shares[0:ROWS]
     for row in range(1, rows):
         share = share + shares[row * ROWS : (row + 1) * ROWS]
-    flipped = jnp.transpose(share)
-    vector = jnp.concatenate([flipped[:size], flipped[size:]], axis=1)
-    zero[...] = jnp.zeros_like(vector)
-    apply_blocks(coarse_inverse, vector, zero, work)
-    value = jnp.transpose(work[...])
+    share = jnp.concatenate([share[:, :size], share[:, size:]], axis=0)
+    lane = lanes(share)
+    value = jnp.zeros_like(share)
+    for i in range(size):
+        total = jnp.sum(coarse_inverse[i].astype(F32) * share, axis=1, keepdims=True)
+        value = jnp.where(lane == i, total, value)
     value = jnp.concatenate([value[:ROWS], value[ROWS:]], axis=1)
     for row in range(rows):
         out[row * ROWS : (row + 1) * ROWS] = value
@@ -242,7 +307,7 @@
 
 def third_kernel(
     group_count, rhs, twice, values, diag, inverse, coupling, own, prolong, aggregate,
-    start, trial, to_right, to_left, work,
+    start_ref, trial, to_right, to_left, work,
 ):
     size = twice.shape[0]
     spread = jnp.zeros(twice.shape, F32)
@@ -254,8 +319,15 @@
                 part, picked, (((0,), (0,)), ((), ())), preferred_element_type=F32
             )
             spread = spread + both[half * size : (half + 1) * size]
-    apply_blocks(prolong, spread, twice, start)
-    right, left = trial_sweep(rhs, start, diag, inverse, coupling, own[2], trial, work)
+    apply_blocks(prolong, spread, twice, start_ref)
+    start = start_ref[...]
+    lane = lanes(start)
+    lower = jnp.where(lane == 0, 0.0, turn(start, 1))
+    upward = operate(diag, coupling, start_ref, work, lower)
+    upper = jnp.where(lane == start.shape[1] - 1, 0.0, turn(upward, -1))
+    apply_blocks(inverse, rhs[...] - (work[...] + upper), start_ref, trial)
+    upward = apply_transposed(coupling, trial)
+    right, left = messages(rhs, start, trial[...], upward, own[2])
     to_right[...] = right
     to_left[...] = left
 
@@ -270,15 +342,17 @@
     )
 
 
-def call(kernel, outs, scratch, *operands):
+def call(kernel, outs, scratch, *operands, space=pltpu.VMEM):
     inside = pl.BlockSpec(memory_space=pltpu.VMEM)
+    if space == pltpu.HBM:
+        operands = [pltpu.with_memory_space_constraint(x, space) for x in operands]
     single = not isinstance(outs, tuple)
     return pl.pallas_call(
         kernel,
         out_shape=outs,
-        in_specs=[inside] * len(operands),
+        in_specs=[pl.BlockSpec(memory_space=space)] * len(operands),
         out_specs=inside if single else (inside,) * len(outs),
-        scratch_shapes=[pltpu.VMEM(shape, F32) for shape in scratch],
+        scratch_shapes=scratch,
         compiler_params=pltpu.CompilerParams(vmem_limit_bytes=24 << 20),
     )(*operands)
 
@@ -287,42 +361,57 @@
     size, count = rhs.shape
     rows = lax.axis_size("row")
     group_count = count * rows // AGG
-    own_coarse = coarse_inverse.shape[2]
-    assert own_coarse == 2 * ROWS and 2 * size == count
-    tile = jax.ShapeDtypeStruct((size, count), F32)
+    assert coarse_inverse.shape[2] == 2 * ROWS and 2 * size == count
     aggregate = aggregate.reshape(1, count)
-
-    def stack(n):
-        return jax.ShapeDtypeStruct((n, size, count), F32)
-
-    packed = jax.ShapeDtypeStruct((group_count // 2, count), F32)
-    own_shape = jax.ShapeDtypeStruct((4, size, size), BF16)
-    plain = (size, count)
-    trial, to_right, to_left, own = call(
-        first_kernel, (tile, stack(2), stack(3), own_shape), [plain, (count, size)],
-        rhs, guess, diag_blocks, diag_inverse, coupling,
+    coarse_inverse = jnp.transpose(coarse_inverse, (0, 2, 1))
+
+    def shape(*sizes, kind=F32):
+        return jax.ShapeDtypeStruct(sizes, kind)
+
+    tile = shape(size, count)
+    blocks = shape(size, size, count)
+    packed = shape(group_count // 2, count)
+    plain = pltpu.VMEM((size, count), F32)
+    half = pltpu.VMEM((size, size, count), BF16)
+    loads = 2 + 3 * (size // LOAD) + 3
+    (
+        rhs, guess, diag, inverse, coupling, prolong, coarse_inverse, aggregate,
+        trial, to_right, to_left, own,
+    ) = call(
+        first_kernel,
+        (
+            tile, tile, blocks, blocks, blocks,
+            shape(size, size, count, kind=BF16),
+            shape(*coarse_inverse.shape, kind=BF16),
+            shape(1, count, kind=jnp.int32),
+            tile, shape(2, size, count), shape(3, size, count), shape(4, size, size, kind=BF16),
+        ),
+        [
+            half, half, half, plain, pltpu.VMEM((3, count, size), F32),
+            pltpu.SemaphoreType.DMA((loads,)),
+        ],
+        rhs, guess, diag_blocks, diag_inverse, coupling, prolong, coarse_inverse, aggregate,
+        space=pltpu.HBM,
     )
     from_left = from_behind(to_right, 1)
     from_right = from_behind(to_left, -1)
     twice, partial = call(
         functools.partial(second_kernel, group_count), (tile, packed), [plain, plain],
-        rhs, guess, trial, diag_blocks, diag_inverse, coupling, own, from_left, from_right,
+        rhs, guess, trial, diag, inverse, coupling, own, from_left, from_right,
         prolong, aggregate,
     )
     shares = lax.all_to_all(partial, "row", 0, 0, tiled=True)
-    corrected = call(
-        coarse_kernel, packed, [(size, own_coarse), (size, own_coarse)], shares, coarse_inverse
-    )
+    corrected = call(coarse_kernel, packed, [], shares, coarse_inverse)
     values = lax.all_to_all(corrected, "row", 0, 0, tiled=True)
     start, trial, to_right, to_left = call(
         functools.partial(third_kernel, group_count), (tile, tile, tile, tile), [plain],
-        rhs, twice, values, diag_blocks, diag_inverse, coupling, own, prolong, aggregate,
+        rhs, twice, values, diag, inverse, coupling, own, prolong, aggregate,
     )
     next_left = from_behind(to_right, 1)
     next_right = from_behind(to_left, -1)
     return call(
         fourth_kernel, (tile, tile), [plain, plain],
-        rhs, start, trial, diag_blocks, diag_inverse, coupling, own, next_left, next_right,
+        rhs, start, trial, diag, inverse, coupling, own, next_left, next_right,
         from_left, from_right,
     )
 

time: 71.8 us -> 57.6 us (0.80)
  local copies, waits for them, and re-layouts: 10.7 us -> 0 us
  blocking collectives: 7.85 us -> 16.9 us
  starting transfers between devices: 28 us -> 20.3 us
  Pallas kernels: 15 us -> 10.7 us
    unnamed x27 -> x0, local copies, waits for them, and re-layouts: 10.7 us -> none
    all_to_all x0 -> x1, blocking collectives: none -> 8.67 us  [local(): shares = lax.all_to_all(partial, 'row', 0, 0, tiled=True)]
    all_to_all x1 -> x0, starting transfers between devices: 7.81 us -> none  [local(): shares = lax.all_to_all(partial, 'row', 0, 0, tiled=True)]
    pallas_call x5, Pallas kernels: 15 us -> 10.7 us  [call(): pl.pallas_call(kernel, out_shape=outs, in_specs=[pl.BlockSpec(memory_spac...]
  transfers between devices with their start and end apart: 5 -> 4, of which waited for: 2 -> 2; matrix products, arithmetic and copies ran while one was open for 3% -> 0% of each run, Pallas kernels for 0% -> 0%
where the time goes in v2:
time: 57.6 us; the launch traced here: 57.3 us
  starting transfers between devices  20.3 us (35%)
  blocking collectives  16.9 us (29%)
  Pallas kernels  10.7 us (19%)
  waiting for transfers between devices  8.78 us (15%)
  between operations  0.73 us (1%)
    ppermute x4, starting transfers between devices, from_behind(): return lax.ppermute(block, BOTH, route)  20.3 us
    pallas_call x5, Pallas kernels, call(): pl.pallas_call(kernel, out_shape=outs, in_specs=[pl.BlockSpec(memory_spac...  10.7 us
    ppermute x4, waiting for transfers between devices, from_behind(): return lax.ppermute(block, BOTH, route)  8.78 us
    all_to_all x1, blocking collectives, local(): shares = lax.all_to_all(partial, 'row', 0, 0, tiled=True)  8.67 us
    all_to_all x1, blocking collectives, local(): values = lax.all_to_all(corrected, 'row', 0, 0, tiled=True)  8.21 us
  transfers between devices with their start and end apart: 4, of which 2 were waited for; matrix products, arithmetic and copies ran while one was open for 0% of the time, Pallas kernels for 0%

profile of v2, /device:TPU:29, one launch (start us, length us, event | category | flops | bytes accessed | tf_op | source)
XLA Modules:
  0.0 57.3 jit_solution(13856307437093601502)
XLA Ops:
  0.6 3.8 %shard_map.95 = (f32[64,128]{1,0:T(8,128)S(1)}, f32[64,128]{1,0:T(8,128)S(1)}, f32[64,64,128]{2,1,0:T(8,128)S(1)}, f32[64,64,128]{2,1,0:T(8,128)S(1)}, f32[64,64...) custom-call(f32[64,128]{1,0:T(8,128)} %rhs_in.1, ...), custom_call_target="tpu_custom_call" | custom-call | tf_op jit(solution)/shard_map/pallas_call | solution.py:350
  4.4 2.1 %collective-permute-start.1 = (f32[3,64,128]{2,1,0:T(8,128)S(1)}, f32[3,64,128]{2,1,0:T(8,128)S(1)}, u32[]{:S(2)}, u32[]{:S(2)}) collective-permute-start(f32[3,64,128]{2,1,0:T(8,128)S(1)} %get-tuple-element.28), channel_id=1, source_target_pairs={{1,0},{2,1},{3,2},{4,3},{5,4},{6,5},{7,6},{8,7},{9,8},{10,9},{11,1... | collective-permute-start | bytes 294920 | tf_op jit(solution)/shard_map/ppermute | solution.py:21
  6.6 7.0 %collective-permute-start = (f32[2,64,128]{2,1,0:T(8,128)S(1)}, f32[2,64,128]{2,1,0:T(8,128)S(1)}, u32[]{:S(2)}, u32[]{:S(2)}) collective-permute-start(f32[2,64,128]{2,1,0:T(8,128)S(1)} %get-tuple-element.27), channel_id=1, source_target_pairs={{0,1},{1,2},{2,3},{3,4},{4,5},{5,6},{6,7},{7,8},{8,9},{9,10},{10,1... | collective-permute-start | bytes 196616 | tf_op jit(solution)/shard_map/ppermute | solution.py:21
  13.6 1.9 %collective-permute-done.from_left.left_blocks = f32[2,64,128]{2,1,0:T(8,128)S(1)} collective-permute-done((f32[2,64,128]{2,1,0:T(8,128)S(1)}, f32[2,64,128]{2,1,0:T(8,128)S(1)}, u32[]{:S(2)}, u32[]{:S(2)}) %collective-permute-start) | collective-permute-done | bytes 65568 | tf_op jit(solution)/shard_map/ppermute | solution.py:21
  15.5 0.0 collective-permute-done.1.from_right.right_blocks
  15.5 2.3 %shard_map.96 = (f32[64,128]{1,0:T(8,128)S(1)}, f32[64,128]{1,0:T(8,128)S(1)}) custom-call(f32[64,128]{1,0:T(8,128)S(1)} %get-tuple-element.20.rhs, f32[64,128]{1,0:T(8,128)S(1)} %get-tuple-element.21.guess, f32[64,128]{1,0:T(8,128)S(1)} %get-tuple-element.22.trial, f32[64,64,128]{2,1,0:T(8,128)S(1)} %get-tuple-element.23.diag, ...), custom_call_target="tpu_custom_call" | custom-call | tf_op jit(solution)/shard_map/pallas_call | solution.py:350
  17.8 8.7 %all_to_all.22 = f32[8,8,128]{2,1,0:T(8,128)S(1)} all-to-all(f32[8,8,128]{2,1,0:T(8,128)S(1)} %bitcast.9), channel_id=1, replica_groups=mesh['grp'=4,'row'=8] {'row'}, dimensions={0} | all-to-all | bytes 65536 | tf_op jit(solution)/shard_map/all_to_all | solution.py:403
  26.5 0.3 shard_map.97
  26.8 8.2 %all_to_all.23 = f32[8,8,128]{2,1,0:T(8,128)S(1)} all-to-all(f32[8,8,128]{2,1,0:T(8,128)S(1)} %bitcast.8), channel_id=1, replica_groups=mesh['grp'=4,'row'=8] {'row'}, dimensions={0} | all-to-all | bytes 65536 | tf_op jit(solution)/shard_map/all_to_all | solution.py:405
  35.0 1.8 %shard_map.98 = (f32[64,128]{1,0:T(8,128)S(1)}, f32[64,128]{1,0:T(8,128)S(1)}, f32[64,128]{1,0:T(8,128)S(1)}, f32[64,128]{1,0:T(8,128)S(1)}) custom-call(f32[64,128]{1,0:T(8,128)S(1)} %get-tuple-element.20.rhs, f32[64,128]{1,0:T(8,128)S(1)} %get-tuple-element.31.twice, f32[64,128]{1,0:T(8,128)S(1)} %bitcast.6, f32[64,64,128]{2,1,0:T(8,128)S(1)} %get-tuple-element.23.diag, ...), custom_call_target="tpu_custom_call" | custom-call | tf_op jit(solution)/shard_map/pallas_call | solution.py:350
  36.8 9.2 %collective-permute-start.2 = (f32[64,128]{1,0:T(8,128)S(1)}, f32[64,128]{1,0:T(8,128)S(1)}, u32[]{:S(2)}, u32[]{:S(2)}) collective-permute-start(f32[64,128]{1,0:T(8,128)S(1)} %get-tuple-element.36), channel_id=1, source_target_pairs={{0,1},{1,2},{2,3},{3,4},{4,5},{5,6},{6,7},{7,8},{8,9},{9,10},{10,1... | collective-permute-start | bytes 98312 | tf_op jit(solution)/shard_map/ppermute | solution.py:21
  46.1 1.9 %collective-permute-start.3 = (f32[64,128]{1,0:T(8,128)S(1)}, f32[64,128]{1,0:T(8,128)S(1)}, u32[]{:S(2)}, u32[]{:S(2)}) collective-permute-start(f32[64,128]{1,0:T(8,128)S(1)} %get-tuple-element.37), channel_id=1, source_target_pairs={{1,0},{2,1},{3,2},{4,3},{5,4},{6,5},{7,6},{8,7},{9,8},{10,9},{11,1... | collective-permute-start | bytes 98312 | tf_op jit(solution)/shard_map/ppermute | solution.py:21
  48.0 0.0 collective-permute-done.2.from_left
  48.0 6.9 %collective-permute-done.3.from_right = f32[64,128]{1,0:T(8,128)S(1)} collective-permute-done((f32[64,128]{1,0:T(8,128)S(1)}, f32[64,128]{1,0:T(8,128)S(1)}, u32[]{:S(2)}, u32[]{:S(2)}) %collective-permute-start.3) | collective-permute-done | bytes 32800 | tf_op jit(solution)/shard_map/ppermute | solution.py:21
  54.9 2.5 %shard_map.99 = (f32[64,128]{1,0:T(8,128)}, f32[64,128]{1,0:T(8,128)}) custom-call(f32[64,128]{1,0:T(8,128)S(1)} %get-tuple-element.20.rhs, f32[64,128]{1,0:T(8,128)S(1)} %get-tuple-element.34.start, f32[64,128]{1,0:T(8,128)S(1)} %get-tuple-element.35.trial, f32[64,64,128]{2,1,0:T(8,128)S(1)} %get-tuple-element.23.diag, ...), custom_call_target="tpu_custom_call" | custom-call | tf_op jit(solution)/shard_map/pallas_call | solution.py:350
Async XLA Ops:
  4.4 11.1 %collective-permute-start.1 = (f32[3,64,128]{2,1,0:T(8,128)S(1)}, f32[3,64,128]{2,1,0:T(8,128)S(1)}, u32[]{:S(2)}, u32[]{:S(2)}) collective-permute-start(f32[3,64,128]{2,1,0:T(8,128)S(1)} %get-tuple-element.28), channel_id=1, source_target_pairs={{1,0},{2,1},{3,2},{4,3},{5,4},{6,5},{7,6},{8,7},{9,8},{10,9},{11,1... | collective-permute-start | bytes 294920 | tf_op jit(solution)/shard_map/ppermute | solution.py:21
  6.6 8.9 %collective-permute-start = (f32[2,64,128]{2,1,0:T(8,128)S(1)}, f32[2,64,128]{2,1,0:T(8,128)S(1)}, u32[]{:S(2)}, u32[]{:S(2)}) collective-permute-start(f32[2,64,128]{2,1,0:T(8,128)S(1)} %get-tuple-element.27), channel_id=1, source_target_pairs={{0,1},{1,2},{2,3},{3,4},{4,5},{5,6},{6,7},{7,8},{8,9},{9,10},{10,1... | collective-permute-start | bytes 196616 | tf_op jit(solution)/shard_map/ppermute | solution.py:21
  36.8 11.1 %collective-permute-start.2 = (f32[64,128]{1,0:T(8,128)S(1)}, f32[64,128]{1,0:T(8,128)S(1)}, u32[]{:S(2)}, u32[]{:S(2)}) collective-permute-start(f32[64,128]{1,0:T(8,128)S(1)} %get-tuple-element.36), channel_id=1, source_target_pairs={{0,1},{1,2},{2,3},{3,4},{4,5},{5,6},{6,7},{7,8},{8,9},{9,10},{10,1... | collective-permute-start | bytes 98312 | tf_op jit(solution)/shard_map/ppermute | solution.py:21
  46.1 8.8 %collective-permute-start.3 = (f32[64,128]{1,0:T(8,128)S(1)}, f32[64,128]{1,0:T(8,128)S(1)}, u32[]{:S(2)}, u32[]{:S(2)}) collective-permute-start(f32[64,128]{1,0:T(8,128)S(1)} %get-tuple-element.37), channel_id=1, source_target_pairs={{1,0},{2,1},{3,2},{4,3},{5,4},{6,5},{7,6},{8,7},{9,8},{10,9},{11,1... | collective-permute-start | bytes 98312 | tf_op jit(solution)/shard_map/ppermute | solution.py:21

commit v3 on v2

--- a/solution.py
+++ b/solution.py
@@ -15,10 +15,13 @@
 LOAD = 16
 
 
-def from_behind(block, distance):
-    devices = range(lax.axis_size(BOTH))
-    route = [(i - distance, i) for i in devices if i - distance in devices]
-    return lax.ppermute(block, BOTH, route)
+def swap(block, first):
+    pairs = [(i, i + 1) for i in range(first, lax.axis_size(BOTH) - 1, 2)]
+    return lax.ppermute(block, BOTH, pairs + [(j, i) for i, j in pairs])
+
+
+def even_device():
+    return lax.rem(lax.axis_index("row"), 2) == 0
 
 
 def lanes(like):
@@ -101,11 +104,11 @@
     return lax.fori_loop(0, count, step, carry, unroll=True)
 
 
-def place(tile, block, row):
+def place(tile, block, row, spacing):
     shape = (tile.shape[0] // ROWS, ROWS, tile.shape[1])
     lane = lax.broadcasted_iota(jnp.int32, (1,) + shape[1:], 2)
-    mine = lax.shift_right_logical(lane, 1) == row
-    turned = pltpu.roll(block, 2 * row + 1, 1).reshape(shape)
+    mine = lax.shift_right_logical(lane, spacing // 2) == row
+    turned = pltpu.roll(block, spacing * row + 1, 1).reshape(shape)
     return jnp.where(mine, turned, tile.reshape(shape)).reshape(tile.shape)
 
 
@@ -115,24 +118,44 @@
     return scratch[pl.ds(1, size, stride=2), :], scratch[pl.ds(0, size, stride=2), :]
 
 
-def messages(rhs_ref, start, trial, upward, last_coupling):
-    lane = lanes(start)
-    end = start.shape[1] - 1
-    to_left = rhs_ref[...] - turn(upward, -1)
-    to_right = rhs_ref[...] - times(last_coupling, turn(trial, 1))
-    right = jnp.where(
-        lane == 0, turn(start, 1), jnp.where(lane == 1, turn(trial, 2), turn(to_right, 3))
-    )
-    left = jnp.where(
-        lane == end, turn(start, -1), jnp.where(lane == end - 1, turn(trial, -2), turn(to_left, -3))
-    )
-    return right, left
+def split_more(tiles, scratch):
+    half = tiles[0].shape[0] // 2
+    for t in (0, 1):
+        scratch[t] = jnp.transpose(tiles[t])
+    return [
+        jnp.concatenate([scratch[t, pl.ds(k, half, stride=4), :] for t in (0, 1)], axis=0)
+        for k in (1, 2, 0)
+    ]
+
+
+def message(columns, rightward):
+    lane = lanes(columns[0])
+    middle = lane.shape[1] // 2
+    shift = middle + jnp.where(rightward, 1, 0)
+    tile = jnp.zeros(lane.shape, F32)
+    for k, column in enumerate(columns):
+        tile = jnp.where(lane == middle + k, pltpu.roll(column, shift + k, 1), tile)
+    high, rest, last = three(tile)
+    return high.astype(F32) + turn(rest.astype(F32), 3) + turn(last.astype(F32), 6)
+
+
+def columns_of(tile):
+    return tile + (turn(tile, -3) + turn(tile, -6))
+
+
+def wrong(rhs_ref, vector_ref, diag, coupling, work):
+    vector = vector_ref[...]
+    lane = lanes(vector)
+    lower = jnp.where(lane == 0, 0.0, turn(vector, 1))
+    upward = operate(diag, coupling, vector_ref, work, lower)
+    upper = jnp.where(lane == vector.shape[1] - 1, 0.0, turn(upward, -1))
+    return rhs_ref[...] - (work[...] + upper)
 
 
 def first_kernel(
     rhs_in, guess_in, diag_in, inverse_in, coupling_in, prolong_in, coarse_in, aggregate_in,
     rhs, guess, diag, inverse, coupling, prolong, coarse, aggregate,
-    trial, to_right, to_left, own, diag_half, inverse_half, coupling_half, work, scratch, sems,
+    trial, defect_out, near, far, own, diag_half, inverse_half, coupling_half, work, scratch, sems,
 ):
     size, count = guess.shape
     parts = diag_half.shape[0] // LOAD
@@ -173,7 +196,7 @@
             block = diag_half[i].astype(F32)
             coupling[i] = pair
             diag[i] = block
-            edge = place(edge, block, i)
+            edge = place(edge, block, i, 2)
             sums.append(jnp.sum(block * start + pair * lower, axis=0, keepdims=True))
             upward = upward + pair * guess[i : i + 1, :]
         work[pl.ds(chunk * ROWS, ROWS), :] = jnp.concatenate(sums, axis=0)
@@ -191,71 +214,107 @@
         for i in range(chunk * ROWS, chunk * ROWS + ROWS):
             block = inverse_half[i].astype(F32)
             inverse[i] = block
-            edge = place(edge, block, i)
+            edge = place(edge, block, i, 2)
             sums.append(jnp.sum(block * defect, axis=0, keepdims=True))
         trial[rows, :] = guess[rows, :] + jnp.concatenate(sums, axis=0)
     first_inverse, last_inverse = split(edge, scratch.at[1])
 
+    second = trial[...]
+    lower = jnp.where(lane == 0, 0.0, turn(second, 1))
     upward = jnp.zeros_like(start)
-    edge = jnp.zeros_like(start)
-    for i in range(size):
-        edge = place(edge, coupling[i], i)
-        upward = upward + coupling[i] * trial[i : i + 1, :]
-    first_coupling, last_coupling = split(edge, scratch.at[2])
-
-    right, left = messages(rhs, start, trial[...], upward, last_coupling)
-    to_right[0] = right
-    to_left[0] = left
-    to_right[1] = jnp.concatenate([last_diag, last_inverse], axis=1)
-    to_left[1] = jnp.concatenate([first_diag, first_inverse], axis=1)
-    to_left[2] = jnp.concatenate([first_coupling, first_coupling], axis=1)
-    own[0] = first_coupling.astype(BF16)
-    own[1] = first_inverse.astype(BF16)
-    own[2] = last_coupling.astype(BF16)
-    own[3] = last_inverse.astype(BF16)
+    edge = [jnp.zeros_like(start), jnp.zeros_like(start)]
+    for chunk in range(size // ROWS):
+        sums = []
+        for i in range(chunk * ROWS, chunk * ROWS + ROWS):
+            pair = coupling[i]
+            t, row = divmod(i, size // 2)
+            edge[t] = place(edge[t], pair, row, 4)
+            sums.append(jnp.sum(diag[i] * second + pair * lower, axis=0, keepdims=True))
+            upward = upward + pair * trial[i : i + 1, :]
+        work[pl.ds(chunk * ROWS, ROWS), :] = jnp.concatenate(sums, axis=0)
+    first_coupling, second_coupling, last_coupling = split_more(edge, scratch.at[2:4])
+    upper = jnp.where(lane == count - 1, 0.0, turn(upward, -1))
+    defect = rhs[...] - (work[...] + upper)
+    defect_out[...] = defect
+
+    even = even_device()
+    columns = (start, second, defect)
+    lasts = jnp.concatenate([last_diag, last_inverse], axis=1)
+    firsts = jnp.concatenate([first_diag, first_inverse], axis=1)
+    link = jnp.concatenate([first_coupling, jnp.zeros_like(first_coupling)], axis=1)
+    near[0] = jnp.where(even, lasts, firsts).astype(BF16)
+    near[1] = (message(columns, even) + link).astype(BF16)
+    far[0] = jnp.where(even, firsts, lasts).astype(BF16)
+    far[1] = (message(columns, jnp.logical_not(even)) + link).astype(BF16)
+    for k, block in enumerate(
+        (
+            first_diag, first_inverse, first_coupling, second_coupling,
+            last_diag, last_inverse, last_coupling,
+        )
+    ):
+        own[k] = block.astype(BF16)
     for copy in copies[-3:]:
         copy.wait()
 
 
 def finish(
-    rhs, start_ref, trial_ref, diag, inverse, coupling, own, left, right,
-    left_blocks, right_blocks, twice_ref, work_ref, once_ref,
+    rhs, start_ref, trial_ref, defect_ref, diag, inverse, coupling, own, near, far,
+    near_blocks, far_blocks, twice_ref, work_ref,
 ):
-    start, trial = start_ref[...], trial_ref[...]
+    start = start_ref[...]
     size = start.shape[0]
     lane = lanes(start)
     end = start.shape[1] - 1
+    middle = start.shape[1] // 2
     at_start, at_end = lane == 0, lane == end
-    left_diag, left_inverse = left_blocks[0][:, :size], left_blocks[0][:, size:]
-    right_diag, right_inverse = right_blocks[0][:, :size], right_blocks[0][:, size:]
-    right_coupling = right_blocks[1][:, :size]
-    first_coupling, first_inverse, last_inverse = own[0], own[1], own[3]
-
-    up_right = times_transposed(right_coupling, right)
-    down_left = times(first_coupling, left)
-    once = trial - jnp.where(
-        at_start,
-        times(first_inverse, down_left),
-        jnp.where(at_end, times(last_inverse, up_right), 0.0),
-    )
-    once_ref[...] = once
-    left_once = turn(left, -1) - times(left_inverse, times_transposed(first_coupling, start))
-    right_once = turn(right, 1) - times(right_inverse, times(right_coupling, start))
-    left_twice = left_once + times(
-        left_inverse,
-        turn(left, -2) - times(left_diag, left_once) - times_transposed(first_coupling, once),
-    )
-    right_twice = right_once + times(
-        right_inverse,
-        turn(right, 2) - times(right_diag, right_once) - times(right_coupling, once),
-    )
-
-    upward = operate(
-        diag, coupling, once_ref, work_ref, jnp.where(at_start, left_once, turn(once, 1))
-    )
-    upper = jnp.where(at_end, times_transposed(right_coupling, right_once), turn(upward, -1))
-    defect = rhs[...] - (work_ref[...] + upper)
-    apply_blocks(inverse, defect, once_ref, twice_ref)
+    even = even_device()
+    near, far = near[...].astype(F32), far[...].astype(F32)
+    left = columns_of(jnp.where(even, far, near))
+    right = columns_of(jnp.where(even, near, far))
+    near_pair, far_pair = near_blocks[0].astype(F32), far_blocks[0].astype(F32)
+    left_pair = jnp.where(even, far_pair, near_pair).astype(BF16)
+    right_pair = jnp.where(even, near_pair, far_pair).astype(BF16)
+    near_link, far_link = near_blocks[1].astype(F32), far_blocks[1].astype(F32)
+    right_coupling = jnp.where(even, near_link, far_link)[:, :size].astype(BF16)
+    left_diag, left_inverse = left_pair[:, :size], left_pair[:, size:]
+    right_diag, right_inverse = right_pair[:, :size], right_pair[:, size:]
+    (
+        first_diag, first_inverse, first_coupling, second_coupling,
+        last_diag, last_inverse, last_coupling,
+    ) = (own[k] for k in range(7))
+
+    def at_ends(first, last):
+        return jnp.where(at_start, first, jnp.where(at_end, last, 0.0))
+
+    down = times(first_coupling, turn(left, -middle))
+    up = times_transposed(right_coupling, turn(right, middle - 1))
+    change = -at_ends(times(first_inverse, down), times(last_inverse, up))
+    once = trial_ref[...] + change
+    left_change = times(left_inverse, times_transposed(first_coupling, -start))
+    right_change = times(right_inverse, times(right_coupling, -start))
+    left_once = turn(left, -middle - 1) + left_change
+    right_once = turn(right, middle - 2) + right_change
+    defect = (
+        defect_ref[...]
+        - at_ends(
+            times(first_diag, change) + times(first_coupling, left_once),
+            times(last_diag, change) + times_transposed(right_coupling, right_once),
+        )
+        - jnp.where(lane == 1, turn(times(second_coupling, change), 1), 0.0)
+        - jnp.where(lane == end - 1, turn(times_transposed(last_coupling, change), -1), 0.0)
+    )
+    work_ref[...] = once
+    apply_blocks(inverse, defect, work_ref, twice_ref)
+    left_defect = (
+        turn(left, -middle - 2)
+        - times(left_diag, left_change)
+        - times_transposed(first_coupling, once)
+    )
+    right_defect = (
+        turn(right, middle - 3) - times(right_diag, right_change) - times(right_coupling, once)
+    )
+    left_twice = left_once + times(left_inverse, left_defect)
+    right_twice = right_once + times(right_inverse, right_defect)
     twice = twice_ref[...]
     upward = operate(
         diag, coupling, twice_ref, work_ref, jnp.where(at_start, left_twice, turn(twice, 1))
@@ -273,12 +332,12 @@
 
 
 def second_kernel(
-    group_count, rhs, guess, trial, diag, inverse, coupling, own, from_left, from_right,
-    prolong, aggregate, twice, partial, work, once,
+    group_count, rhs, guess, trial, defect, diag, inverse, coupling, own, near, far,
+    prolong, aggregate, twice, partial, work,
 ):
     residual = finish(
-        rhs, guess, trial, diag, inverse, coupling, own, from_left[0], from_right[0],
-        from_left.at[1:], from_right.at[1:], twice, work, once,
+        rhs, guess, trial, defect, diag, inverse, coupling, own, near.at[1], far.at[1],
+        near, far, twice, work,
     )
     work[...] = residual
     pieces = apply_transposed(prolong, work)
@@ -307,7 +366,7 @@
 
 def third_kernel(
     group_count, rhs, twice, values, diag, inverse, coupling, own, prolong, aggregate,
-    start_ref, trial, to_right, to_left, work,
+    start_ref, trial, defect_out, near, far, work,
 ):
     size = twice.shape[0]
     spread = jnp.zeros(twice.shape, F32)
@@ -320,25 +379,22 @@
             )
             spread = spread + both[half * size : (half + 1) * size]
     apply_blocks(prolong, spread, twice, start_ref)
-    start = start_ref[...]
-    lane = lanes(start)
-    lower = jnp.where(lane == 0, 0.0, turn(start, 1))
-    upward = operate(diag, coupling, start_ref, work, lower)
-    upper = jnp.where(lane == start.shape[1] - 1, 0.0, turn(upward, -1))
-    apply_blocks(inverse, rhs[...] - (work[...] + upper), start_ref, trial)
-    upward = apply_transposed(coupling, trial)
-    right, left = messages(rhs, start, trial[...], upward, own[2])
-    to_right[...] = right
-    to_left[...] = left
+    apply_blocks(inverse, wrong(rhs, start_ref, diag, coupling, work), start_ref, trial)
+    defect = wrong(rhs, trial, diag, coupling, work)
+    defect_out[...] = defect
+    even = even_device()
+    columns = (start_ref[...], trial[...], defect)
+    near[...] = message(columns, even).astype(BF16)
+    far[...] = message(columns, jnp.logical_not(even)).astype(BF16)
 
 
 def fourth_kernel(
-    rhs, start, trial, diag, inverse, coupling, own, from_left, from_right,
-    left_blocks, right_blocks, twice, residual, work, once,
+    rhs, start, trial, defect, diag, inverse, coupling, own, near, far, near_blocks, far_blocks,
+    twice, residual, work,
 ):
     residual[...] = finish(
-        rhs, start, trial, diag, inverse, coupling, own, from_left[...], from_right[...],
-        left_blocks.at[1:], right_blocks.at[1:], twice, work, once,
+        rhs, start, trial, defect, diag, inverse, coupling, own, near, far,
+        near_blocks, far_blocks, twice, work,
     )
 
 
@@ -361,7 +417,7 @@
     size, count = rhs.shape
     rows = lax.axis_size("row")
     group_count = count * rows // AGG
-    assert coarse_inverse.shape[2] == 2 * ROWS and 2 * size == count
+    assert coarse_inverse.shape[2] == 2 * ROWS and 2 * size == count and rows % 2 == 0
     aggregate = aggregate.reshape(1, count)
     coarse_inverse = jnp.transpose(coarse_inverse, (0, 2, 1))
 
@@ -371,12 +427,14 @@
     tile = shape(size, count)
     blocks = shape(size, size, count)
     packed = shape(group_count // 2, count)
+    edge = shape(2, size, count, kind=BF16)
+    line = shape(size, count, kind=BF16)
     plain = pltpu.VMEM((size, count), F32)
     half = pltpu.VMEM((size, size, count), BF16)
     loads = 2 + 3 * (size // LOAD) + 3
     (
         rhs, guess, diag, inverse, coupling, prolong, coarse_inverse, aggregate,
-        trial, to_right, to_left, own,
+        trial, defect, near, far, own,
     ) = call(
         first_kernel,
         (
@@ -384,35 +442,35 @@
             shape(size, size, count, kind=BF16),
             shape(*coarse_inverse.shape, kind=BF16),
             shape(1, count, kind=jnp.int32),
-            tile, shape(2, size, count), shape(3, size, count), shape(4, size, size, kind=BF16),
+            tile, tile, edge, edge, shape(7, size, size, kind=BF16),
         ),
         [
-            half, half, half, plain, pltpu.VMEM((3, count, size), F32),
+            half, half, half, plain, pltpu.VMEM((4, count, size), F32),
             pltpu.SemaphoreType.DMA((loads,)),
         ],
         rhs, guess, diag_blocks, diag_inverse, coupling, prolong, coarse_inverse, aggregate,
         space=pltpu.HBM,
     )
-    from_left = from_behind(to_right, 1)
-    from_right = from_behind(to_left, -1)
+    far_blocks = swap(far, 1)
+    near_blocks = swap(near, 0)
     twice, partial = call(
-        functools.partial(second_kernel, group_count), (tile, packed), [plain, plain],
-        rhs, guess, trial, diag, inverse, coupling, own, from_left, from_right,
+        functools.partial(second_kernel, group_count), (tile, packed), [plain],
+        rhs, guess, trial, defect, diag, inverse, coupling, own, near_blocks, far_blocks,
         prolong, aggregate,
     )
     shares = lax.all_to_all(partial, "row", 0, 0, tiled=True)
     corrected = call(coarse_kernel, packed, [], shares, coarse_inverse)
     values = lax.all_to_all(corrected, "row", 0, 0, tiled=True)
-    start, trial, to_right, to_left = call(
-        functools.partial(third_kernel, group_count), (tile, tile, tile, tile), [plain],
+    start, trial, defect, near, far = call(
+        functools.partial(third_kernel, group_count), (tile, tile, tile, line, line), [plain],
         rhs, twice, values, diag, inverse, coupling, own, prolong, aggregate,
     )
-    next_left = from_behind(to_right, 1)
-    next_right = from_behind(to_left, -1)
+    far = swap(far, 1)
+    near = swap(near, 0)
     return call(
-        fourth_kernel, (tile, tile), [plain, plain],
-        rhs, start, trial, diag, inverse, coupling, own, next_left, next_right,
-        from_left, from_right,
+        fourth_kernel, (tile, tile), [plain],
+        rhs, start, trial, defect, diag, inverse, coupling, own, near, far,
+        near_blocks, far_blocks,
     )
 
 

time: 57.6 us -> 51.7 us (0.90)
  the two profiles are of different devices: /device:TPU:29 before, /device:TPU:2 now
where the time goes in v3:
time: 51.7 us; the launch traced here: 51.5 us
  blocking collectives  19.5 us (38%)
  Pallas kernels  11.7 us (23%)
  waiting for transfers between devices  11 us (21%)
  starting transfers between devices  8.6 us (17%)
  between operations  0.71 us (1%)
    pallas_call x5, Pallas kernels, call(): pl.pallas_call(kernel, out_shape=outs, in_specs=[pl.BlockSpec(memory_spac...  11.7 us
    ppermute x4, waiting for transfers between devices, swap(): return lax.ppermute(block, BOTH, pairs + [(j, i) for i, j in pairs])  11 us
    all_to_all x1, blocking collectives, local(): shares = lax.all_to_all(partial, 'row', 0, 0, tiled=True)  10.5 us
    all_to_all x1, blocking collectives, local(): values = lax.all_to_all(corrected, 'row', 0, 0, tiled=True)  9.05 us
    ppermute x4, starting transfers between devices, swap(): return lax.ppermute(block, BOTH, pairs + [(j, i) for i, j in pairs])  8.6 us
  transfers between devices with their start and end apart: 4, of which 3 were waited for; matrix products, arithmetic and copies ran while one was open for 0% of the time, Pallas kernels for 0%

profile of v3, /device:TPU:2, one launch (start us, length us, event | category | flops | bytes accessed | tf_op | source)
XLA Modules:
  0.0 51.5 jit_solution(3757542646091089276)
XLA Ops:
  0.6 3.9 %shard_map.95 = (f32[64,128]{1,0:T(8,128)S(1)}, f32[64,128]{1,0:T(8,128)S(1)}, f32[64,64,128]{2,1,0:T(8,128)S(1)}, f32[64,64,128]{2,1,0:T(8,128)S(1)}, f32[64,64...) custom-call(f32[64,128]{1,0:T(8,128)} %rhs_in.1, ...), custom_call_target="tpu_custom_call" | custom-call | tf_op jit(solution)/shard_map/pallas_call | solution.py:406
  4.5 1.6 %collective-permute-start = (bf16[2,64,128]{2,1,0:T(8,128)(2,1)S(1)}, bf16[2,64,128]{2,1,0:T(8,128)(2,1)S(1)}, u32[]{:S(2)}, u32[]{:S(2)}) collective-permute-start(bf16[2,64,128]{2,1,0:T(8,128)(2,1)S(1)} %get-tuple-element.30), channel_id=1, source_target_pairs={{0,1},{2,3},{4,5},{6,7},{8,9},{10,11},{12,13},{14,15},{16,17},{18,... | collective-permute-start | bytes 98312 | tf_op jit(solution)/shard_map/ppermute | solution.py:20
  6.1 4.6 %collective-permute-start.1 = (bf16[2,64,128]{2,1,0:T(8,128)(2,1)S(1)}, bf16[2,64,128]{2,1,0:T(8,128)(2,1)S(1)}, u32[]{:S(2)}, u32[]{:S(2)}) collective-permute-start(bf16[2,64,128]{2,1,0:T(8,128)(2,1)S(1)} %get-tuple-element.31), channel_id=1, source_target_pairs={{1,2},{3,4},{5,6},{7,8},{9,10},{11,12},{13,14},{15,16},{17,18},{19... | collective-permute-start | bytes 98312 | tf_op jit(solution)/shard_map/ppermute | solution.py:20
  10.7 0.0 collective-permute-done.near.near_blocks
  10.7 4.2 %collective-permute-done.1.far.far_blocks = bf16[2,64,128]{2,1,0:T(8,128)(2,1)S(1)} collective-permute-done((bf16[2,64,128]{2,1,0:T(8,128)(2,1)S(1)}, bf16[2,64,128]{2,1,0:T(8,128)(2,1)S(1)}, u32[]{:S(2)}, u32[]{:S(2)}) %collective-permute-start.1) | collective-permute-done | bytes 32800 | tf_op jit(solution)/shard_map/ppermute | solution.py:20
  14.9 2.5 %shard_map.96 = (f32[64,128]{1,0:T(8,128)S(1)}, f32[64,128]{1,0:T(8,128)S(1)}) custom-call(f32[64,128]{1,0:T(8,128)S(1)} %get-tuple-element.22.rhs, f32[64,128]{1,0:T(8,128)S(1)} %get-tuple-element.23.guess, f32[64,128]{1,0:T(8,128)S(1)} %get-tuple-element.24.trial, f32[64,128]{1,0:T(8,128)S(1)} %get-tuple-element.25.defect, ...), custom_call_target="tpu_custom_call" | custom-call | tf_op jit(solution)/shard_map/pallas_call | solution.py:406
  17.4 10.5 %all_to_all.22 = f32[8,8,128]{2,1,0:T(8,128)S(1)} all-to-all(f32[8,8,128]{2,1,0:T(8,128)S(1)} %bitcast.9), channel_id=1, replica_groups=mesh['grp'=4,'row'=8] {'row'}, dimensions={0} | all-to-all | bytes 65536 | tf_op jit(solution)/shard_map/all_to_all | solution.py:461
  27.9 0.3 shard_map.97
  28.2 9.1 %all_to_all.23 = f32[8,8,128]{2,1,0:T(8,128)S(1)} all-to-all(f32[8,8,128]{2,1,0:T(8,128)S(1)} %bitcast.8), channel_id=1, replica_groups=mesh['grp'=4,'row'=8] {'row'}, dimensions={0} | all-to-all | bytes 65536 | tf_op jit(solution)/shard_map/all_to_all | solution.py:463
  37.3 2.3 %shard_map.98 = (f32[64,128]{1,0:T(8,128)S(1)}, f32[64,128]{1,0:T(8,128)S(1)}, f32[64,128]{1,0:T(8,128)S(1)}, bf16[64,128]{1,0:T(8,128)(2,1)S(1)}, bf16[64,128]{1,0:T(8,128)(2,1)S(1)}) custom-call(f32[64,128]{1,0:T(8,128)S(1)} %get-tuple-element.22.rhs, f32[64,128]{1,0:T(8,128)S(1)} %get-tuple-element.34.twice, f32[64,128]{1,0:T(8,128)S(1)} %bitcast.6, ...), custom_call_target="tpu_custom_call" | custom-call | tf_op jit(solution)/shard_map/pallas_call | solution.py:406
  39.6 0.5 %collective-permute-start.2 = (bf16[64,128]{1,0:T(8,128)(2,1)S(1)}, bf16[64,128]{1,0:T(8,128)(2,1)S(1)}, u32[]{:S(2)}, u32[]{:S(2)}) collective-permute-start(bf16[64,128]{1,0:T(8,128)(2,1)S(1)} %get-tuple-element.40), channel_id=1, source_target_pairs={{0,1},{2,3},{4,5},{6,7},{8,9},{10,11},{12,13},{14,15},{16,17},{18,... | collective-permute-start | bytes 49160 | tf_op jit(solution)/shard_map/ppermute | solution.py:20
  40.2 1.9 %collective-permute-start.3 = (bf16[64,128]{1,0:T(8,128)(2,1)S(1)}, bf16[64,128]{1,0:T(8,128)(2,1)S(1)}, u32[]{:S(2)}, u32[]{:S(2)}) collective-permute-start(bf16[64,128]{1,0:T(8,128)(2,1)S(1)} %get-tuple-element.41), channel_id=1, source_target_pairs={{1,2},{3,4},{5,6},{7,8},{9,10},{11,12},{13,14},{15,16},{17,18},{19... | collective-permute-start | bytes 49160 | tf_op jit(solution)/shard_map/ppermute | solution.py:20
  42.1 1.3 %collective-permute-done.2.near = bf16[64,128]{1,0:T(8,128)(2,1)S(1)} collective-permute-done((bf16[64,128]{1,0:T(8,128)(2,1)S(1)}, bf16[64,128]{1,0:T(8,128)(2,1)S(1)}, u32[]{:S(2)}, u32[]{:S(2)}) %collective-permute-start.2) | collective-permute-done | bytes 16416 | tf_op jit(solution)/shard_map/ppermute | solution.py:20
  43.4 5.4 %collective-permute-done.3.far = bf16[64,128]{1,0:T(8,128)(2,1)S(1)} collective-permute-done((bf16[64,128]{1,0:T(8,128)(2,1)S(1)}, bf16[64,128]{1,0:T(8,128)(2,1)S(1)}, u32[]{:S(2)}, u32[]{:S(2)}) %collective-permute-start.3) | collective-permute-done | bytes 16416 | tf_op jit(solution)/shard_map/ppermute | solution.py:20
  48.8 2.7 %shard_map.99 = (f32[64,128]{1,0:T(8,128)}, f32[64,128]{1,0:T(8,128)}) custom-call(f32[64,128]{1,0:T(8,128)S(1)} %get-tuple-element.22.rhs, f32[64,128]{1,0:T(8,128)S(1)} %get-tuple-element.37.start, f32[64,128]{1,0:T(8,128)S(1)} %get-tuple-element.38.trial, f32[64,128]{1,0:T(8,128)S(1)} %get-tuple-element.39.defect, ...), custom_call_target="tpu_custom_call" | custom-call | tf_op jit(solution)/shard_map/pallas_call | solution.py:406
Async XLA Ops:
  4.5 6.2 %collective-permute-start = (bf16[2,64,128]{2,1,0:T(8,128)(2,1)S(1)}, bf16[2,64,128]{2,1,0:T(8,128)(2,1)S(1)}, u32[]{:S(2)}, u32[]{:S(2)}) collective-permute-start(bf16[2,64,128]{2,1,0:T(8,128)(2,1)S(1)} %get-tuple-element.30), channel_id=1, source_target_pairs={{0,1},{2,3},{4,5},{6,7},{8,9},{10,11},{12,13},{14,15},{16,17},{18,... | collective-permute-start | bytes 98312 | tf_op jit(solution)/shard_map/ppermute | solution.py:20
  6.1 8.8 %collective-permute-start.1 = (bf16[2,64,128]{2,1,0:T(8,128)(2,1)S(1)}, bf16[2,64,128]{2,1,0:T(8,128)(2,1)S(1)}, u32[]{:S(2)}, u32[]{:S(2)}) collective-permute-start(bf16[2,64,128]{2,1,0:T(8,128)(2,1)S(1)} %get-tuple-element.31), channel_id=1, source_target_pairs={{1,2},{3,4},{5,6},{7,8},{9,10},{11,12},{13,14},{15,16},{17,18},{19... | collective-permute-start | bytes 98312 | tf_op jit(solution)/shard_map/ppermute | solution.py:20
  39.6 3.8 %collective-permute-start.2 = (bf16[64,128]{1,0:T(8,128)(2,1)S(1)}, bf16[64,128]{1,0:T(8,128)(2,1)S(1)}, u32[]{:S(2)}, u32[]{:S(2)}) collective-permute-start(bf16[64,128]{1,0:T(8,128)(2,1)S(1)} %get-tuple-element.40), channel_id=1, source_target_pairs={{0,1},{2,3},{4,5},{6,7},{8,9},{10,11},{12,13},{14,15},{16,17},{18,... | collective-permute-start | bytes 49160 | tf_op jit(solution)/shard_map/ppermute | solution.py:20
  40.2 8.6 %collective-permute-start.3 = (bf16[64,128]{1,0:T(8,128)(2,1)S(1)}, bf16[64,128]{1,0:T(8,128)(2,1)S(1)}, u32[]{:S(2)}, u32[]{:S(2)}) collective-permute-start(bf16[64,128]{1,0:T(8,128)(2,1)S(1)} %get-tuple-element.41), channel_id=1, source_target_pairs={{1,2},{3,4},{5,6},{7,8},{9,10},{11,12},{13,14},{15,16},{17,18},{19... | collective-permute-start | bytes 49160 | tf_op jit(solution)/shard_map/ppermute | solution.py:20

commit v4 on v3

--- a/solution.py
+++ b/solution.py
@@ -48,12 +48,37 @@
     return parts[0] + (parts[1] + parts[2])
 
 
-def times(block, columns):
-    return product(block, columns, ((1,), (0,)))
-
-
-def times_transposed(block, columns):
-    return product(block, columns, ((0,), (0,)))
+def stack(rows):
+    return jnp.concatenate([part.astype(F32) for part in three(rows)], axis=0)
+
+
+def one(block, row, transposed=False):
+    row = jnp.broadcast_to(row, (2 * ROWS, row.shape[1]))
+    place = lax.broadcasted_iota(jnp.int32, row.shape, 0)
+    high, middle, low = (part.astype(F32) for part in three(row))
+    parts = jnp.where(
+        place == 0, high, jnp.where(place == 1, middle, jnp.where(place == 2, low, 0.0))
+    )
+    dims = ((1,), (0,)) if transposed else ((1,), (1,))
+    both = lax.dot_general(
+        parts.astype(BF16), block, (dims, ((), ())), preferred_element_type=F32
+    )
+    return jnp.sum(both, axis=0, keepdims=True)
+
+
+def at_ends(count, first, second, before_last, last):
+    rest = jnp.zeros((ROWS - 4, first.shape[1]), F32)
+    parts = stack(jnp.concatenate([first, second, before_last, last, rest], axis=0))
+    spare = jnp.zeros((ROWS, first.shape[1]), F32)
+    parts = jnp.concatenate([parts, spare], axis=0).astype(BF16)
+    shape = (4 * ROWS, count)
+    row = lax.rem(lax.broadcasted_iota(jnp.int32, shape, 0), ROWS)
+    lane = lax.broadcasted_iota(jnp.int32, shape, 1)
+    target = jnp.where(row < 2, row, jnp.where(row < 4, row + (count - 4), -1))
+    chosen_lane = jnp.where(lane == target, 1.0, 0.0).astype(BF16)
+    return lax.dot_general(
+        parts, chosen_lane, (((0,), (0,)), ((), ())), preferred_element_type=F32
+    )
 
 
 def operate(diag, coupling, vector_ref, out_ref, lower):
@@ -104,18 +129,18 @@
     return lax.fori_loop(0, count, step, carry, unroll=True)
 
 
-def place(tile, block, row, spacing):
+def place(tile, block, row, ends):
     shape = (tile.shape[0] // ROWS, ROWS, tile.shape[1])
     lane = lax.broadcasted_iota(jnp.int32, (1,) + shape[1:], 2)
-    mine = lax.shift_right_logical(lane, spacing // 2) == row
-    turned = pltpu.roll(block, spacing * row + 1, 1).reshape(shape)
+    mine = lax.shift_right_logical(lane, ends) == row
+    turned = pltpu.roll(block, 2 * ends * row + ends, 1).reshape(shape)
     return jnp.where(mine, turned, tile.reshape(shape)).reshape(tile.shape)
 
 
 def split(tile, scratch):
     size = tile.shape[0]
     scratch[...] = jnp.transpose(tile)
-    return scratch[pl.ds(1, size, stride=2), :], scratch[pl.ds(0, size, stride=2), :]
+    return [scratch[pl.ds(k, size, stride=2), :] for k in (0, 1)]
 
 
 def split_more(tiles, scratch):
@@ -124,23 +149,18 @@
         scratch[t] = jnp.transpose(tiles[t])
     return [
         jnp.concatenate([scratch[t, pl.ds(k, half, stride=4), :] for t in (0, 1)], axis=0)
-        for k in (1, 2, 0)
+        for k in range(4)
     ]
 
 
-def message(columns, rightward):
+def edge_rows(columns):
     lane = lanes(columns[0])
-    middle = lane.shape[1] // 2
-    shift = middle + jnp.where(rightward, 1, 0)
     tile = jnp.zeros(lane.shape, F32)
     for k, column in enumerate(columns):
-        tile = jnp.where(lane == middle + k, pltpu.roll(column, shift + k, 1), tile)
-    high, rest, last = three(tile)
-    return high.astype(F32) + turn(rest.astype(F32), 3) + turn(last.astype(F32), 6)
-
-
-def columns_of(tile):
-    return tile + (turn(tile, -3) + turn(tile, -6))
+        last = len(columns) + k
+        tile = jnp.where(lane == k, turn(column, k), tile)
+        tile = jnp.where(lane == last, turn(column, last + 1), tile)
+    return jnp.transpose(tile)[:ROWS]
 
 
 def wrong(rhs_ref, vector_ref, diag, coupling, work):
@@ -154,8 +174,8 @@
 
 def first_kernel(
     rhs_in, guess_in, diag_in, inverse_in, coupling_in, prolong_in, coarse_in, aggregate_in,
-    rhs, guess, diag, inverse, coupling, prolong, coarse, aggregate,
-    trial, defect_out, near, far, own, diag_half, inverse_half, coupling_half, work, scratch, sems,
+    rhs, diag, inverse, coupling, prolong, coarse, aggregate,
+    trial, defect_out, near, far, own, rows_out, guess, diag_half, inverse_half, coupling_half, work, scratch, sems,
 ):
     size, count = guess.shape
     parts = diag_half.shape[0] // LOAD
@@ -196,16 +216,16 @@
             block = diag_half[i].astype(F32)
             coupling[i] = pair
             diag[i] = block
-            edge = place(edge, block, i, 2)
+            edge = place(edge, block, i, 1)
             sums.append(jnp.sum(block * start + pair * lower, axis=0, keepdims=True))
             upward = upward + pair * guess[i : i + 1, :]
         work[pl.ds(chunk * ROWS, ROWS), :] = jnp.concatenate(sums, axis=0)
-    first_diag, last_diag = split(edge, scratch.at[0])
+    last_diag, first_diag = split(edge, scratch.at[0])
     upper = jnp.where(lane == count - 1, 0.0, turn(upward, -1))
     copies[1].wait()
     defect = rhs[...] - (work[...] + upper)
 
-    edge = jnp.zeros_like(start)
+    edge = [jnp.zeros_like(start), jnp.zeros_like(start)]
     for chunk in range(size // ROWS):
         if chunk * ROWS % LOAD == 0:
             copies[2 + 2 * parts + chunk * ROWS // LOAD].wait()
@@ -214,10 +234,11 @@
         for i in range(chunk * ROWS, chunk * ROWS + ROWS):
             block = inverse_half[i].astype(F32)
             inverse[i] = block
-            edge = place(edge, block, i, 2)
+            t, row = divmod(i, size // 2)
+            edge[t] = place(edge[t], block, row, 2)
             sums.append(jnp.sum(block * defect, axis=0, keepdims=True))
         trial[rows, :] = guess[rows, :] + jnp.concatenate(sums, axis=0)
-    first_inverse, last_inverse = split(edge, scratch.at[1])
+    inverses = split_more(edge, scratch.at[1:3])
 
     second = trial[...]
     lower = jnp.where(lane == 0, 0.0, turn(second, 1))
@@ -228,49 +249,41 @@
         for i in range(chunk * ROWS, chunk * ROWS + ROWS):
             pair = coupling[i]
             t, row = divmod(i, size // 2)
-            edge[t] = place(edge[t], pair, row, 4)
+            edge[t] = place(edge[t], pair, row, 2)
             sums.append(jnp.sum(diag[i] * second + pair * lower, axis=0, keepdims=True))
             upward = upward + pair * trial[i : i + 1, :]
         work[pl.ds(chunk * ROWS, ROWS), :] = jnp.concatenate(sums, axis=0)
-    first_coupling, second_coupling, last_coupling = split_more(edge, scratch.at[2:4])
+    couplings = split_more(edge, scratch.at[3:5])
     upper = jnp.where(lane == count - 1, 0.0, turn(upward, -1))
     defect = rhs[...] - (work[...] + upper)
     defect_out[...] = defect
 
     even = even_device()
-    columns = (start, second, defect)
-    lasts = jnp.concatenate([last_diag, last_inverse], axis=1)
-    firsts = jnp.concatenate([first_diag, first_inverse], axis=1)
-    link = jnp.concatenate([first_coupling, jnp.zeros_like(first_coupling)], axis=1)
+    rows = edge_rows((start, second, defect))
+    rows_out[...] = rows
+    lasts = jnp.concatenate([last_diag, inverses[1]], axis=1)
+    firsts = jnp.concatenate([first_diag, inverses[2]], axis=1)
+    parts = jnp.concatenate([stack(rows), jnp.zeros((size - 3 * ROWS, size), F32)], axis=0)
+    link = jnp.concatenate([couplings[2], parts], axis=1).astype(BF16)
     near[0] = jnp.where(even, lasts, firsts).astype(BF16)
-    near[1] = (message(columns, even) + link).astype(BF16)
+    near[1] = link
     far[0] = jnp.where(even, firsts, lasts).astype(BF16)
-    far[1] = (message(columns, jnp.logical_not(even)) + link).astype(BF16)
-    for k, block in enumerate(
-        (
-            first_diag, first_inverse, first_coupling, second_coupling,
-            last_diag, last_inverse, last_coupling,
-        )
-    ):
+    far[1] = link
+    for k, block in enumerate([last_diag, first_diag] + inverses + couplings[1:]):
         own[k] = block.astype(BF16)
     for copy in copies[-3:]:
         copy.wait()
 
 
 def finish(
-    rhs, start_ref, trial_ref, defect_ref, diag, inverse, coupling, own, near, far,
+    rhs, trial_ref, defect_ref, diag, inverse, coupling, own, rows, near, far,
     near_blocks, far_blocks, twice_ref, work_ref,
 ):
-    start = start_ref[...]
-    size = start.shape[0]
-    lane = lanes(start)
-    end = start.shape[1] - 1
-    middle = start.shape[1] // 2
-    at_start, at_end = lane == 0, lane == end
+    size, count = trial_ref.shape
     even = even_device()
-    near, far = near[...].astype(F32), far[...].astype(F32)
-    left = columns_of(jnp.where(even, far, near))
-    right = columns_of(jnp.where(even, near, far))
+    apply_blocks(inverse, defect_ref[...], trial_ref, twice_ref)
+
+    left, right = jnp.where(even, far, near), jnp.where(even, near, far)
     near_pair, far_pair = near_blocks[0].astype(F32), far_blocks[0].astype(F32)
     left_pair = jnp.where(even, far_pair, near_pair).astype(BF16)
     right_pair = jnp.where(even, near_pair, far_pair).astype(BF16)
@@ -279,48 +292,41 @@
     left_diag, left_inverse = left_pair[:, :size], left_pair[:, size:]
     right_diag, right_inverse = right_pair[:, :size], right_pair[:, size:]
     (
-        first_diag, first_inverse, first_coupling, second_coupling,
-        last_diag, last_inverse, last_coupling,
-    ) = (own[k] for k in range(7))
-
-    def at_ends(first, last):
-        return jnp.where(at_start, first, jnp.where(at_end, last, 0.0))
-
-    down = times(first_coupling, turn(left, -middle))
-    up = times_transposed(right_coupling, turn(right, middle - 1))
-    change = -at_ends(times(first_inverse, down), times(last_inverse, up))
-    once = trial_ref[...] + change
-    left_change = times(left_inverse, times_transposed(first_coupling, -start))
-    right_change = times(right_inverse, times(right_coupling, -start))
-    left_once = turn(left, -middle - 1) + left_change
-    right_once = turn(right, middle - 2) + right_change
-    defect = (
-        defect_ref[...]
-        - at_ends(
-            times(first_diag, change) + times(first_coupling, left_once),
-            times(last_diag, change) + times_transposed(right_coupling, right_once),
-        )
-        - jnp.where(lane == 1, turn(times(second_coupling, change), 1), 0.0)
-        - jnp.where(lane == end - 1, turn(times_transposed(last_coupling, change), -1), 0.0)
-    )
-    work_ref[...] = once
-    apply_blocks(inverse, defect, work_ref, twice_ref)
-    left_defect = (
-        turn(left, -middle - 2)
-        - times(left_diag, left_change)
-        - times_transposed(first_coupling, once)
-    )
-    right_defect = (
-        turn(right, middle - 3) - times(right_diag, right_change) - times(right_coupling, once)
-    )
-    left_twice = left_once + times(left_inverse, left_defect)
-    right_twice = right_once + times(right_inverse, right_defect)
-    twice = twice_ref[...]
-    upward = operate(
-        diag, coupling, twice_ref, work_ref, jnp.where(at_start, left_twice, turn(twice, 1))
-    )
-    upper = jnp.where(at_end, times_transposed(right_coupling, right_twice), turn(upward, -1))
-    return rhs[...] - (work_ref[...] + upper)
+        last_diag, first_diag,
+        before_inverse, last_inverse, first_inverse, second_inverse,
+        last_coupling, first_coupling, second_coupling,
+    ) = (own[k] for k in range(9))
+    first_start, first_trial, last_start, last_trial = (rows[k : k + 1] for k in (0, 1, 3, 4))
+    left_start, left_trial, left_wrong = (left[k : k + 1] for k in (3, 4, 5))
+    right_start, right_trial, right_wrong = (right[k : k + 1] for k in (0, 1, 2))
+
+    first_change = -one(first_inverse, one(first_coupling, left_start))
+    last_change = -one(last_inverse, one(right_coupling, right_start, True))
+    left_change = -one(left_inverse, one(first_coupling, first_start, True))
+    right_change = -one(right_inverse, one(right_coupling, last_start))
+    left_once, right_once = left_trial + left_change, right_trial + right_change
+    first_added = one(first_diag, first_change) + one(first_coupling, left_once)
+    last_added = one(last_diag, last_change) + one(right_coupling, right_once, True)
+    left_added = one(left_diag, left_change)
+    left_added = left_added + one(first_coupling, first_trial + first_change, True)
+    right_added = one(right_diag, right_change)
+    right_added = right_added + one(right_coupling, last_trial + last_change)
+    left_twice = left_once + one(left_inverse, left_wrong - left_added)
+    right_twice = right_once + one(right_inverse, right_wrong - right_added)
+    twice_ref[...] = twice_ref[...] + at_ends(
+        count,
+        first_change - one(first_inverse, first_added),
+        -one(second_inverse, one(second_coupling, first_change)),
+        -one(before_inverse, one(last_coupling, last_change, True)),
+        last_change - one(last_inverse, last_added),
+    )
+    nothing = jnp.zeros_like(left_start)
+    beyond = at_ends(
+        count,
+        one(first_coupling, left_twice), nothing, nothing,
+        one(right_coupling, right_twice, True),
+    )
+    return wrong(rhs, twice_ref, diag, coupling, work_ref) - beyond
 
 
 def chosen(aggregate, group_count, half):
@@ -332,11 +338,16 @@
 
 
 def second_kernel(
-    group_count, rhs, guess, trial, defect, diag, inverse, coupling, own, near, far,
+    group_count, rhs, trial, defect, diag, inverse, coupling, own, rows, near, far,
     prolong, aggregate, twice, partial, work,
 ):
+    size = rhs.shape[0]
+    near_rows, far_rows = (
+        sum(side[1][k * ROWS : (k + 1) * ROWS, size:].astype(F32) for k in range(3))
+        for side in (near, far)
+    )
     residual = finish(
-        rhs, guess, trial, defect, diag, inverse, coupling, own, near.at[1], far.at[1],
+        rhs, trial, defect, diag, inverse, coupling, own, rows[...], near_rows, far_rows,
         near, far, twice, work,
     )
     work[...] = residual
@@ -365,8 +376,8 @@
 
 
 def third_kernel(
-    group_count, rhs, twice, values, diag, inverse, coupling, own, prolong, aggregate,
-    start_ref, trial, defect_out, near, far, work,
+    group_count, rhs, twice, values, diag, inverse, coupling, prolong, aggregate,
+    trial, defect_out, rows, start_ref, work,
 ):
     size = twice.shape[0]
     spread = jnp.zeros(twice.shape, F32)
@@ -382,18 +393,15 @@
     apply_blocks(inverse, wrong(rhs, start_ref, diag, coupling, work), start_ref, trial)
     defect = wrong(rhs, trial, diag, coupling, work)
     defect_out[...] = defect
-    even = even_device()
-    columns = (start_ref[...], trial[...], defect)
-    near[...] = message(columns, even).astype(BF16)
-    far[...] = message(columns, jnp.logical_not(even)).astype(BF16)
+    rows[...] = edge_rows((start_ref[...], trial[...], defect))
 
 
 def fourth_kernel(
-    rhs, start, trial, defect, diag, inverse, coupling, own, near, far, near_blocks, far_blocks,
+    rhs, trial, defect, diag, inverse, coupling, own, rows, near, far, near_blocks, far_blocks,
     twice, residual, work,
 ):
     residual[...] = finish(
-        rhs, start, trial, defect, diag, inverse, coupling, own, near, far,
+        rhs, trial, defect, diag, inverse, coupling, own, rows[...], near[...], far[...],
         near_blocks, far_blocks, twice, work,
     )
 
@@ -415,9 +423,9 @@
 
 def local(rhs, guess, diag_blocks, diag_inverse, coupling, prolong, coarse_inverse, aggregate):
     size, count = rhs.shape
-    rows = lax.axis_size("row")
-    group_count = count * rows // AGG
-    assert coarse_inverse.shape[2] == 2 * ROWS and 2 * size == count and rows % 2 == 0
+    members = lax.axis_size("row")
+    group_count = count * members // AGG
+    assert coarse_inverse.shape[2] == 2 * ROWS and 2 * size == count and members % 2 == 0
     aggregate = aggregate.reshape(1, count)
     coarse_inverse = jnp.transpose(coarse_inverse, (0, 2, 1))
 
@@ -428,24 +436,24 @@
     blocks = shape(size, size, count)
     packed = shape(group_count // 2, count)
     edge = shape(2, size, count, kind=BF16)
-    line = shape(size, count, kind=BF16)
+    line = shape(ROWS, size)
     plain = pltpu.VMEM((size, count), F32)
     half = pltpu.VMEM((size, size, count), BF16)
     loads = 2 + 3 * (size // LOAD) + 3
     (
-        rhs, guess, diag, inverse, coupling, prolong, coarse_inverse, aggregate,
-        trial, defect, near, far, own,
+        rhs, diag, inverse, coupling, prolong, coarse_inverse, aggregate,
+        trial, defect, near, far, own, rows,
     ) = call(
         first_kernel,
         (
-            tile, tile, blocks, blocks, blocks,
+            tile, blocks, blocks, blocks,
             shape(size, size, count, kind=BF16),
             shape(*coarse_inverse.shape, kind=BF16),
             shape(1, count, kind=jnp.int32),
-            tile, tile, edge, edge, shape(7, size, size, kind=BF16),
+            tile, tile, edge, edge, shape(9, size, size, kind=BF16), line,
         ),
         [
-            half, half, half, plain, pltpu.VMEM((4, count, size), F32),
+            plain, half, half, half, plain, pltpu.VMEM((5, count, size), F32),
             pltpu.SemaphoreType.DMA((loads,)),
         ],
         rhs, guess, diag_blocks, diag_inverse, coupling, prolong, coarse_inverse, aggregate,
@@ -455,21 +463,21 @@
     near_blocks = swap(near, 0)
     twice, partial = call(
         functools.partial(second_kernel, group_count), (tile, packed), [plain],
-        rhs, guess, trial, defect, diag, inverse, coupling, own, near_blocks, far_blocks,
+        rhs, trial, defect, diag, inverse, coupling, own, rows, near_blocks, far_blocks,
         prolong, aggregate,
     )
     shares = lax.all_to_all(partial, "row", 0, 0, tiled=True)
     corrected = call(coarse_kernel, packed, [], shares, coarse_inverse)
     values = lax.all_to_all(corrected, "row", 0, 0, tiled=True)
-    start, trial, defect, near, far = call(
-        functools.partial(third_kernel, group_count), (tile, tile, tile, line, line), [plain],
-        rhs, twice, values, diag, inverse, coupling, own, prolong, aggregate,
-    )
-    far = swap(far, 1)
-    near = swap(near, 0)
+    trial, defect, rows = call(
+        functools.partial(third_kernel, group_count), (tile, tile, line), [plain, plain],
+        rhs, twice, values, diag, inverse, coupling, prolong, aggregate,
+    )
+    far = swap(rows, 1)
+    near = swap(rows, 0)
     return call(
         fourth_kernel, (tile, tile), [plain],
-        rhs, start, trial, defect, diag, inverse, coupling, own, near, far,
+        rhs, trial, defect, diag, inverse, coupling, own, rows, near, far,
         near_blocks, far_blocks,
     )
 

time: 51.7 us -> 50.8 us (0.983)
  waiting for transfers between devices: 11 us -> 8.92 us
  starting transfers between devices: 8.6 us -> 9.97 us
    ppermute x4, waiting for transfers between devices: 11 us -> 8.92 us  [swap(): return lax.ppermute(block, BOTH, pairs + [(j, i) for i, j in pairs])]
    ppermute x4, starting transfers between devices: 8.6 us -> 9.97 us  [swap(): return lax.ppermute(block, BOTH, pairs + [(j, i) for i, j in pairs])]
  transfers between devices with their start and end apart: 4 -> 4, of which waited for: 3 -> 2; matrix products, arithmetic and copies ran while one was open for 0% -> 0% of each run, Pallas kernels for 0% -> 0%
where the time goes in v4:
time: 50.8 us; the launch traced here: 50.6 us
  blocking collectives  19.5 us (38%)
  Pallas kernels  11.5 us (23%)
  starting transfers between devices  9.97 us (20%)
  waiting for transfers between devices  8.92 us (18%)
  between operations  0.7 us (1%)
    pallas_call x5, Pallas kernels, call(): pl.pallas_call(kernel, out_shape=outs, in_specs=[pl.BlockSpec(memory_spac...  11.5 us
    all_to_all x1, blocking collectives, local(): shares = lax.all_to_all(partial, 'row', 0, 0, tiled=True)  10.5 us
    ppermute x4, starting transfers between devices, swap(): return lax.ppermute(block, BOTH, pairs + [(j, i) for i, j in pairs])  9.97 us
    all_to_all x1, blocking collectives, local(): values = lax.all_to_all(corrected, 'row', 0, 0, tiled=True)  9.05 us
    ppermute x4, waiting for transfers between devices, swap(): return lax.ppermute(block, BOTH, pairs + [(j, i) for i, j in pairs])  8.92 us
  transfers between devices with their start and end apart: 4, of which 2 were waited for; matrix products, arithmetic and copies ran while one was open for 0% of the time, Pallas kernels for 0%

profile of v4, /device:TPU:2, one launch (start us, length us, event | category | flops | bytes accessed | tf_op | source)
XLA Modules:
  0.0 50.6 jit_solution(2679067098536841338)
XLA Ops:
  0.6 3.8 %shard_map.95 = (f32[64,128]{1,0:T(8,128)S(1)}, f32[64,64,128]{2,1,0:T(8,128)S(1)}, f32[64,64,128]{2,1,0:T(8,128)S(1)}, f32[64,64,128]{2,1,0:T(8,128)S(1)}, bf16...) custom-call(f32[64,128]{1,0:T(8,128)} %rhs_in.1, ...), custom_call_target="tpu_custom_call" | custom-call | tf_op jit(solution)/shard_map/pallas_call | solution.py:414
  4.4 1.6 %collective-permute-start = (bf16[2,64,128]{2,1,0:T(8,128)(2,1)S(1)}, bf16[2,64,128]{2,1,0:T(8,128)(2,1)S(1)}, u32[]{:S(2)}, u32[]{:S(2)}) collective-permute-start(bf16[2,64,128]{2,1,0:T(8,128)(2,1)S(1)} %get-tuple-element.28), channel_id=1, source_target_pairs={{0,1},{2,3},{4,5},{6,7},{8,9},{10,11},{12,13},{14,15},{16,17},{18,... | collective-permute-start | bytes 98312 | tf_op jit(solution)/shard_map/ppermute | solution.py:20
  6.0 4.6 %collective-permute-start.1 = (bf16[2,64,128]{2,1,0:T(8,128)(2,1)S(1)}, bf16[2,64,128]{2,1,0:T(8,128)(2,1)S(1)}, u32[]{:S(2)}, u32[]{:S(2)}) collective-permute-start(bf16[2,64,128]{2,1,0:T(8,128)(2,1)S(1)} %get-tuple-element.29), channel_id=1, source_target_pairs={{1,2},{3,4},{5,6},{7,8},{9,10},{11,12},{13,14},{15,16},{17,18},{19... | collective-permute-start | bytes 98312 | tf_op jit(solution)/shard_map/ppermute | solution.py:20
  10.6 0.0 collective-permute-done.near.near_blocks
  10.6 4.2 %collective-permute-done.1.far.far_blocks = bf16[2,64,128]{2,1,0:T(8,128)(2,1)S(1)} collective-permute-done((bf16[2,64,128]{2,1,0:T(8,128)(2,1)S(1)}, bf16[2,64,128]{2,1,0:T(8,128)(2,1)S(1)}, u32[]{:S(2)}, u32[]{:S(2)}) %collective-permute-start.1) | collective-permute-done | bytes 32800 | tf_op jit(solution)/shard_map/ppermute | solution.py:20
  14.8 2.7 %shard_map.96 = (f32[64,128]{1,0:T(8,128)S(1)}, f32[64,128]{1,0:T(8,128)S(1)}) custom-call(f32[64,128]{1,0:T(8,128)S(1)} %get-tuple-element.20.rhs, f32[64,128]{1,0:T(8,128)S(1)} %get-tuple-element.21.trial, f32[64,128]{1,0:T(8,128)S(1)} %get-tuple-element.22.defect, f32[64,64,128]{2,1,0:T(8,128)S(1)} %get-tuple-element.23.diag, ...), custom_call_target="tpu_custom_call" | custom-call | tf_op jit(solution)/shard_map/pallas_call | solution.py:414
  17.5 10.5 %all_to_all.22 = f32[8,8,128]{2,1,0:T(8,128)S(1)} all-to-all(f32[8,8,128]{2,1,0:T(8,128)S(1)} %bitcast.9), channel_id=1, replica_groups=mesh['grp'=4,'row'=8] {'row'}, dimensions={0} | all-to-all | bytes 65536 | tf_op jit(solution)/shard_map/all_to_all | solution.py:469
  28.0 0.3 shard_map.97
  28.3 9.1 %all_to_all.23 = f32[8,8,128]{2,1,0:T(8,128)S(1)} all-to-all(f32[8,8,128]{2,1,0:T(8,128)S(1)} %bitcast.8), channel_id=1, replica_groups=mesh['grp'=4,'row'=8] {'row'}, dimensions={0} | all-to-all | bytes 65536 | tf_op jit(solution)/shard_map/all_to_all | solution.py:471
  37.3 2.3 %shard_map.98 = (f32[64,128]{1,0:T(8,128)S(1)}, f32[64,128]{1,0:T(8,128)S(1)}, f32[8,64]{1,0:T(8,128)S(1)}) custom-call(f32[64,128]{1,0:T(8,128)S(1)} %get-tuple-element.20.rhs, f32[64,128]{1,0:T(8,128)S(1)} %get-tuple-element.32.twice, f32[64,128]{1,0:T(8,128)S(1)} %bitcast.6, f32[64,64,128]{2,1,0:T(8,128)S(1)} %get-tuple-element.23.diag, ...), custom_call_target="tpu_custom_call" | custom-call | tf_op jit(solution)/shard_map/pallas_call | solution.py:414
  39.6 1.9 %collective-permute-start.3 = (f32[8,64]{1,0:T(8,128)S(1)}, f32[8,64]{1,0:T(8,128)S(1)}, u32[]{:S(2)}, u32[]{:S(2)}) collective-permute-start(f32[8,64]{1,0:T(8,128)S(1)} %get-tuple-element.37.rows), channel_id=1, source_target_pairs={{1,2},{3,4},{5,6},{7,8},{9,10},{11,12},{13,14},{15,16},{17,18},{19... | collective-permute-start | bytes 6152 | tf_op jit(solution)/shard_map/ppermute | solution.py:20
  41.5 1.9 %collective-permute-start.2 = (f32[8,64]{1,0:T(8,128)S(1)}, f32[8,64]{1,0:T(8,128)S(1)}, u32[]{:S(2)}, u32[]{:S(2)}) collective-permute-start(f32[8,64]{1,0:T(8,128)S(1)} %get-tuple-element.37.rows), channel_id=1, source_target_pairs={{0,1},{2,3},{4,5},{6,7},{8,9},{10,11},{12,13},{14,15},{16,17},{18,... | collective-permute-start | bytes 6152 | tf_op jit(solution)/shard_map/ppermute | solution.py:20
  43.4 4.7 %collective-permute-done.3.far = f32[8,64]{1,0:T(8,128)S(1)} collective-permute-done((f32[8,64]{1,0:T(8,128)S(1)}, f32[8,64]{1,0:T(8,128)S(1)}, u32[]{:S(2)}, u32[]{:S(2)}) %collective-permute-start.3) | collective-permute-done | bytes 2080 | tf_op jit(solution)/shard_map/ppermute | solution.py:20
  48.1 0.0 collective-permute-done.2.near
  48.1 2.5 %shard_map.99 = (f32[64,128]{1,0:T(8,128)}, f32[64,128]{1,0:T(8,128)}) custom-call(f32[64,128]{1,0:T(8,128)S(1)} %get-tuple-element.20.rhs, f32[64,128]{1,0:T(8,128)S(1)} %get-tuple-element.35.trial, f32[64,128]{1,0:T(8,128)S(1)} %get-tuple-element.36.defect, f32[64,64,128]{2,1,0:T(8,128)S(1)} %get-tuple-element.23.diag, ...), custom_call_target="tpu_custom_call" | custom-call | tf_op jit(solution)/shard_map/pallas_call | solution.py:414
Async XLA Ops:
  4.4 6.2 %collective-permute-start = (bf16[2,64,128]{2,1,0:T(8,128)(2,1)S(1)}, bf16[2,64,128]{2,1,0:T(8,128)(2,1)S(1)}, u32[]{:S(2)}, u32[]{:S(2)}) collective-permute-start(bf16[2,64,128]{2,1,0:T(8,128)(2,1)S(1)} %get-tuple-element.28), channel_id=1, source_target_pairs={{0,1},{2,3},{4,5},{6,7},{8,9},{10,11},{12,13},{14,15},{16,17},{18,... | collective-permute-start | bytes 98312 | tf_op jit(solution)/shard_map/ppermute | solution.py:20
  6.0 8.8 %collective-permute-start.1 = (bf16[2,64,128]{2,1,0:T(8,128)(2,1)S(1)}, bf16[2,64,128]{2,1,0:T(8,128)(2,1)S(1)}, u32[]{:S(2)}, u32[]{:S(2)}) collective-permute-start(bf16[2,64,128]{2,1,0:T(8,128)(2,1)S(1)} %get-tuple-element.29), channel_id=1, source_target_pairs={{1,2},{3,4},{5,6},{7,8},{9,10},{11,12},{13,14},{15,16},{17,18},{19... | collective-permute-start | bytes 98312 | tf_op jit(solution)/shard_map/ppermute | solution.py:20
  39.6 8.5 %collective-permute-start.3 = (f32[8,64]{1,0:T(8,128)S(1)}, f32[8,64]{1,0:T(8,128)S(1)}, u32[]{:S(2)}, u32[]{:S(2)}) collective-permute-start(f32[8,64]{1,0:T(8,128)S(1)} %get-tuple-element.37.rows), channel_id=1, source_target_pairs={{1,2},{3,4},{5,6},{7,8},{9,10},{11,12},{13,14},{15,16},{17,18},{19... | collective-permute-start | bytes 6152 | tf_op jit(solution)/shard_map/ppermute | solution.py:20
  41.5 6.6 %collective-permute-start.2 = (f32[8,64]{1,0:T(8,128)S(1)}, f32[8,64]{1,0:T(8,128)S(1)}, u32[]{:S(2)}, u32[]{:S(2)}) collective-permute-start(f32[8,64]{1,0:T(8,128)S(1)} %get-tuple-element.37.rows), channel_id=1, source_target_pairs={{0,1},{2,3},{4,5},{6,7},{8,9},{10,11},{12,13},{14,15},{16,17},{18,... | collective-permute-start | bytes 6152 | tf_op jit(solution)/shard_map/ppermute | solution.py:20

commit v5 on v4

--- a/solution.py
+++ b/solution.py
@@ -52,33 +52,12 @@
     return jnp.concatenate([part.astype(F32) for part in three(rows)], axis=0)
 
 
-def one(block, row, transposed=False):
-    row = jnp.broadcast_to(row, (2 * ROWS, row.shape[1]))
-    place = lax.broadcasted_iota(jnp.int32, row.shape, 0)
-    high, middle, low = (part.astype(F32) for part in three(row))
-    parts = jnp.where(
-        place == 0, high, jnp.where(place == 1, middle, jnp.where(place == 2, low, 0.0))
-    )
-    dims = ((1,), (0,)) if transposed else ((1,), (1,))
-    both = lax.dot_general(
-        parts.astype(BF16), block, (dims, ((), ())), preferred_element_type=F32
-    )
-    return jnp.sum(both, axis=0, keepdims=True)
-
-
-def at_ends(count, first, second, before_last, last):
-    rest = jnp.zeros((ROWS - 4, first.shape[1]), F32)
-    parts = stack(jnp.concatenate([first, second, before_last, last, rest], axis=0))
-    spare = jnp.zeros((ROWS, first.shape[1]), F32)
-    parts = jnp.concatenate([parts, spare], axis=0).astype(BF16)
-    shape = (4 * ROWS, count)
-    row = lax.rem(lax.broadcasted_iota(jnp.int32, shape, 0), ROWS)
-    lane = lax.broadcasted_iota(jnp.int32, shape, 1)
-    target = jnp.where(row < 2, row, jnp.where(row < 4, row + (count - 4), -1))
-    chosen_lane = jnp.where(lane == target, 1.0, 0.0).astype(BF16)
-    return lax.dot_general(
-        parts, chosen_lane, (((0,), (0,)), ((), ())), preferred_element_type=F32
-    )
+def to_column(block, row):
+    return jnp.sum(block * row, axis=1, keepdims=True)
+
+
+def to_row(block, column):
+    return jnp.sum(block * column, axis=0, keepdims=True)
 
 
 def operate(diag, coupling, vector_ref, out_ref, lower):
@@ -129,18 +108,18 @@
     return lax.fori_loop(0, count, step, carry, unroll=True)
 
 
-def place(tile, block, row, ends):
+def at_lane(tile, turned, lane):
+    shape = (tile.shape[0] // ROWS, ROWS, tile.shape[1])
+    mine = lax.broadcasted_iota(jnp.int32, (1,) + shape[1:], 2) == lane
+    return jnp.where(mine, turned.reshape(shape), tile.reshape(shape)).reshape(tile.shape)
+
+
+def place(tile, block, row):
     shape = (tile.shape[0] // ROWS, ROWS, tile.shape[1])
     lane = lax.broadcasted_iota(jnp.int32, (1,) + shape[1:], 2)
-    mine = lax.shift_right_logical(lane, ends) == row
-    turned = pltpu.roll(block, 2 * ends * row + ends, 1).reshape(shape)
+    mine = lax.shift_right_logical(lane, 2) == row
+    turned = pltpu.roll(block, 4 * row + 2, 1).reshape(shape)
     return jnp.where(mine, turned, tile.reshape(shape)).reshape(tile.shape)
-
-
-def split(tile, scratch):
-    size = tile.shape[0]
-    scratch[...] = jnp.transpose(tile)
-    return [scratch[pl.ds(k, size, stride=2), :] for k in (0, 1)]
 
 
 def split_more(tiles, scratch):
@@ -175,7 +154,8 @@
 def first_kernel(
     rhs_in, guess_in, diag_in, inverse_in, coupling_in, prolong_in, coarse_in, aggregate_in,
     rhs, diag, inverse, coupling, prolong, coarse, aggregate,
-    trial, defect_out, near, far, own, rows_out, guess, diag_half, inverse_half, coupling_half, work, scratch, sems,
+    trial, defect_out, near, far, own, rows_out,
+    guess, diag_half, inverse_half, coupling_half, work, scratch, sems,
 ):
     size, count = guess.shape
     parts = diag_half.shape[0] // LOAD
@@ -204,7 +184,8 @@
     lane = lanes(start)
     lower = jnp.where(lane == 0, 0.0, turn(start, 1))
     upward = jnp.zeros_like(start)
-    edge = jnp.zeros_like(start)
+    first_diag = jnp.zeros_like(start)
+    last_diag = jnp.zeros_like(start)
     for chunk in range(size // ROWS):
         if chunk * ROWS % LOAD == 0:
             at = 2 + 2 * (chunk * ROWS // LOAD)
@@ -216,11 +197,13 @@
             block = diag_half[i].astype(F32)
             coupling[i] = pair
             diag[i] = block
-            edge = place(edge, block, i, 1)
+            turned = turn(block, i)
+            first_diag = at_lane(first_diag, turned, i)
+            last_diag = at_lane(last_diag, turned, (i - 1) % count)
             sums.append(jnp.sum(block * start + pair * lower, axis=0, keepdims=True))
             upward = upward + pair * guess[i : i + 1, :]
         work[pl.ds(chunk * ROWS, ROWS), :] = jnp.concatenate(sums, axis=0)
-    last_diag, first_diag = split(edge, scratch.at[0])
+    last_diag = turn(last_diag, 1)
     upper = jnp.where(lane == count - 1, 0.0, turn(upward, -1))
     copies[1].wait()
     defect = rhs[...] - (work[...] + upper)
@@ -235,10 +218,10 @@
             block = inverse_half[i].astype(F32)
             inverse[i] = block
             t, row = divmod(i, size // 2)
-            edge[t] = place(edge[t], block, row, 2)
+            edge[t] = place(edge[t], block, row)
             sums.append(jnp.sum(block * defect, axis=0, keepdims=True))
         trial[rows, :] = guess[rows, :] + jnp.concatenate(sums, axis=0)
-    inverses = split_more(edge, scratch.at[1:3])
+    inverses = split_more(edge, scratch.at[0:2])
 
     second = trial[...]
     lower = jnp.where(lane == 0, 0.0, turn(second, 1))
@@ -249,11 +232,11 @@
         for i in range(chunk * ROWS, chunk * ROWS + ROWS):
             pair = coupling[i]
             t, row = divmod(i, size // 2)
-            edge[t] = place(edge[t], pair, row, 2)
+            edge[t] = place(edge[t], pair, row)
             sums.append(jnp.sum(diag[i] * second + pair * lower, axis=0, keepdims=True))
             upward = upward + pair * trial[i : i + 1, :]
         work[pl.ds(chunk * ROWS, ROWS), :] = jnp.concatenate(sums, axis=0)
-    couplings = split_more(edge, scratch.at[3:5])
+    couplings = split_more(edge, scratch.at[2:4])
     upper = jnp.where(lane == count - 1, 0.0, turn(upward, -1))
     defect = rhs[...] - (work[...] + upper)
     defect_out[...] = defect
@@ -261,16 +244,27 @@
     even = even_device()
     rows = edge_rows((start, second, defect))
     rows_out[...] = rows
+    scratch[4] = jnp.transpose(jnp.concatenate(couplings[2:], axis=1))
+    first_turned, second_turned = scratch[4, :size], scratch[4, size:]
+    last_diag, first_diag = last_diag[:, :size], first_diag[:, :size]
     lasts = jnp.concatenate([last_diag, inverses[1]], axis=1)
     firsts = jnp.concatenate([first_diag, inverses[2]], axis=1)
-    parts = jnp.concatenate([stack(rows), jnp.zeros((size - 3 * ROWS, size), F32)], axis=0)
-    link = jnp.concatenate([couplings[2], parts], axis=1).astype(BF16)
-    near[0] = jnp.where(even, lasts, firsts).astype(BF16)
-    near[1] = link
-    far[0] = jnp.where(even, firsts, lasts).astype(BF16)
-    far[1] = link
-    for k, block in enumerate([last_diag, first_diag] + inverses + couplings[1:]):
-        own[k] = block.astype(BF16)
+    link = jnp.concatenate([couplings[2], first_turned], axis=1).astype(BF16)
+    near[:size] = jnp.where(even, lasts, firsts).astype(BF16)
+    far[:size] = jnp.where(even, firsts, lasts).astype(BF16)
+    parts = jnp.concatenate([stack(rows), jnp.zeros((ROWS, size), F32)], axis=0)
+    parts = jnp.concatenate([parts, parts], axis=1).astype(BF16)
+    for side in (near, far):
+        side[size : 2 * size] = link
+        side[2 * size :] = parts
+    own[0] = last_diag
+    own[1] = first_diag
+    for k in range(4):
+        own[2 + k] = inverses[k]
+    own[6] = couplings[1]
+    own[7] = couplings[2]
+    own[8] = first_turned
+    own[9] = second_turned
     for copy in copies[-3:]:
         copy.wait()
 
@@ -284,47 +278,63 @@
     apply_blocks(inverse, defect_ref[...], trial_ref, twice_ref)
 
     left, right = jnp.where(even, far, near), jnp.where(even, near, far)
-    near_pair, far_pair = near_blocks[0].astype(F32), far_blocks[0].astype(F32)
-    left_pair = jnp.where(even, far_pair, near_pair).astype(BF16)
-    right_pair = jnp.where(even, near_pair, far_pair).astype(BF16)
-    near_link, far_link = near_blocks[1].astype(F32), far_blocks[1].astype(F32)
-    right_coupling = jnp.where(even, near_link, far_link)[:, :size].astype(BF16)
-    left_diag, left_inverse = left_pair[:, :size], left_pair[:, size:]
-    right_diag, right_inverse = right_pair[:, :size], right_pair[:, size:]
-    (
-        last_diag, first_diag,
-        before_inverse, last_inverse, first_inverse, second_inverse,
-        last_coupling, first_coupling, second_coupling,
-    ) = (own[k] for k in range(9))
-    first_start, first_trial, last_start, last_trial = (rows[k : k + 1] for k in (0, 1, 3, 4))
-    left_start, left_trial, left_wrong = (left[k : k + 1] for k in (3, 4, 5))
-    right_start, right_trial, right_wrong = (right[k : k + 1] for k in (0, 1, 2))
-
-    first_change = -one(first_inverse, one(first_coupling, left_start))
-    last_change = -one(last_inverse, one(right_coupling, right_start, True))
-    left_change = -one(left_inverse, one(first_coupling, first_start, True))
-    right_change = -one(right_inverse, one(right_coupling, last_start))
+    near_all, far_all = near_blocks[: 2 * size].astype(F32), far_blocks[: 2 * size].astype(F32)
+    left_all, right_all = jnp.where(even, far_all, near_all), jnp.where(even, near_all, far_all)
+    left_diag, left_inverse = left_all[:size, :size], left_all[:size, size:]
+    right_diag, right_inverse = right_all[:size, :size], right_all[:size, size:]
+    right_coupling, right_turned = right_all[size:, :size], right_all[size:, size:]
+    last_diag, first_diag = own[0], own[1]
+    before_inverse, last_inverse, first_inverse, second_inverse = (own[2 + k] for k in range(4))
+    last_coupling, first_coupling, first_turned, second_turned = (own[6 + k] for k in range(4))
+    shape = (size, size)
+    unit = lax.broadcasted_iota(jnp.int32, shape, 0) == lax.broadcasted_iota(jnp.int32, shape, 1)
+
+    def column(row):
+        return jnp.sum(jnp.where(unit, row, 0.0), axis=1, keepdims=True)
+
+    first_start, first_trial, last_start, last_trial = (
+        column(rows[k : k + 1]) for k in (0, 1, 3, 4)
+    )
+    left_start, left_trial, right_start, right_trial = (
+        column(side[k : k + 1]) for side, k in ((left, 3), (left, 4), (right, 0), (right, 1))
+    )
+    left_wrong, right_wrong = left[5:6], right[2:3]
+
+    first_change = -to_column(first_inverse, to_row(first_turned, left_start))
+    last_change = -to_column(last_inverse, to_row(right_coupling, right_start))
+    left_change = -to_column(left_inverse, to_row(first_coupling, first_start))
+    right_change = -to_column(right_inverse, to_row(right_turned, last_start))
     left_once, right_once = left_trial + left_change, right_trial + right_change
-    first_added = one(first_diag, first_change) + one(first_coupling, left_once)
-    last_added = one(last_diag, last_change) + one(right_coupling, right_once, True)
-    left_added = one(left_diag, left_change)
-    left_added = left_added + one(first_coupling, first_trial + first_change, True)
-    right_added = one(right_diag, right_change)
-    right_added = right_added + one(right_coupling, last_trial + last_change)
-    left_twice = left_once + one(left_inverse, left_wrong - left_added)
-    right_twice = right_once + one(right_inverse, right_wrong - right_added)
-    twice_ref[...] = twice_ref[...] + at_ends(
-        count,
-        first_change - one(first_inverse, first_added),
-        -one(second_inverse, one(second_coupling, first_change)),
-        -one(before_inverse, one(last_coupling, last_change, True)),
-        last_change - one(last_inverse, last_added),
-    )
-    nothing = jnp.zeros_like(left_start)
-    beyond = at_ends(
-        count,
-        one(first_coupling, left_twice), nothing, nothing,
-        one(right_coupling, right_twice, True),
+    first_added = to_row(first_diag, first_change) + to_row(first_turned, left_once)
+    last_added = to_row(last_diag, last_change) + to_row(right_coupling, right_once)
+    left_added = to_row(left_diag, left_change)
+    left_added = left_added + to_row(first_coupling, first_trial + first_change)
+    right_added = to_row(right_diag, right_change)
+    right_added = right_added + to_row(right_turned, last_trial + last_change)
+    left_twice = left_once + to_column(left_inverse, left_wrong - left_added)
+    right_twice = right_once + to_column(right_inverse, right_wrong - right_added)
+    second_added = to_row(second_turned, first_change)
+    before_added = to_row(last_coupling, last_change)
+    lane = lax.broadcasted_iota(jnp.int32, (size, count), 1)
+    twice_ref[...] = twice_ref[...] + jnp.where(
+        lane == 0,
+        first_change - to_column(first_inverse, first_added),
+        jnp.where(
+            lane == 1,
+            -to_column(second_inverse, second_added),
+            jnp.where(
+                lane == count - 2,
+                -to_column(before_inverse, before_added),
+                jnp.where(
+                    lane == count - 1, last_change - to_column(last_inverse, last_added), 0.0
+                ),
+            ),
+        ),
+    )
+    beyond = jnp.where(
+        lane == 0,
+        column(to_row(first_turned, left_twice)),
+        jnp.where(lane == count - 1, column(to_row(right_coupling, right_twice)), 0.0),
     )
     return wrong(rhs, twice_ref, diag, coupling, work_ref) - beyond
 
@@ -343,7 +353,9 @@
 ):
     size = rhs.shape[0]
     near_rows, far_rows = (
-        sum(side[1][k * ROWS : (k + 1) * ROWS, size:].astype(F32) for k in range(3))
+        sum(
+            side[2 * size :, :size].astype(F32)[k * ROWS : (k + 1) * ROWS] for k in range(3)
+        )
         for side in (near, far)
     )
     residual = finish(
@@ -435,7 +447,7 @@
     tile = shape(size, count)
     blocks = shape(size, size, count)
     packed = shape(group_count // 2, count)
-    edge = shape(2, size, count, kind=BF16)
+    edge = shape(2 * size + 4 * ROWS, count, kind=BF16)
     line = shape(ROWS, size)
     plain = pltpu.VMEM((size, count), F32)
     half = pltpu.VMEM((size, size, count), BF16)
@@ -450,7 +462,7 @@
             shape(size, size, count, kind=BF16),
             shape(*coarse_inverse.shape, kind=BF16),
             shape(1, count, kind=jnp.int32),
-            tile, tile, edge, edge, shape(9, size, size, kind=BF16), line,
+            tile, tile, edge, edge, shape(10, size, size), line,
         ),
         [
             plain, half, half, half, plain, pltpu.VMEM((5, count, size), F32),

time: 50.8 us -> 49.7 us (0.978)
  Pallas kernels: 11.5 us -> 10.2 us
    pallas_call x5, Pallas kernels: 11.5 us -> 10.2 us  [call(): pl.pallas_call(kernel, out_shape=outs, in_specs=[pl.BlockSpec(memory_spac...]
where the time goes in v5:
time: 49.7 us; the launch traced here: 49.5 us
  blocking collectives  19.6 us (39%)
  Pallas kernels  10.2 us (21%)
  starting transfers between devices  9.97 us (20%)
  waiting for transfers between devices  9.01 us (18%)
  between operations  0.68 us (1%)
    all_to_all x1, blocking collectives, local(): shares = lax.all_to_all(partial, 'row', 0, 0, tiled=True)  10.5 us
    pallas_call x5, Pallas kernels, call(): pl.pallas_call(kernel, out_shape=outs, in_specs=[pl.BlockSpec(memory_spac...  10.2 us
    ppermute x4, starting transfers between devices, swap(): return lax.ppermute(block, BOTH, pairs + [(j, i) for i, j in pairs])  9.97 us
    all_to_all x1, blocking collectives, local(): values = lax.all_to_all(corrected, 'row', 0, 0, tiled=True)  9.05 us
    ppermute x4, waiting for transfers between devices, swap(): return lax.ppermute(block, BOTH, pairs + [(j, i) for i, j in pairs])  9.01 us
  transfers between devices with their start and end apart: 4, of which 2 were waited for; matrix products, arithmetic and copies ran while one was open for 0% of the time, Pallas kernels for 0%

profile of v5, /device:TPU:2, one launch (start us, length us, event | category | flops | bytes accessed | tf_op | source)
XLA Modules:
  0.0 49.5 jit_solution(16388190267731015984)
XLA Ops:
  0.6 3.8 %shard_map.95 = (f32[64,128]{1,0:T(8,128)S(1)}, f32[64,64,128]{2,1,0:T(8,128)S(1)}, f32[64,64,128]{2,1,0:T(8,128)S(1)}, f32[64,64,128]{2,1,0:T(8,128)S(1)}, bf16...) custom-call(f32[64,128]{1,0:T(8,128)} %rhs_in.1, ...), custom_call_target="tpu_custom_call" | custom-call | tf_op jit(solution)/shard_map/pallas_call | solution.py:426
  4.5 1.6 %collective-permute-start = (bf16[160,128]{1,0:T(8,128)(2,1)S(1)}, bf16[160,128]{1,0:T(8,128)(2,1)S(1)}, u32[]{:S(2)}, u32[]{:S(2)}) collective-permute-start(bf16[160,128]{1,0:T(8,128)(2,1)S(1)} %get-tuple-element.28), channel_id=1, source_target_pairs={{0,1},{2,3},{4,5},{6,7},{8,9},{10,11},{12,13},{14,15},{16,17},{18,... | collective-permute-start | bytes 122888 | tf_op jit(solution)/shard_map/ppermute | solution.py:20
  6.1 4.6 %collective-permute-start.1 = (bf16[160,128]{1,0:T(8,128)(2,1)S(1)}, bf16[160,128]{1,0:T(8,128)(2,1)S(1)}, u32[]{:S(2)}, u32[]{:S(2)}) collective-permute-start(bf16[160,128]{1,0:T(8,128)(2,1)S(1)} %get-tuple-element.29), channel_id=1, source_target_pairs={{1,2},{3,4},{5,6},{7,8},{9,10},{11,12},{13,14},{15,16},{17,18},{19... | collective-permute-start | bytes 122888 | tf_op jit(solution)/shard_map/ppermute | solution.py:20
  10.6 0.0 collective-permute-done.near.near_blocks
  10.7 4.3 %collective-permute-done.1.far.far_blocks = bf16[160,128]{1,0:T(8,128)(2,1)S(1)} collective-permute-done((bf16[160,128]{1,0:T(8,128)(2,1)S(1)}, bf16[160,128]{1,0:T(8,128)(2,1)S(1)}, u32[]{:S(2)}, u32[]{:S(2)}) %collective-permute-start.1) | collective-permute-done | bytes 40992 | tf_op jit(solution)/shard_map/ppermute | solution.py:20
  15.0 1.8 %shard_map.96 = (f32[64,128]{1,0:T(8,128)S(1)}, f32[64,128]{1,0:T(8,128)S(1)}) custom-call(f32[64,128]{1,0:T(8,128)S(1)} %get-tuple-element.20.rhs, f32[64,128]{1,0:T(8,128)S(1)} %get-tuple-element.21.trial, f32[64,128]{1,0:T(8,128)S(1)} %get-tuple-element.22.defect, f32[64,64,128]{2,1,0:T(8,128)S(1)} %get-tuple-element.23.diag, ...), custom_call_target="tpu_custom_call" | custom-call | tf_op jit(solution)/shard_map/pallas_call | solution.py:426
  16.8 10.5 %all_to_all.22 = f32[8,8,128]{2,1,0:T(8,128)S(1)} all-to-all(f32[8,8,128]{2,1,0:T(8,128)S(1)} %bitcast.9), channel_id=1, replica_groups=mesh['grp'=4,'row'=8] {'row'}, dimensions={0} | all-to-all | bytes 65536 | tf_op jit(solution)/shard_map/all_to_all | solution.py:481
  27.4 0.3 shard_map.97
  27.7 9.1 %all_to_all.23 = f32[8,8,128]{2,1,0:T(8,128)S(1)} all-to-all(f32[8,8,128]{2,1,0:T(8,128)S(1)} %bitcast.8), channel_id=1, replica_groups=mesh['grp'=4,'row'=8] {'row'}, dimensions={0} | all-to-all | bytes 65536 | tf_op jit(solution)/shard_map/all_to_all | solution.py:483
  36.7 2.3 %shard_map.98 = (f32[64,128]{1,0:T(8,128)S(1)}, f32[64,128]{1,0:T(8,128)S(1)}, f32[8,64]{1,0:T(8,128)S(1)}) custom-call(f32[64,128]{1,0:T(8,128)S(1)} %get-tuple-element.20.rhs, f32[64,128]{1,0:T(8,128)S(1)} %get-tuple-element.32.twice, f32[64,128]{1,0:T(8,128)S(1)} %bitcast.6, f32[64,64,128]{2,1,0:T(8,128)S(1)} %get-tuple-element.23.diag, ...), custom_call_target="tpu_custom_call" | custom-call | tf_op jit(solution)/shard_map/pallas_call | solution.py:426
  39.0 1.9 %collective-permute-start.3 = (f32[8,64]{1,0:T(8,128)S(1)}, f32[8,64]{1,0:T(8,128)S(1)}, u32[]{:S(2)}, u32[]{:S(2)}) collective-permute-start(f32[8,64]{1,0:T(8,128)S(1)} %get-tuple-element.37.rows), channel_id=1, source_target_pairs={{1,2},{3,4},{5,6},{7,8},{9,10},{11,12},{13,14},{15,16},{17,18},{19... | collective-permute-start | bytes 6152 | tf_op jit(solution)/shard_map/ppermute | solution.py:20
  40.9 1.9 %collective-permute-start.2 = (f32[8,64]{1,0:T(8,128)S(1)}, f32[8,64]{1,0:T(8,128)S(1)}, u32[]{:S(2)}, u32[]{:S(2)}) collective-permute-start(f32[8,64]{1,0:T(8,128)S(1)} %get-tuple-element.37.rows), channel_id=1, source_target_pairs={{0,1},{2,3},{4,5},{6,7},{8,9},{10,11},{12,13},{14,15},{16,17},{18,... | collective-permute-start | bytes 6152 | tf_op jit(solution)/shard_map/ppermute | solution.py:20
  42.8 4.7 %collective-permute-done.3.far = f32[8,64]{1,0:T(8,128)S(1)} collective-permute-done((f32[8,64]{1,0:T(8,128)S(1)}, f32[8,64]{1,0:T(8,128)S(1)}, u32[]{:S(2)}, u32[]{:S(2)}) %collective-permute-start.3) | collective-permute-done | bytes 2080 | tf_op jit(solution)/shard_map/ppermute | solution.py:20
  47.5 0.0 collective-permute-done.2.near
  47.5 1.9 %shard_map.99 = (f32[64,128]{1,0:T(8,128)}, f32[64,128]{1,0:T(8,128)}) custom-call(f32[64,128]{1,0:T(8,128)S(1)} %get-tuple-element.20.rhs, f32[64,128]{1,0:T(8,128)S(1)} %get-tuple-element.35.trial, f32[64,128]{1,0:T(8,128)S(1)} %get-tuple-element.36.defect, f32[64,64,128]{2,1,0:T(8,128)S(1)} %get-tuple-element.23.diag, ...), custom_call_target="tpu_custom_call" | custom-call | tf_op jit(solution)/shard_map/pallas_call | solution.py:426
Async XLA Ops:
  4.5 6.2 %collective-permute-start = (bf16[160,128]{1,0:T(8,128)(2,1)S(1)}, bf16[160,128]{1,0:T(8,128)(2,1)S(1)}, u32[]{:S(2)}, u32[]{:S(2)}) collective-permute-start(bf16[160,128]{1,0:T(8,128)(2,1)S(1)} %get-tuple-element.28), channel_id=1, source_target_pairs={{0,1},{2,3},{4,5},{6,7},{8,9},{10,11},{12,13},{14,15},{16,17},{18,... | collective-permute-start | bytes 122888 | tf_op jit(solution)/shard_map/ppermute | solution.py:20
  6.1 8.9 %collective-permute-start.1 = (bf16[160,128]{1,0:T(8,128)(2,1)S(1)}, bf16[160,128]{1,0:T(8,128)(2,1)S(1)}, u32[]{:S(2)}, u32[]{:S(2)}) collective-permute-start(bf16[160,128]{1,0:T(8,128)(2,1)S(1)} %get-tuple-element.29), channel_id=1, source_target_pairs={{1,2},{3,4},{5,6},{7,8},{9,10},{11,12},{13,14},{15,16},{17,18},{19... | collective-permute-start | bytes 122888 | tf_op jit(solution)/shard_map/ppermute | solution.py:20
  39.0 8.5 %collective-permute-start.3 = (f32[8,64]{1,0:T(8,128)S(1)}, f32[8,64]{1,0:T(8,128)S(1)}, u32[]{:S(2)}, u32[]{:S(2)}) collective-permute-start(f32[8,64]{1,0:T(8,128)S(1)} %get-tuple-element.37.rows), channel_id=1, source_target_pairs={{1,2},{3,4},{5,6},{7,8},{9,10},{11,12},{13,14},{15,16},{17,18},{19... | collective-permute-start | bytes 6152 | tf_op jit(solution)/shard_map/ppermute | solution.py:20
  40.9 6.6 %collective-permute-start.2 = (f32[8,64]{1,0:T(8,128)S(1)}, f32[8,64]{1,0:T(8,128)S(1)}, u32[]{:S(2)}, u32[]{:S(2)}) collective-permute-start(f32[8,64]{1,0:T(8,128)S(1)} %get-tuple-element.37.rows), channel_id=1, source_target_pairs={{0,1},{2,3},{4,5},{6,7},{8,9},{10,11},{12,13},{14,15},{16,17},{18,... | collective-permute-start | bytes 6152 | tf_op jit(solution)/shard_map/ppermute | solution.py:20

commit v6 on v5

v6 whole, which is shorter than its diff:
```python
import functools

import jax
import jax.numpy as jnp
from jax import lax
from jax.experimental import pallas as pl
from jax.experimental.pallas import tpu as pltpu
from jax.sharding import PartitionSpec as P

AGG = 8
BOTH = ("grp", "row")
F32 = jnp.float32
BF16 = jnp.bfloat16
ROWS = 8
LOAD = 16
EDGES = 24
EDGE_ROWS = 10


def swap(block, first):
    pairs = [(i, i + 1) for i in range(first, lax.axis_size(BOTH) - 1, 2)]
    return lax.ppermute(block, BOTH, pairs + [(j, i) for i, j in pairs])


def even_device():
    return lax.rem(lax.axis_index("row"), 2) == 0


def lanes(like):
    return lax.broadcasted_iota(jnp.int32, like.shape, 1)


def turn(tile, shift):
    return pltpu.roll(tile, shift % tile.shape[1], 1)


def three(tile):
    high = tile.astype(BF16)
    rest = tile - high.astype(F32)
    middle = rest.astype(BF16)
    return high, middle, (rest - middle.astype(F32)).astype(BF16)


def product(left, right, dims):
    left = left.astype(BF16)
    parts = [
        lax.dot_general(left, part, (dims, ((), ())), preferred_element_type=F32)
        for part in three(right)
    ]
    return parts[0] + (parts[1] + parts[2])


def stack(rows):
    return jnp.concatenate([part.astype(F32) for part in three(rows)], axis=0)


def to_column(block, row):
    return jnp.sum(block * row, axis=1, keepdims=True)


def to_row(block, column):
    return jnp.sum(block * column, axis=0, keepdims=True)


def operate(diag, coupling, vector_ref, out_ref, lower):
    vector = vector_ref[...]

    def step(chunk, upward):
        start = pl.multiple_of(chunk * ROWS, ROWS)
        own = vector_ref[pl.ds(start, ROWS), :]
        sums = []
        for s in range(ROWS):
            pair = coupling[start + s]
            terms = diag[start + s] * vector + pair * lower
            sums.append(jnp.sum(terms, axis=0, keepdims=True))
            upward = upward + pair * own[s : s + 1, :]
        out_ref[pl.ds(start, ROWS), :] = jnp.concatenate(sums, axis=0)
        return upward

    return loop(vector.shape[0] // ROWS, step, jnp.zeros_like(vector))


def apply_blocks(blocks, vector, base_ref, out_ref):
    def step(chunk, carry):
        start = pl.multiple_of(chunk * ROWS, ROWS)
        sums = [
            jnp.sum(blocks[start + s].astype(F32) * vector, axis=0, keepdims=True)
            for s in range(ROWS)
        ]
        base = base_ref[pl.ds(start, ROWS), :]
        out_ref[pl.ds(start, ROWS), :] = base + jnp.concatenate(sums, axis=0)
        return carry

    loop(vector.shape[0] // ROWS, step, 0)


def apply_transposed(blocks, vector_ref):
    def step(chunk, total):
        start = pl.multiple_of(chunk * ROWS, ROWS)
        own = vector_ref[pl.ds(start, ROWS), :]
        for s in range(ROWS):
            total = total + blocks[start + s].astype(F32) * own[s : s + 1, :]
        return total

    zero = jnp.zeros(vector_ref.shape, F32)
    return loop(vector_ref.shape[0] // ROWS, step, zero)


def loop(count, step, carry):
    return lax.fori_loop(0, count, step, carry, unroll=True)


def place(tile, block, row):
    shape = (tile.shape[0] // ROWS, ROWS, tile.shape[1])
    lane = lax.broadcasted_iota(jnp.int32, (1,) + shape[1:], 2)
    mine = lax.shift_right_logical(lane, 3) == row
    turned = pltpu.roll(block, 8 * row + 3, 1).reshape(shape)
    return jnp.where(mine, turned, tile.reshape(shape)).reshape(tile.shape)


def picker(size, width, ends):
    shape = (size * len(ends), width)
    row = lax.broadcasted_iota(jnp.int32, shape, 0)
    lane = lax.broadcasted_iota(jnp.int32, shape, 1)
    target = 8 * lax.rem(row, size) + row // size + ends[0]
    return jnp.where(lane == target, 1.0, 0.0).astype(BF16)


def end_blocks(tiles, ends):
    packed = jnp.concatenate(tiles, axis=1).astype(BF16)
    size = packed.shape[0]
    blocks = lax.dot_general(
        picker(size, packed.shape[1], ends), packed, (((1,), (1,)), ((), ())),
        preferred_element_type=F32,
    )
    return [blocks[k * size : (k + 1) * size] for k in range(len(ends))]


def end_blocks_turned(tiles, ends):
    packed = jnp.concatenate(tiles, axis=1).astype(BF16)
    return lax.dot_general(
        packed, picker(packed.shape[0], packed.shape[1], ends), (((1,), (1,)), ((), ())),
        preferred_element_type=F32,
    )


def edge_rows(firsts, lasts, count):
    lane = lanes(firsts[0][0])
    tile = jnp.zeros(lane.shape, F32)
    for k, (column, where) in enumerate(firsts + lasts):
        tile = jnp.where(lane == k, turn(column, k - where), tile)
    return jnp.transpose(tile)[:EDGES]


def wrong(rhs_ref, vector_ref, diag, coupling, work):
    vector = vector_ref[...]
    lane = lanes(vector)
    lower = jnp.where(lane == 0, 0.0, turn(vector, 1))
    upward = operate(diag, coupling, vector_ref, work, lower)
    upper = jnp.where(lane == vector.shape[1] - 1, 0.0, turn(upward, -1))
    return rhs_ref[...] - (work[...] + upper)


def first_kernel(
    rhs_in, guess_in, diag_in, inverse_in, coupling_in, prolong_in, coarse_in, aggregate_in,
    rhs, diag, inverse, coupling, prolong, coarse, aggregate,
    trial, twice, near, far, own, rows_out,
    guess, diag_half, inverse_half, coupling_half, work, sems,
):
    size, count = guess.shape
    parts = diag_half.shape[0] // LOAD
    copies = [
        pltpu.make_async_copy(guess_in, guess, sems.at[0]),
        pltpu.make_async_copy(rhs_in, rhs, sems.at[1]),
    ]
    for p in range(parts):
        rows = pl.ds(p * LOAD, LOAD)
        for source, target in ((coupling_in, coupling_half), (diag_in, diag_half)):
            copies.append(
                pltpu.make_async_copy(source.at[rows], target.at[rows], sems.at[len(copies)])
            )
    for p in range(parts):
        rows = pl.ds(p * LOAD, LOAD)
        copies.append(
            pltpu.make_async_copy(inverse_in.at[rows], inverse_half.at[rows], sems.at[len(copies)])
        )
    for source, target in ((prolong_in, prolong), (coarse_in, coarse), (aggregate_in, aggregate)):
        copies.append(pltpu.make_async_copy(source, target, sems.at[len(copies)]))
    for copy in copies:
        copy.start()
    copies[0].wait()

    start = guess[...]
    lane = lanes(start)
    lower = jnp.where(lane == 0, 0.0, turn(start, 1))
    upward = jnp.zeros_like(start)
    diag_ends = [jnp.zeros_like(start) for _ in range(4)]
    inverse_ends, coupling_ends, prolong_ends = list(diag_ends), list(diag_ends), list(diag_ends)
    for chunk in range(size // ROWS):
        if chunk * ROWS % LOAD == 0:
            at = 2 + 2 * (chunk * ROWS // LOAD)
            copies[at].wait()
            copies[at + 1].wait()
        sums = []
        for i in range(chunk * ROWS, chunk * ROWS + ROWS):
            pair = coupling_half[i].astype(F32)
            block = diag_half[i].astype(F32)
            coupling[i] = pair
            diag[i] = block
            t, row = divmod(i, size // 4)
            diag_ends[t] = place(diag_ends[t], block, row)
            sums.append(jnp.sum(block * start + pair * lower, axis=0, keepdims=True))
            upward = upward + pair * guess[i : i + 1, :]
        work[pl.ds(chunk * ROWS, ROWS), :] = jnp.concatenate(sums, axis=0)
    upper = jnp.where(lane == count - 1, 0.0, turn(upward, -1))
    copies[1].wait()
    defect = rhs[...] - (work[...] + upper)

    for chunk in range(size // ROWS):
        if chunk * ROWS % LOAD == 0:
            copies[2 + 2 * parts + chunk * ROWS // LOAD].wait()
        rows = pl.ds(chunk * ROWS, ROWS)
        sums = []
        for i in range(chunk * ROWS, chunk * ROWS + ROWS):
            block = inverse_half[i].astype(F32)
            inverse[i] = block
            t, row = divmod(i, size // 4)
            inverse_ends[t] = place(inverse_ends[t], block, row)
            sums.append(jnp.sum(block * defect, axis=0, keepdims=True))
        trial[rows, :] = guess[rows, :] + jnp.concatenate(sums, axis=0)

    second = trial[...]
    lower = jnp.where(lane == 0, 0.0, turn(second, 1))
    upward = jnp.zeros_like(start)
    for chunk in range(size // ROWS):
        sums = []
        for i in range(chunk * ROWS, chunk * ROWS + ROWS):
            pair = coupling[i]
            t, row = divmod(i, size // 4)
            coupling_ends[t] = place(coupling_ends[t], pair, row)
            sums.append(jnp.sum(diag[i] * second + pair * lower, axis=0, keepdims=True))
            upward = upward + pair * trial[i : i + 1, :]
        work[pl.ds(chunk * ROWS, ROWS), :] = jnp.concatenate(sums, axis=0)
    upper = jnp.where(lane == count - 1, 0.0, turn(upward, -1))
    defect = rhs[...] - (work[...] + upper)

    for copy in copies[-3:]:
        copy.wait()
    for chunk in range(size // ROWS):
        rows = pl.ds(chunk * ROWS, ROWS)
        sums = []
        for i in range(chunk * ROWS, chunk * ROWS + ROWS):
            t, row = divmod(i, size // 4)
            prolong_ends[t] = place(prolong_ends[t], prolong[i].astype(F32), row)
            sums.append(jnp.sum(inverse[i] * defect, axis=0, keepdims=True))
        twice[rows, :] = trial[rows, :] + jnp.concatenate(sums, axis=0)

    last = count - 1
    named = jnp.broadcast_to(aggregate[...].astype(F32), (size, count))
    after = twice[...]
    both = [(start, 0), (second, 0), (defect, 0), (after, 1), (after, 2), (rhs[...], 0), (rhs[...], 1)]
    both = both + [(named, 0), (named, 1), (named, 2)]
    rows = edge_rows(both, [(column, last - k) for column, k in both], count)
    rows_out[...] = rows
    diag_turned = end_blocks_turned(diag_ends, (1, 2, 3, 4))
    coupling_turned = end_blocks_turned(coupling_ends, (1, 2, 3, 4))
    inverses = end_blocks(inverse_ends, (1, 2, 3, 4))
    couplings = end_blocks(coupling_ends, (2, 3, 4, 5))
    prolongs = end_blocks(prolong_ends, (0, 1, 2, 3, 4, 5))
    turned_diag = [diag_turned[:, k * size : (k + 1) * size] for k in range(4)]
    turned = [coupling_turned[:, k * size : (k + 1) * size] for k in range(4)]
    lasts = (
        (turned_diag[1], inverses[1]), (couplings[0], turned[1]), (prolongs[2], prolongs[1]),
        (prolongs[0], turned[0]), (turned_diag[0], inverses[0]), (couplings[2], turned[3]),
    )
    firsts = (
        (turned_diag[2], inverses[2]), (couplings[1], turned[2]), (prolongs[3], prolongs[4]),
        (prolongs[5], couplings[3]), (turned_diag[3], inverses[3]), (couplings[2], turned[3]),
    )
    even = even_device()
    for k, (one, other) in enumerate(zip(lasts, firsts)):
        one, other = jnp.concatenate(one, axis=1), jnp.concatenate(other, axis=1)
        at = slice(k * size, (k + 1) * size)
        near[at] = jnp.where(even, one, other).astype(BF16)
        far[at] = jnp.where(even, other, one).astype(BF16)
    shares = jnp.concatenate([stack(rows), jnp.zeros((ROWS, size), F32)], axis=0)
    shares = jnp.concatenate([shares, shares], axis=1).astype(BF16)
    near[len(lasts) * size :] = shares
    far[len(lasts) * size :] = shares
    blocks = [turned_diag[1], turned_diag[2]] + inverses
    for k, block in enumerate(blocks + [couplings[0], couplings[1], turned[2], turned[3]]):
        own[k] = block


def beyond_ends(even, near, far, size):
    tiles = 6
    near_pairs = near[: tiles * size].astype(F32)
    far_pairs = far[: tiles * size].astype(F32)
    sides = []
    for pairs in (jnp.where(even, far_pairs, near_pairs), jnp.where(even, near_pairs, far_pairs)):
        pairs = [pairs[k * size : (k + 1) * size] for k in range(tiles)]
        sides.append([(pair[:, :size], pair[:, size:]) for pair in pairs])
    near_rows, far_rows = (
        sum(
            side[tiles * size :, :size].astype(F32)[k * EDGES : (k + 1) * EDGES]
            for k in range(3)
        )
        for side in (near, far)
    )
    rows = [jnp.where(even, far_rows, near_rows), jnp.where(even, near_rows, far_rows)]
    return sides, rows


def columns_from(size):
    shape = (size, size)
    unit = lax.broadcasted_iota(jnp.int32, shape, 0) == lax.broadcasted_iota(jnp.int32, shape, 1)
    return lambda row: jnp.sum(jnp.where(unit, row, 0.0), axis=1, keepdims=True)


def ends(lane, first, last):
    return jnp.where(lane == 0, first, jnp.where(lane == lane.shape[1] - 1, last, 0.0))


def second_kernel(
    group_count, rhs, trial, trial_twice, diag, coupling, own, rows, near, far,
    prolong, aggregate, twice, partial, ghosts, work,
):
    size, count = rhs.shape
    (left_blocks, right_blocks), (left, right) = beyond_ends(even_device(), near, far, size)
    column = columns_from(size)
    half = EDGE_ROWS
    (left_diag, left_inverse), (left_coupling, _), _, _, (_, left_next_inverse), _ = left_blocks
    (right_diag, right_inverse), (right_coupling, right_turned) = right_blocks[:2]
    right_next_inverse, right_next_turned = right_blocks[4][1], right_blocks[5][1]
    last_diag, first_diag = own[0], own[1]
    before_inverse, last_inverse, first_inverse, second_inverse = (own[2 + k] for k in range(4))
    last_coupling, first_coupling, first_turned, second_turned = (own[6 + k] for k in range(4))
    first_start, first_trial, last_start, last_trial = (
        column(rows[k : k + 1]) for k in (0, 1, half, half + 1)
    )
    left_start, left_trial, left_second, left_third = (
        column(left[half + k : half + k + 1]) for k in (0, 1, 3, 4)
    )
    right_start, right_trial, right_second, right_third = (
        column(right[k : k + 1]) for k in (0, 1, 3, 4)
    )
    left_wrong, right_wrong = left[half + 2 : half + 3], right[2:3]

    first_change = -to_column(first_inverse, to_row(first_turned, left_start))
    last_change = -to_column(last_inverse, to_row(right_coupling, right_start))
    left_change = -to_column(left_inverse, to_row(first_coupling, first_start))
    right_change = -to_column(right_inverse, to_row(right_turned, last_start))
    left_once, right_once = left_trial + left_change, right_trial + right_change
    first_added = to_row(first_diag, first_change) + to_row(first_turned, left_once)
    last_added = to_row(last_diag, last_change) + to_row(right_coupling, right_once)
    left_added = to_row(left_diag, left_change)
    left_added = left_added + to_row(first_coupling, first_trial + first_change)
    right_added = to_row(right_diag, right_change)
    right_added = right_added + to_row(right_turned, last_trial + last_change)
    left_twice = left_once + to_column(left_inverse, left_wrong - left_added)
    right_twice = right_once + to_column(right_inverse, right_wrong - right_added)
    left_second = left_second - to_column(left_next_inverse, to_row(left_coupling, left_change))
    right_second = right_second - to_column(
        right_next_inverse, to_row(right_next_turned, right_change)
    )
    second_added = to_row(second_turned, first_change)
    before_added = to_row(last_coupling, last_change)
    lane = lax.broadcasted_iota(jnp.int32, (size, count), 1)
    change = ends(
        lane,
        first_change - to_column(first_inverse, first_added),
        last_change - to_column(last_inverse, last_added),
    )
    change = jnp.where(lane == 1, -to_column(second_inverse, second_added), change)
    change = jnp.where(lane == count - 2, -to_column(before_inverse, before_added), change)
    twice[...] = trial_twice[...] + change
    tile = jnp.zeros((size, count), F32)
    beyond = (left_twice, left_second, left_third, right_twice, right_second, right_third)
    for k, ghost in enumerate(beyond):
        tile = jnp.where(lane == k, ghost, tile)
    ghosts[...] = tile
    added = ends(
        lane,
        column(to_row(first_turned, left_twice)),
        column(to_row(right_coupling, right_twice)),
    )
    work[...] = wrong(rhs, twice, diag, coupling, work) - added
    pieces = apply_transposed(prolong, work)
    partial[...] = jnp.concatenate(
        [product(chosen(aggregate, group_count, half), pieces, ((1,), (1,))) for half in (0, 1)],
        axis=1,
    )


def chosen(aggregate, group_count, half):
    rows = group_count // 2
    local_index = jnp.broadcast_to(lax.rem(aggregate[...], group_count), (rows, aggregate.shape[1]))
    row = lax.broadcasted_iota(jnp.int32, local_index.shape, 0)
    named = (row // ROWS) * (2 * ROWS) + lax.rem(row, ROWS) + half * ROWS
    return jnp.where(local_index == named, 1.0, 0.0).astype(F32)


def coarse_kernel(shares, coarse_inverse, out):
    size = coarse_inverse.shape[0]
    rows = shares.shape[0] // ROWS
    share = shares[0:ROWS]
    for row in range(1, rows):
        share = share + shares[row * ROWS : (row + 1) * ROWS]
    share = jnp.concatenate([share[:, :size], share[:, size:]], axis=0)
    lane = lanes(share)
    value = jnp.zeros_like(share)
    for i in range(size):
        total = jnp.sum(coarse_inverse[i].astype(F32) * share, axis=1, keepdims=True)
        value = jnp.where(lane == i, total, value)
    value = jnp.concatenate([value[:ROWS], value[ROWS:]], axis=1)
    for row in range(out.shape[0] // ROWS):
        out[row * ROWS : (row + 1) * ROWS] = value


def third_kernel(
    group_count, rhs, twice, values, diag, inverse, coupling, own, near, far, ghosts,
    prolong, aggregate, solution_out, residual, start, once, work,
):
    size, count = rhs.shape
    every = values.shape[0]
    in_group = group_count // 2
    group = pl.ds(pl.multiple_of(lax.axis_index("grp") * in_group, ROWS), in_group)
    mine = three(values[group, :])
    spread = jnp.zeros((size, count), F32)
    for half in (0, 1):
        picked = chosen(aggregate, group_count, half).astype(BF16)
        for part in mine:
            both = lax.dot_general(
                part, picked, (((0,), (0,)), ((), ())), preferred_element_type=F32
            )
            spread = spread + both[half * size : (half + 1) * size]
    apply_blocks(prolong, spread, twice, start)

    (left_blocks, right_blocks), (left, right) = beyond_ends(even_device(), near, far, size)
    column = columns_from(size)
    lane = lax.broadcasted_iota(jnp.int32, (size, count), 1)
    half = EDGE_ROWS
    blank = jnp.zeros((2, size), F32)
    names = jnp.concatenate([left[half + 7 : half + 10], right[7:10], blank], axis=0)[:, 0:1]
    source = lax.broadcasted_iota(jnp.int32, (ROWS, every), 1)
    first_name = (source // ROWS) * (2 * ROWS) + lax.rem(source, ROWS)
    everything = three(values[...])
    coarse = jnp.zeros((ROWS, size), F32)
    for k in (0, 1):
        named = jnp.where(names == (first_name + k * ROWS).astype(F32), 1.0, 0.0).astype(BF16)
        for part in everything:
            both = jnp.dot(named, part, preferred_element_type=F32)
            coarse = coarse + both[:, k * size : (k + 1) * size]

    (left_diag, left_inverse), (left_coupling, left_turned) = left_blocks[:2]
    left_next_diag, left_next_inverse = left_blocks[4]
    left_next_turned = left_blocks[3][1]
    (right_diag, right_inverse), (right_coupling, right_turned) = right_blocks[:2]
    right_next_diag, right_next_inverse = right_blocks[4]
    right_next_coupling, right_next_turned = right_blocks[5]
    right_third_coupling = right_blocks[3][1]
    first_coupling, first_turned = own[7], own[8]
    prolongs = (left_blocks[2][0], left_blocks[2][1], left_blocks[3][0])
    prolongs = prolongs + (right_blocks[2][0], right_blocks[2][1], right_blocks[3][0])
    left_x, left_y, left_z, right_x, right_y, right_z = (
        ghosts[:, k : k + 1] + to_column(block, coarse[k : k + 1])
        for k, block in enumerate(prolongs)
    )
    left_rhs, left_next_rhs = left[half + 5 : half + 6], left[half + 6 : half + 7]
    right_rhs, right_next_rhs = right[5:6], right[6:7]

    def added(left_column, right_column):
        return ends(
            lane,
            column(to_row(first_turned, left_column)),
            column(to_row(right_coupling, right_column)),
        )

    def nearest(vector, left_x, left_y, right_x, right_y):
        left_sum = to_row(left_diag, left_x) + to_row(left_turned, left_y)
        left_sum = left_sum + to_row(first_coupling, vector[:, 0:1])
        right_sum = to_row(right_diag, right_x) + to_row(right_turned, vector[:, count - 1 : count])
        right_sum = right_sum + to_row(right_next_coupling, right_y)
        return (
            left_x + to_column(left_inverse, left_rhs - left_sum),
            right_x + to_column(right_inverse, right_rhs - right_sum),
        )

    defect = wrong(rhs, start, diag, coupling, work) - added(left_x, right_x)
    left_once, right_once = nearest(start, left_x, left_y, right_x, right_y)
    left_sum = to_row(left_next_diag, left_y) + to_row(left_next_turned, left_z)
    left_sum = left_sum + to_row(left_coupling, left_x)
    left_y = left_y + to_column(left_next_inverse, left_next_rhs - left_sum)
    right_sum = to_row(right_next_diag, right_y) + to_row(right_next_turned, right_x)
    right_sum = right_sum + to_row(right_third_coupling, right_z)
    right_y = right_y + to_column(right_next_inverse, right_next_rhs - right_sum)
    apply_blocks(inverse, defect, start, once)
    defect = wrong(rhs, once, diag, coupling, work) - added(left_once, right_once)
    left_twice, right_twice = nearest(once, left_once, left_y, right_once, right_y)
    apply_blocks(inverse, defect, once, solution_out)
    defect = wrong(rhs, solution_out, diag, coupling, work)
    residual[...] = defect - added(left_twice, right_twice)


def call(kernel, outs, scratch, *operands, space=pltpu.VMEM):
    inside = pl.BlockSpec(memory_space=pltpu.VMEM)
    if space == pltpu.HBM:
        operands = [pltpu.with_memory_space_constraint(x, space) for x in operands]
    single = not isinstance(outs, tuple)
    return pl.pallas_call(
        kernel,
        out_shape=outs,
        in_specs=[pl.BlockSpec(memory_space=space)] * len(operands),
        out_specs=inside if single else (inside,) * len(outs),
        scratch_shapes=scratch,
        compiler_params=pltpu.CompilerParams(vmem_limit_bytes=24 << 20),
    )(*operands)


def local(rhs, guess, diag_blocks, diag_inverse, coupling, prolong, coarse_inverse, aggregate):
    size, count = rhs.shape
    members = lax.axis_size("row")
    group_count = count * members // AGG
    assert coarse_inverse.shape[2] == 2 * ROWS and 2 * size == count and members % 2 == 0
    aggregate = aggregate.reshape(1, count)
    coarse_inverse = jnp.transpose(coarse_inverse, (0, 2, 1))

    def shape(*sizes, kind=F32):
        return jax.ShapeDtypeStruct(sizes, kind)

    tile = shape(size, count)
    blocks = shape(size, size, count)
    packed = shape(group_count // 2, count)
    edge = shape(6 * size + 3 * EDGES + ROWS, count, kind=BF16)
    line = shape(EDGES, size)
    plain = pltpu.VMEM((size, count), F32)
    half = pltpu.VMEM((size, size, count), BF16)
    loads = 2 + 3 * (size // LOAD) + 3
    (
        rhs, diag, inverse, coupling, prolong, coarse_inverse, aggregate,
        trial, trial_twice, near, far, own, rows,
    ) = call(
        first_kernel,
        (
            tile, blocks, blocks, blocks,
            shape(size, size, count, kind=BF16),
            shape(*coarse_inverse.shape, kind=BF16),
            shape(1, count, kind=jnp.int32),
            tile, tile, edge, edge, shape(10, size, size), line,
        ),
        [
            plain, half, half, half, plain,
            pltpu.SemaphoreType.DMA((loads,)),
        ],
        rhs, guess, diag_blocks, diag_inverse, coupling, prolong, coarse_inverse, aggregate,
        space=pltpu.HBM,
    )
    far = swap(far, 1)
    near = swap(near, 0)
    twice, partial, ghosts = call(
        functools.partial(second_kernel, group_count), (tile, packed, tile), [plain],
        rhs, trial, trial_twice, diag, coupling, own, rows, near, far, prolong, aggregate,
    )
    shares = lax.all_to_all(partial, "row", 0, 0, tiled=True)
    corrected = call(
        coarse_kernel, shape(lax.axis_size(BOTH) * ROWS, count), [], shares, coarse_inverse
    )
    values = lax.all_to_all(corrected, BOTH, 0, 0, tiled=True)
    return call(
        functools.partial(third_kernel, group_count), (tile, tile), [plain, plain, plain],
        rhs, twice, values, diag, inverse, coupling, own, near, far, ghosts, prolong, aggregate,
    )


def solution(mesh):
    vector = P(None, BOTH)
    blocks = P(None, None, BOTH)
    return jax.shard_map(
        local,
        mesh=mesh,
        in_specs=(vector, vector, blocks, blocks, blocks, blocks, blocks, P(BOTH)),
        out_specs=(vector, vector),
        check_vma=False,
    )
```

time: 49.7 us -> 44.7 us (0.90)
  the two profiles are of different devices: /device:TPU:2 before, /device:TPU:0 now
where the time goes in v6:
time: 44.7 us; the launch traced here: 44.5 us
  blocking collectives  27.4 us (61%)
  Pallas kernels  10.2 us (23%)
  starting transfers between devices  3.69 us (8%)
  waiting for transfers between devices  2.57 us (6%)
  between operations  0.65 us (1%)
    all_to_all x1, blocking collectives, local(): shares = lax.all_to_all(partial, 'row', 0, 0, tiled=True)  17.4 us
    pallas_call x4, Pallas kernels, call(): pl.pallas_call(kernel, out_shape=outs, in_specs=[pl.BlockSpec(memory_spac...  10.2 us
    all_to_all x1, blocking collectives, local(): values = lax.all_to_all(corrected, BOTH, 0, 0, tiled=True)  10.1 us
    ppermute x2, starting transfers between devices, swap(): return lax.ppermute(block, BOTH, pairs + [(j, i) for i, j in pairs])  3.69 us
    ppermute x2, waiting for transfers between devices, swap(): return lax.ppermute(block, BOTH, pairs + [(j, i) for i, j in pairs])  2.57 us
  transfers between devices with their start and end apart: 2, of which 1 were waited for; matrix products, arithmetic and copies ran while one was open for 0% of the time, Pallas kernels for 0%

profile of v6, /device:TPU:0, one launch (start us, length us, event | category | flops | bytes accessed | tf_op | source)
XLA Modules:
  0.0 44.5 jit_solution(529392558103835737)
XLA Ops:
  0.6 4.3 %shard_map.95 = (f32[64,128]{1,0:T(8,128)S(1)}, f32[64,64,128]{2,1,0:T(8,128)S(1)}, f32[64,64,128]{2,1,0:T(8,128)S(1)}, f32[64,64,128]{2,1,0:T(8,128)S(1)}, bf16...) custom-call(f32[64,128]{1,0:T(8,128)} %rhs_in.1, ...), custom_call_target="tpu_custom_call" | custom-call | tf_op jit(solution)/shard_map/pallas_call | solution.py:510
  4.9 3.0 %collective-permute-start = (bf16[464,128]{1,0:T(8,128)(2,1)S(1)}, bf16[464,128]{1,0:T(8,128)(2,1)S(1)}, u32[]{:S(2)}, u32[]{:S(2)}) collective-permute-start(bf16[464,128]{1,0:T(8,128)(2,1)S(1)} %get-tuple-element.25), channel_id=1, source_target_pairs={{0,1},{2,3},{4,5},{6,7},{8,9},{10,11},{12,13},{14,15},{16,17},{18,... | collective-permute-start | bytes 356360 | tf_op jit(solution)/shard_map/ppermute | solution.py:22
  7.9 0.7 %collective-permute-start.1 = (bf16[464,128]{1,0:T(8,128)(2,1)S(1)}, bf16[464,128]{1,0:T(8,128)(2,1)S(1)}, u32[]{:S(2)}, u32[]{:S(2)}) collective-permute-start(bf16[464,128]{1,0:T(8,128)(2,1)S(1)} %get-tuple-element.26), channel_id=1, source_target_pairs={{1,2},{3,4},{5,6},{7,8},{9,10},{11,12},{13,14},{15,16},{17,18},{19... | collective-permute-start | bytes 356360 | tf_op jit(solution)/shard_map/ppermute | solution.py:22
  8.6 2.6 %collective-permute-done.near = bf16[464,128]{1,0:T(8,128)(2,1)S(1)} collective-permute-done((bf16[464,128]{1,0:T(8,128)(2,1)S(1)}, bf16[464,128]{1,0:T(8,128)(2,1)S(1)}, u32[]{:S(2)}, u32[]{:S(2)}) %collective-permute-start) | collective-permute-done | bytes 118816 | tf_op jit(solution)/shard_map/ppermute | solution.py:22
  11.2 0.0 collective-permute-done.1.far
  11.2 1.7 %shard_map.96 = (f32[64,128]{1,0:T(8,128)S(1)}, f32[64,128]{1,0:T(8,128)S(1)}, f32[64,128]{1,0:T(8,128)S(1)}) custom-call(f32[64,128]{1,0:T(8,128)S(1)} %get-tuple-element.18.rhs, f32[64,128]{1,0:T(8,128)S(1)} %get-tuple-element.19.trial, f32[64,128]{1,0:T(8,128)S(1)} %get-tuple-element.20.trial_twice, f32[64,64,128]{2,1,0:T(8,128)S(1)} %get-tuple-element.21.diag, ...), custom_call_target="tpu_custom_call" | custom-call | tf_op jit(solution)/shard_map/pallas_call | solution.py:510
  12.8 17.4 %all_to_all.22 = f32[8,8,128]{2,1,0:T(8,128)S(1)} all-to-all(f32[8,8,128]{2,1,0:T(8,128)S(1)} %bitcast.9), channel_id=1, replica_groups=mesh['grp'=4,'row'=8] {'row'}, dimensions={0} | all-to-all | bytes 65536 | tf_op jit(solution)/shard_map/all_to_all | solution.py:564
  30.2 0.3 shard_map.97
  30.5 10.1 %all_to_all.23 = f32[32,8,128]{2,1,0:T(8,128)S(1)} all-to-all(f32[32,8,128]{2,1,0:T(8,128)S(1)} %bitcast.7), channel_id=1, replica_groups=mesh['grp'=4,'row'=8] {'grp','row'}, dimensions={0} | all-to-all | bytes 262144 | tf_op jit(solution)/shard_map/all_to_all | solution.py:568
  40.6 4.0 %shard_map.98 = (f32[64,128]{1,0:T(8,128)}, f32[64,128]{1,0:T(8,128)}) custom-call(f32[64,128]{1,0:T(8,128)S(1)} %get-tuple-element.18.rhs, f32[64,128]{1,0:T(8,128)S(1)} %get-tuple-element.29.twice, f32[256,128]{1,0:T(8,128)S(1)} %bitcast.6, f32[64,64,128]{2,1,0:T(8,128)S(1)} %get-tuple-element.21.diag, f32[64,64,128]{2,1,0:T(8,128)S(1)} %get-tuple-element.32.inverse, ...), custom_call_target="tpu_custom_call" | custom-call | tf_op jit(solution)/shard_map/pallas_call | solution.py:510
Async XLA Ops:
  4.9 6.3 %collective-permute-start = (bf16[464,128]{1,0:T(8,128)(2,1)S(1)}, bf16[464,128]{1,0:T(8,128)(2,1)S(1)}, u32[]{:S(2)}, u32[]{:S(2)}) collective-permute-start(bf16[464,128]{1,0:T(8,128)(2,1)S(1)} %get-tuple-element.25), channel_id=1, source_target_pairs={{0,1},{2,3},{4,5},{6,7},{8,9},{10,11},{12,13},{14,15},{16,17},{18,... | collective-permute-start | bytes 356360 | tf_op jit(solution)/shard_map/ppermute | solution.py:22
  7.9 3.2 %collective-permute-start.1 = (bf16[464,128]{1,0:T(8,128)(2,1)S(1)}, bf16[464,128]{1,0:T(8,128)(2,1)S(1)}, u32[]{:S(2)}, u32[]{:S(2)}) collective-permute-start(bf16[464,128]{1,0:T(8,128)(2,1)S(1)} %get-tuple-element.26), channel_id=1, source_target_pairs={{1,2},{3,4},{5,6},{7,8},{9,10},{11,12},{13,14},{15,16},{17,18},{19... | collective-permute-start | bytes 356360 | tf_op jit(solution)/shard_map/ppermute | solution.py:22

commit v7 on v6

--- a/solution.py
+++ b/solution.py
@@ -322,7 +322,7 @@
 
 
 def second_kernel(
-    group_count, rhs, trial, trial_twice, diag, coupling, own, rows, near, far,
+    group_count, rhs, trial, trial_twice, diag, coupling, own, rows, far, near,
     prolong, aggregate, twice, partial, ghosts, work,
 ):
     size, count = rhs.shape
@@ -559,7 +559,7 @@
     near = swap(near, 0)
     twice, partial, ghosts = call(
         functools.partial(second_kernel, group_count), (tile, packed, tile), [plain],
-        rhs, trial, trial_twice, diag, coupling, own, rows, near, far, prolong, aggregate,
+        rhs, trial, trial_twice, diag, coupling, own, rows, far, near, prolong, aggregate,
     )
     shares = lax.all_to_all(partial, "row", 0, 0, tiled=True)
     corrected = call(

time: 44.7 us -> 44.5 us (level)
  blocking collectives: 27.4 us -> 22.9 us
  starting transfers between devices: 3.69 us -> 6.46 us
  waiting for transfers between devices: 2.57 us -> 4.08 us
    all_to_all x1, blocking collectives: 17.4 us -> 13.1 us  [local(): shares = lax.all_to_all(partial, 'row', 0, 0, tiled=True)]
    ppermute x2, starting transfers between devices: 3.69 us -> 6.46 us  [swap(): return lax.ppermute(block, BOTH, pairs + [(j, i) for i, j in pairs])]
    ppermute x2, waiting for transfers between devices: 2.57 us -> 4.08 us  [swap(): return lax.ppermute(block, BOTH, pairs + [(j, i) for i, j in pairs])]
where the time goes in v7:
time: 44.5 us; the launch traced here: 44.3 us
  blocking collectives  22.9 us (51%)
  Pallas kernels  10.2 us (23%)
  starting transfers between devices  6.46 us (15%)
  waiting for transfers between devices  4.08 us (9%)
  between operations  0.65 us (1%)
    all_to_all x1, blocking collectives, local(): shares = lax.all_to_all(partial, 'row', 0, 0, tiled=True)  13.1 us
    pallas_call x4, Pallas kernels, call(): pl.pallas_call(kernel, out_shape=outs, in_specs=[pl.BlockSpec(memory_spac...  10.2 us
    all_to_all x1, blocking collectives, local(): values = lax.all_to_all(corrected, BOTH, 0, 0, tiled=True)  9.79 us
    ppermute x2, starting transfers between devices, swap(): return lax.ppermute(block, BOTH, pairs + [(j, i) for i, j in pairs])  6.46 us
    ppermute x2, waiting for transfers between devices, swap(): return lax.ppermute(block, BOTH, pairs + [(j, i) for i, j in pairs])  4.08 us
  transfers between devices with their start and end apart: 2, of which 1 were waited for; matrix products, arithmetic and copies ran while one was open for 0% of the time, Pallas kernels for 0%

profile of v7, /device:TPU:0, one launch (start us, length us, event | category | flops | bytes accessed | tf_op | source)
XLA Modules:
  0.0 44.3 jit_solution(16293114028324058700)
XLA Ops:
  0.6 4.3 %shard_map.95 = (f32[64,128]{1,0:T(8,128)S(1)}, f32[64,64,128]{2,1,0:T(8,128)S(1)}, f32[64,64,128]{2,1,0:T(8,128)S(1)}, f32[64,64,128]{2,1,0:T(8,128)S(1)}, bf16...) custom-call(f32[64,128]{1,0:T(8,128)} %rhs_in.1, ...), custom_call_target="tpu_custom_call" | custom-call | tf_op jit(solution)/shard_map/pallas_call | solution.py:510
  4.9 0.7 %collective-permute-start = (bf16[464,128]{1,0:T(8,128)(2,1)S(1)}, bf16[464,128]{1,0:T(8,128)(2,1)S(1)}, u32[]{:S(2)}, u32[]{:S(2)}) collective-permute-start(bf16[464,128]{1,0:T(8,128)(2,1)S(1)} %get-tuple-element.25), channel_id=1, source_target_pairs={{1,2},{3,4},{5,6},{7,8},{9,10},{11,12},{13,14},{15,16},{17,18},{19... | collective-permute-start | bytes 356360 | tf_op jit(solution)/shard_map/ppermute | solution.py:22
  5.6 5.8 %collective-permute-start.1 = (bf16[464,128]{1,0:T(8,128)(2,1)S(1)}, bf16[464,128]{1,0:T(8,128)(2,1)S(1)}, u32[]{:S(2)}, u32[]{:S(2)}) collective-permute-start(bf16[464,128]{1,0:T(8,128)(2,1)S(1)} %get-tuple-element.26), channel_id=1, source_target_pairs={{0,1},{2,3},{4,5},{6,7},{8,9},{10,11},{12,13},{14,15},{16,17},{18,... | collective-permute-start | bytes 356360 | tf_op jit(solution)/shard_map/ppermute | solution.py:22
  11.4 0.0 collective-permute-done.far
  11.4 4.1 %collective-permute-done.1.near = bf16[464,128]{1,0:T(8,128)(2,1)S(1)} collective-permute-done((bf16[464,128]{1,0:T(8,128)(2,1)S(1)}, bf16[464,128]{1,0:T(8,128)(2,1)S(1)}, u32[]{:S(2)}, u32[]{:S(2)}) %collective-permute-start.1) | collective-permute-done | bytes 118816 | tf_op jit(solution)/shard_map/ppermute | solution.py:22
  15.4 1.7 %shard_map.96 = (f32[64,128]{1,0:T(8,128)S(1)}, f32[64,128]{1,0:T(8,128)S(1)}, f32[64,128]{1,0:T(8,128)S(1)}) custom-call(f32[64,128]{1,0:T(8,128)S(1)} %get-tuple-element.18.rhs, f32[64,128]{1,0:T(8,128)S(1)} %get-tuple-element.19.trial, f32[64,128]{1,0:T(8,128)S(1)} %get-tuple-element.20.trial_twice, f32[64,64,128]{2,1,0:T(8,128)S(1)} %get-tuple-element.21.diag, ...), custom_call_target="tpu_custom_call" | custom-call | tf_op jit(solution)/shard_map/pallas_call | solution.py:510
  17.1 13.1 %all_to_all.22 = f32[8,8,128]{2,1,0:T(8,128)S(1)} all-to-all(f32[8,8,128]{2,1,0:T(8,128)S(1)} %bitcast.9), channel_id=1, replica_groups=mesh['grp'=4,'row'=8] {'row'}, dimensions={0} | all-to-all | bytes 65536 | tf_op jit(solution)/shard_map/all_to_all | solution.py:564
  30.2 0.3 shard_map.97
  30.5 9.8 %all_to_all.23 = f32[32,8,128]{2,1,0:T(8,128)S(1)} all-to-all(f32[32,8,128]{2,1,0:T(8,128)S(1)} %bitcast.7), channel_id=1, replica_groups=mesh['grp'=4,'row'=8] {'grp','row'}, dimensions={0} | all-to-all | bytes 262144 | tf_op jit(solution)/shard_map/all_to_all | solution.py:568
  40.3 4.0 %shard_map.98 = (f32[64,128]{1,0:T(8,128)}, f32[64,128]{1,0:T(8,128)}) custom-call(f32[64,128]{1,0:T(8,128)S(1)} %get-tuple-element.18.rhs, f32[64,128]{1,0:T(8,128)S(1)} %get-tuple-element.29.twice, f32[256,128]{1,0:T(8,128)S(1)} %bitcast.6, f32[64,64,128]{2,1,0:T(8,128)S(1)} %get-tuple-element.21.diag, f32[64,64,128]{2,1,0:T(8,128)S(1)} %get-tuple-element.32.inverse, ...), custom_call_target="tpu_custom_call" | custom-call | tf_op jit(solution)/shard_map/pallas_call | solution.py:510
Async XLA Ops:
  4.9 6.5 %collective-permute-start = (bf16[464,128]{1,0:T(8,128)(2,1)S(1)}, bf16[464,128]{1,0:T(8,128)(2,1)S(1)}, u32[]{:S(2)}, u32[]{:S(2)}) collective-permute-start(bf16[464,128]{1,0:T(8,128)(2,1)S(1)} %get-tuple-element.25), channel_id=1, source_target_pairs={{1,2},{3,4},{5,6},{7,8},{9,10},{11,12},{13,14},{15,16},{17,18},{19... | collective-permute-start | bytes 356360 | tf_op jit(solution)/shard_map/ppermute | solution.py:22
  5.6 9.9 %collective-permute-start.1 = (bf16[464,128]{1,0:T(8,128)(2,1)S(1)}, bf16[464,128]{1,0:T(8,128)(2,1)S(1)}, u32[]{:S(2)}, u32[]{:S(2)}) collective-permute-start(bf16[464,128]{1,0:T(8,128)(2,1)S(1)} %get-tuple-element.26), channel_id=1, source_target_pairs={{0,1},{2,3},{4,5},{6,7},{8,9},{10,11},{12,13},{14,15},{16,17},{18,... | collective-permute-start | bytes 356360 | tf_op jit(solution)/shard_map/ppermute | solution.py:22

commit v8 on v7

--- a/solution.py
+++ b/solution.py
@@ -15,6 +15,7 @@
 LOAD = 16
 EDGES = 24
 EDGE_ROWS = 10
+TILES = 5
 
 
 def swap(block, first):
@@ -263,19 +264,19 @@
     rows = edge_rows(both, [(column, last - k) for column, k in both], count)
     rows_out[...] = rows
     diag_turned = end_blocks_turned(diag_ends, (1, 2, 3, 4))
-    coupling_turned = end_blocks_turned(coupling_ends, (1, 2, 3, 4))
+    coupling_turned = end_blocks_turned(coupling_ends, (3, 4))
     inverses = end_blocks(inverse_ends, (1, 2, 3, 4))
-    couplings = end_blocks(coupling_ends, (2, 3, 4, 5))
+    couplings = end_blocks(coupling_ends, (1, 2, 3, 4, 5))
     prolongs = end_blocks(prolong_ends, (0, 1, 2, 3, 4, 5))
     turned_diag = [diag_turned[:, k * size : (k + 1) * size] for k in range(4)]
-    turned = [coupling_turned[:, k * size : (k + 1) * size] for k in range(4)]
+    turned = [coupling_turned[:, k * size : (k + 1) * size] for k in range(2)]
     lasts = (
-        (turned_diag[1], inverses[1]), (couplings[0], turned[1]), (prolongs[2], prolongs[1]),
-        (prolongs[0], turned[0]), (turned_diag[0], inverses[0]), (couplings[2], turned[3]),
+        (turned_diag[1], inverses[1]), (couplings[1], couplings[0]), (prolongs[2], prolongs[1]),
+        (prolongs[0], couplings[4]), (turned_diag[0], inverses[0]),
     )
     firsts = (
-        (turned_diag[2], inverses[2]), (couplings[1], turned[2]), (prolongs[3], prolongs[4]),
-        (prolongs[5], couplings[3]), (turned_diag[3], inverses[3]), (couplings[2], turned[3]),
+        (turned_diag[2], inverses[2]), (couplings[2], couplings[3]), (prolongs[3], prolongs[4]),
+        (prolongs[5], couplings[4]), (turned_diag[3], inverses[3]),
     )
     even = even_device()
     for k, (one, other) in enumerate(zip(lasts, firsts)):
@@ -283,31 +284,25 @@
         at = slice(k * size, (k + 1) * size)
         near[at] = jnp.where(even, one, other).astype(BF16)
         far[at] = jnp.where(even, other, one).astype(BF16)
-    shares = jnp.concatenate([stack(rows), jnp.zeros((ROWS, size), F32)], axis=0)
-    shares = jnp.concatenate([shares, shares], axis=1).astype(BF16)
-    near[len(lasts) * size :] = shares
-    far[len(lasts) * size :] = shares
+    high, middle, low = (part.astype(F32) for part in three(rows))
+    shares = jnp.concatenate(
+        [jnp.concatenate([high, low], axis=1), jnp.concatenate([middle, low], axis=1)], axis=0
+    ).astype(BF16)
+    near[TILES * size :] = shares
+    far[TILES * size :] = shares
     blocks = [turned_diag[1], turned_diag[2]] + inverses
-    for k, block in enumerate(blocks + [couplings[0], couplings[1], turned[2], turned[3]]):
+    for k, block in enumerate(blocks + [couplings[1], couplings[2], turned[0], turned[1]]):
         own[k] = block
 
 
 def beyond_ends(even, near, far, size):
-    tiles = 6
-    near_pairs = near[: tiles * size].astype(F32)
-    far_pairs = far[: tiles * size].astype(F32)
-    sides = []
-    for pairs in (jnp.where(even, far_pairs, near_pairs), jnp.where(even, near_pairs, far_pairs)):
-        pairs = [pairs[k * size : (k + 1) * size] for k in range(tiles)]
-        sides.append([(pair[:, :size], pair[:, size:]) for pair in pairs])
-    near_rows, far_rows = (
-        sum(
-            side[tiles * size :, :size].astype(F32)[k * EDGES : (k + 1) * EDGES]
-            for k in range(3)
-        )
-        for side in (near, far)
-    )
-    rows = [jnp.where(even, far_rows, near_rows), jnp.where(even, near_rows, far_rows)]
+    near, far = near[...].astype(F32), far[...].astype(F32)
+    sides, rows = [], []
+    for side in (jnp.where(even, far, near), jnp.where(even, near, far)):
+        pairs = [side[k * size : (k + 1) * size] for k in range(TILES)]
+        sides.append(([(pair[:, :size], pair[:, size:]) for pair in pairs], pairs[1]))
+        tail = side[TILES * size :]
+        rows.append(tail[:EDGES, :size] + tail[EDGES:, :size] + tail[:EDGES, size:])
     return sides, rows
 
 
@@ -326,24 +321,21 @@
     prolong, aggregate, twice, partial, ghosts, work,
 ):
     size, count = rhs.shape
-    (left_blocks, right_blocks), (left, right) = beyond_ends(even_device(), near, far, size)
+    sides, (left, right) = beyond_ends(even_device(), near, far, size)
+    (left_blocks, _), (right_blocks, right_pair) = sides
     column = columns_from(size)
     half = EDGE_ROWS
-    (left_diag, left_inverse), (left_coupling, _), _, _, (_, left_next_inverse), _ = left_blocks
-    (right_diag, right_inverse), (right_coupling, right_turned) = right_blocks[:2]
-    right_next_inverse, right_next_turned = right_blocks[4][1], right_blocks[5][1]
+    left_diag, left_inverse = left_blocks[0]
+    (right_diag, right_inverse), (right_coupling, _) = right_blocks[:2]
+    right_turned = jnp.transpose(right_pair)[:size]
     last_diag, first_diag = own[0], own[1]
     before_inverse, last_inverse, first_inverse, second_inverse = (own[2 + k] for k in range(4))
     last_coupling, first_coupling, first_turned, second_turned = (own[6 + k] for k in range(4))
     first_start, first_trial, last_start, last_trial = (
         column(rows[k : k + 1]) for k in (0, 1, half, half + 1)
     )
-    left_start, left_trial, left_second, left_third = (
-        column(left[half + k : half + k + 1]) for k in (0, 1, 3, 4)
-    )
-    right_start, right_trial, right_second, right_third = (
-        column(right[k : k + 1]) for k in (0, 1, 3, 4)
-    )
+    left_start, left_trial = (column(left[half + k : half + k + 1]) for k in (0, 1))
+    right_start, right_trial = (column(right[k : k + 1]) for k in (0, 1))
     left_wrong, right_wrong = left[half + 2 : half + 3], right[2:3]
 
     first_change = -to_column(first_inverse, to_row(first_turned, left_start))
@@ -359,10 +351,6 @@
     right_added = right_added + to_row(right_turned, last_trial + last_change)
     left_twice = left_once + to_column(left_inverse, left_wrong - left_added)
     right_twice = right_once + to_column(right_inverse, right_wrong - right_added)
-    left_second = left_second - to_column(left_next_inverse, to_row(left_coupling, left_change))
-    right_second = right_second - to_column(
-        right_next_inverse, to_row(right_next_turned, right_change)
-    )
     second_added = to_row(second_turned, first_change)
     before_added = to_row(last_coupling, last_change)
     lane = lax.broadcasted_iota(jnp.int32, (size, count), 1)
@@ -375,8 +363,7 @@
     change = jnp.where(lane == count - 2, -to_column(before_inverse, before_added), change)
     twice[...] = trial_twice[...] + change
     tile = jnp.zeros((size, count), F32)
-    beyond = (left_twice, left_second, left_third, right_twice, right_second, right_third)
-    for k, ghost in enumerate(beyond):
+    for k, ghost in enumerate((left_twice, left_change, right_twice, right_change)):
         tile = jnp.where(lane == k, ghost, tile)
     ghosts[...] = tile
     added = ends(
@@ -386,10 +373,10 @@
     )
     work[...] = wrong(rhs, twice, diag, coupling, work) - added
     pieces = apply_transposed(prolong, work)
-    partial[...] = jnp.concatenate(
-        [product(chosen(aggregate, group_count, half), pieces, ((1,), (1,))) for half in (0, 1)],
-        axis=1,
-    )
+    picked = [chosen(aggregate, group_count, half) for half in (0, 1)]
+    both = product(jnp.concatenate(picked, axis=0), pieces, ((1,), (1,)))
+    rows_out = group_count // 2
+    partial[...] = jnp.concatenate([both[:rows_out], both[rows_out:]], axis=1)
 
 
 def chosen(aggregate, group_count, half):
@@ -426,17 +413,16 @@
     in_group = group_count // 2
     group = pl.ds(pl.multiple_of(lax.axis_index("grp") * in_group, ROWS), in_group)
     mine = three(values[group, :])
+    picked = [chosen(aggregate, group_count, half) for half in (0, 1)]
+    picked = jnp.concatenate(picked, axis=1).astype(BF16)
     spread = jnp.zeros((size, count), F32)
-    for half in (0, 1):
-        picked = chosen(aggregate, group_count, half).astype(BF16)
-        for part in mine:
-            both = lax.dot_general(
-                part, picked, (((0,), (0,)), ((), ())), preferred_element_type=F32
-            )
-            spread = spread + both[half * size : (half + 1) * size]
+    for part in mine:
+        both = lax.dot_general(part, picked, (((0,), (0,)), ((), ())), preferred_element_type=F32)
+        spread = spread + (both[:size, :count] + both[size:, count:])
     apply_blocks(prolong, spread, twice, start)
 
-    (left_blocks, right_blocks), (left, right) = beyond_ends(even_device(), near, far, size)
+    sides, (left, right) = beyond_ends(even_device(), near, far, size)
+    (left_blocks, left_pair), (right_blocks, right_pair) = sides
     column = columns_from(size)
     lane = lax.broadcasted_iota(jnp.int32, (size, count), 1)
     half = EDGE_ROWS
@@ -445,26 +431,35 @@
     source = lax.broadcasted_iota(jnp.int32, (ROWS, every), 1)
     first_name = (source // ROWS) * (2 * ROWS) + lax.rem(source, ROWS)
     everything = three(values[...])
+    named = [
+        jnp.where(names == (first_name + k * ROWS).astype(F32), 1.0, 0.0) for k in (0, 1)
+    ]
+    named = jnp.concatenate(named, axis=0).astype(BF16)
     coarse = jnp.zeros((ROWS, size), F32)
-    for k in (0, 1):
-        named = jnp.where(names == (first_name + k * ROWS).astype(F32), 1.0, 0.0).astype(BF16)
-        for part in everything:
-            both = jnp.dot(named, part, preferred_element_type=F32)
-            coarse = coarse + both[:, k * size : (k + 1) * size]
-
-    (left_diag, left_inverse), (left_coupling, left_turned) = left_blocks[:2]
+    for part in everything:
+        both = jnp.dot(named, part, preferred_element_type=F32)
+        coarse = coarse + (both[:ROWS, :size] + both[ROWS:, size:])
+
+    (left_diag, left_inverse), (left_coupling, _) = left_blocks[:2]
     left_next_diag, left_next_inverse = left_blocks[4]
-    left_next_turned = left_blocks[3][1]
-    (right_diag, right_inverse), (right_coupling, right_turned) = right_blocks[:2]
+    left_pair, right_pair = jnp.transpose(left_pair), jnp.transpose(right_pair)
+    left_turned, left_next_turned = left_pair[:size], left_pair[size:]
+    (right_diag, right_inverse), (right_coupling, right_next_coupling) = right_blocks[:2]
     right_next_diag, right_next_inverse = right_blocks[4]
-    right_next_coupling, right_next_turned = right_blocks[5]
+    right_turned, right_next_turned = right_pair[:size], right_pair[size:]
     right_third_coupling = right_blocks[3][1]
     first_coupling, first_turned = own[7], own[8]
+    left_x, left_change, right_x, right_change = (ghosts[:, k : k + 1] for k in range(4))
+    left_y, left_z = (column(left[half + k : half + k + 1]) for k in (3, 4))
+    right_y, right_z = (column(right[k : k + 1]) for k in (3, 4))
+    left_y = left_y - to_column(left_next_inverse, to_row(left_coupling, left_change))
+    right_y = right_y - to_column(right_next_inverse, to_row(right_next_turned, right_change))
     prolongs = (left_blocks[2][0], left_blocks[2][1], left_blocks[3][0])
     prolongs = prolongs + (right_blocks[2][0], right_blocks[2][1], right_blocks[3][0])
+    known = (left_x, left_y, left_z, right_x, right_y, right_z)
     left_x, left_y, left_z, right_x, right_y, right_z = (
-        ghosts[:, k : k + 1] + to_column(block, coarse[k : k + 1])
-        for k, block in enumerate(prolongs)
+        value + to_column(block, coarse[k : k + 1])
+        for k, (value, block) in enumerate(zip(known, prolongs))
     )
     left_rhs, left_next_rhs = left[half + 5 : half + 6], left[half + 6 : half + 7]
     right_rhs, right_next_rhs = right[5:6], right[6:7]
@@ -531,7 +526,7 @@
     tile = shape(size, count)
     blocks = shape(size, size, count)
     packed = shape(group_count // 2, count)
-    edge = shape(6 * size + 3 * EDGES + ROWS, count, kind=BF16)
+    edge = shape(TILES * size + 2 * EDGES, count, kind=BF16)
     line = shape(EDGES, size)
     plain = pltpu.VMEM((size, count), F32)
     half = pltpu.VMEM((size, size, count), BF16)

time: 44.5 us -> 43.9 us (0.987)
  waiting for transfers between devices: 4.08 us -> 2.76 us
  blocking collectives: 22.9 us -> 23.7 us
    ppermute x2, waiting for transfers between devices: 4.08 us -> 2.76 us  [swap(): return lax.ppermute(block, BOTH, pairs + [(j, i) for i, j in pairs])]
    all_to_all x1, blocking collectives: 9.79 us -> 10.5 us  [local(): values = lax.all_to_all(corrected, BOTH, 0, 0, tiled=True)]
where the time goes in v8:
time: 43.9 us; the launch traced here: 43.7 us
  blocking collectives  23.7 us (54%)
  Pallas kernels  10.1 us (23%)
  starting transfers between devices  6.46 us (15%)
  waiting for transfers between devices  2.76 us (6%)
  between operations  0.66 us (2%)
    all_to_all x1, blocking collectives, local(): shares = lax.all_to_all(partial, 'row', 0, 0, tiled=True)  13.2 us
    all_to_all x1, blocking collectives, local(): values = lax.all_to_all(corrected, BOTH, 0, 0, tiled=True)  10.5 us
    pallas_call x4, Pallas kernels, call(): pl.pallas_call(kernel, out_shape=outs, in_specs=[pl.BlockSpec(memory_spac...  10.1 us
    ppermute x2, starting transfers between devices, swap(): return lax.ppermute(block, BOTH, pairs + [(j, i) for i, j in pairs])  6.46 us
    ppermute x2, waiting for transfers between devices, swap(): return lax.ppermute(block, BOTH, pairs + [(j, i) for i, j in pairs])  2.76 us
  transfers between devices with their start and end apart: 2, of which 1 were waited for; matrix products, arithmetic and copies ran while one was open for 0% of the time, Pallas kernels for 0%

profile of v8, /device:TPU:0, one launch (start us, length us, event | category | flops | bytes accessed | tf_op | source)
XLA Modules:
  0.0 43.7 jit_solution(2236881858473971113)
XLA Ops:
  0.6 4.3 %shard_map.95 = (f32[64,128]{1,0:T(8,128)S(1)}, f32[64,64,128]{2,1,0:T(8,128)S(1)}, f32[64,64,128]{2,1,0:T(8,128)S(1)}, f32[64,64,128]{2,1,0:T(8,128)S(1)}, bf16...) custom-call(f32[64,128]{1,0:T(8,128)} %rhs_in.1, ...), custom_call_target="tpu_custom_call" | custom-call | tf_op jit(solution)/shard_map/pallas_call | solution.py:505
  4.9 0.7 %collective-permute-start = (bf16[368,128]{1,0:T(8,128)(2,1)S(1)}, bf16[368,128]{1,0:T(8,128)(2,1)S(1)}, u32[]{:S(2)}, u32[]{:S(2)}) collective-permute-start(bf16[368,128]{1,0:T(8,128)(2,1)S(1)} %get-tuple-element.25), channel_id=1, source_target_pairs={{1,2},{3,4},{5,6},{7,8},{9,10},{11,12},{13,14},{15,16},{17,18},{19... | collective-permute-start | bytes 282632 | tf_op jit(solution)/shard_map/ppermute | solution.py:23
  5.6 5.8 %collective-permute-start.1 = (bf16[368,128]{1,0:T(8,128)(2,1)S(1)}, bf16[368,128]{1,0:T(8,128)(2,1)S(1)}, u32[]{:S(2)}, u32[]{:S(2)}) collective-permute-start(bf16[368,128]{1,0:T(8,128)(2,1)S(1)} %get-tuple-element.26), channel_id=1, source_target_pairs={{0,1},{2,3},{4,5},{6,7},{8,9},{10,11},{12,13},{14,15},{16,17},{18,... | collective-permute-start | bytes 282632 | tf_op jit(solution)/shard_map/ppermute | solution.py:23
  11.4 0.0 collective-permute-done.far
  11.4 2.8 %collective-permute-done.1.near = bf16[368,128]{1,0:T(8,128)(2,1)S(1)} collective-permute-done((bf16[368,128]{1,0:T(8,128)(2,1)S(1)}, bf16[368,128]{1,0:T(8,128)(2,1)S(1)}, u32[]{:S(2)}, u32[]{:S(2)}) %collective-permute-start.1) | collective-permute-done | bytes 94240 | tf_op jit(solution)/shard_map/ppermute | solution.py:23
  14.1 1.6 %shard_map.96 = (f32[64,128]{1,0:T(8,128)S(1)}, f32[64,128]{1,0:T(8,128)S(1)}, f32[64,128]{1,0:T(8,128)S(1)}) custom-call(f32[64,128]{1,0:T(8,128)S(1)} %get-tuple-element.18.rhs, f32[64,128]{1,0:T(8,128)S(1)} %get-tuple-element.19.trial, f32[64,128]{1,0:T(8,128)S(1)} %get-tuple-element.20.trial_twice, f32[64,64,128]{2,1,0:T(8,128)S(1)} %get-tuple-element.21.diag, ...), custom_call_target="tpu_custom_call" | custom-call | tf_op jit(solution)/shard_map/pallas_call | solution.py:505
  15.7 13.2 %all_to_all.22 = f32[8,8,128]{2,1,0:T(8,128)S(1)} all-to-all(f32[8,8,128]{2,1,0:T(8,128)S(1)} %bitcast.9), channel_id=1, replica_groups=mesh['grp'=4,'row'=8] {'row'}, dimensions={0} | all-to-all | bytes 65536 | tf_op jit(solution)/shard_map/all_to_all | solution.py:559
  28.9 0.3 shard_map.97
  29.2 10.5 %all_to_all.23 = f32[32,8,128]{2,1,0:T(8,128)S(1)} all-to-all(f32[32,8,128]{2,1,0:T(8,128)S(1)} %bitcast.7), channel_id=1, replica_groups=mesh['grp'=4,'row'=8] {'grp','row'}, dimensions={0} | all-to-all | bytes 262144 | tf_op jit(solution)/shard_map/all_to_all | solution.py:563
  39.7 4.0 %shard_map.98 = (f32[64,128]{1,0:T(8,128)}, f32[64,128]{1,0:T(8,128)}) custom-call(f32[64,128]{1,0:T(8,128)S(1)} %get-tuple-element.18.rhs, f32[64,128]{1,0:T(8,128)S(1)} %get-tuple-element.29.twice, f32[256,128]{1,0:T(8,128)S(1)} %bitcast.6, f32[64,64,128]{2,1,0:T(8,128)S(1)} %get-tuple-element.21.diag, f32[64,64,128]{2,1,0:T(8,128)S(1)} %get-tuple-element.32.inverse, ...), custom_call_target="tpu_custom_call" | custom-call | tf_op jit(solution)/shard_map/pallas_call | solution.py:505
Async XLA Ops:
  4.9 6.5 %collective-permute-start = (bf16[368,128]{1,0:T(8,128)(2,1)S(1)}, bf16[368,128]{1,0:T(8,128)(2,1)S(1)}, u32[]{:S(2)}, u32[]{:S(2)}) collective-permute-start(bf16[368,128]{1,0:T(8,128)(2,1)S(1)} %get-tuple-element.25), channel_id=1, source_target_pairs={{1,2},{3,4},{5,6},{7,8},{9,10},{11,12},{13,14},{15,16},{17,18},{19... | collective-permute-start | bytes 282632 | tf_op jit(solution)/shard_map/ppermute | solution.py:23
  5.6 8.6 %collective-permute-start.1 = (bf16[368,128]{1,0:T(8,128)(2,1)S(1)}, bf16[368,128]{1,0:T(8,128)(2,1)S(1)}, u32[]{:S(2)}, u32[]{:S(2)}) collective-permute-start(bf16[368,128]{1,0:T(8,128)(2,1)S(1)} %get-tuple-element.26), channel_id=1, source_target_pairs={{0,1},{2,3},{4,5},{6,7},{8,9},{10,11},{12,13},{14,15},{16,17},{18,... | collective-permute-start | bytes 282632 | tf_op jit(solution)/shard_map/ppermute | solution.py:23

commit v9 on v8

--- a/solution.py
+++ b/solution.py
@@ -264,12 +264,12 @@
     rows = edge_rows(both, [(column, last - k) for column, k in both], count)
     rows_out[...] = rows
     diag_turned = end_blocks_turned(diag_ends, (1, 2, 3, 4))
-    coupling_turned = end_blocks_turned(coupling_ends, (3, 4))
+    coupling_turned = end_blocks_turned(coupling_ends, (2, 3, 4, 5))
     inverses = end_blocks(inverse_ends, (1, 2, 3, 4))
     couplings = end_blocks(coupling_ends, (1, 2, 3, 4, 5))
     prolongs = end_blocks(prolong_ends, (0, 1, 2, 3, 4, 5))
     turned_diag = [diag_turned[:, k * size : (k + 1) * size] for k in range(4)]
-    turned = [coupling_turned[:, k * size : (k + 1) * size] for k in range(2)]
+    turned = [coupling_turned[:, k * size : (k + 1) * size] for k in range(4)]
     lasts = (
         (turned_diag[1], inverses[1]), (couplings[1], couplings[0]), (prolongs[2], prolongs[1]),
         (prolongs[0], couplings[4]), (turned_diag[0], inverses[0]),
@@ -291,7 +291,9 @@
     near[TILES * size :] = shares
     far[TILES * size :] = shares
     blocks = [turned_diag[1], turned_diag[2]] + inverses
-    for k, block in enumerate(blocks + [couplings[1], couplings[2], turned[0], turned[1]]):
+    blocks = blocks + [couplings[1], couplings[2], turned[1], turned[2]]
+    blocks = blocks + [turned_diag[0], turned_diag[3], couplings[0], couplings[3]]
+    for k, block in enumerate(blocks + [turned[0], turned[3]] + prolongs):
         own[k] = block
 
 
@@ -316,11 +318,21 @@
     return jnp.where(lane == 0, first, jnp.where(lane == lane.shape[1] - 1, last, 0.0))
 
 
+def trial_kernel(
+    group_count, rhs, trial_twice, diag, coupling, prolong, aggregate, partial, work,
+):
+    work[...] = wrong(rhs, trial_twice, diag, coupling, work)
+    pieces = apply_transposed(prolong, work)
+    picked = [chosen(aggregate, group_count, half) for half in (0, 1)]
+    both = product(jnp.concatenate(picked, axis=0), pieces, ((1,), (1,)))
+    rows_out = group_count // 2
+    partial[...] = jnp.concatenate([both[:rows_out], both[rows_out:]], axis=1)
+
+
 def second_kernel(
-    group_count, rhs, trial, trial_twice, diag, coupling, own, rows, far, near,
-    prolong, aggregate, twice, partial, ghosts, work,
+    group_count, trial_partial, trial_twice, own, rows, near, far, twice, partial, ghosts,
 ):
-    size, count = rhs.shape
+    size, count = trial_twice.shape
     sides, (left, right) = beyond_ends(even_device(), near, far, size)
     (left_blocks, _), (right_blocks, right_pair) = sides
     column = columns_from(size)
@@ -354,29 +366,46 @@
     second_added = to_row(second_turned, first_change)
     before_added = to_row(last_coupling, last_change)
     lane = lax.broadcasted_iota(jnp.int32, (size, count), 1)
-    change = ends(
-        lane,
-        first_change - to_column(first_inverse, first_added),
-        last_change - to_column(last_inverse, last_added),
-    )
-    change = jnp.where(lane == 1, -to_column(second_inverse, second_added), change)
-    change = jnp.where(lane == count - 2, -to_column(before_inverse, before_added), change)
+    first_new = first_change - to_column(first_inverse, first_added)
+    second_new = -to_column(second_inverse, second_added)
+    before_new = -to_column(before_inverse, before_added)
+    last_new = last_change - to_column(last_inverse, last_added)
+    change = ends(lane, first_new, last_new)
+    change = jnp.where(lane == 1, second_new, change)
+    change = jnp.where(lane == count - 2, before_new, change)
     twice[...] = trial_twice[...] + change
     tile = jnp.zeros((size, count), F32)
     for k, ghost in enumerate((left_twice, left_change, right_twice, right_change)):
         tile = jnp.where(lane == k, ghost, tile)
     ghosts[...] = tile
-    added = ends(
-        lane,
-        column(to_row(first_turned, left_twice)),
-        column(to_row(right_coupling, right_twice)),
-    )
-    work[...] = wrong(rhs, twice, diag, coupling, work) - added
-    pieces = apply_transposed(prolong, work)
-    picked = [chosen(aggregate, group_count, half) for half in (0, 1)]
-    both = product(jnp.concatenate(picked, axis=0), pieces, ((1,), (1,)))
+    before_diag, second_diag, before_coupling, second_coupling = (own[10 + k] for k in range(4))
+    last_turned, third_turned = own[14], own[15]
+    prolongs = [own[16 + k] for k in range(6)]
+    added = (
+        to_row(before_coupling, before_new),
+        to_row(before_diag, before_new) + to_row(last_coupling, last_new),
+        to_row(last_diag, last_new) + to_row(last_turned, before_new)
+        + to_row(right_coupling, right_twice),
+        to_row(first_diag, first_new) + to_row(second_coupling, second_new)
+        + to_row(first_turned, left_twice),
+        to_row(second_diag, second_new) + to_row(second_turned, first_new),
+        to_row(third_turned, second_new),
+    )
+    pieces = [to_row(block, column(row)) for block, row in zip(prolongs, added)]
+    order = (half + 9, half + 8, half + 7, 7, 8, 9)
+    names = [rows[k : k + 1] for k in order]
+    blank = jnp.zeros((ROWS - 6, size), F32)
+    pieces = jnp.concatenate(pieces + [blank], axis=0)
+    names = jnp.concatenate(names + [blank], axis=0)[:, 0:1]
     rows_out = group_count // 2
-    partial[...] = jnp.concatenate([both[:rows_out], both[rows_out:]], axis=1)
+    start = (lax.axis_index("grp") * group_count).astype(F32)
+    row = lax.broadcasted_iota(jnp.int32, (ROWS, 2 * rows_out), 1)
+    half_row = lax.rem(row, rows_out)
+    named = (half_row // ROWS) * (2 * ROWS) + lax.rem(row, ROWS) + (row // rows_out) * ROWS
+    mine = jnp.where(names - start == named.astype(F32), 1.0, 0.0)
+    both = product(mine, pieces, ((0,), (0,)))
+    both = jnp.concatenate([both[:rows_out], both[rows_out:]], axis=1)
+    partial[...] = trial_partial[...] - both
 
 
 def chosen(aggregate, group_count, half):
@@ -497,7 +526,7 @@
     residual[...] = defect - added(left_twice, right_twice)
 
 
-def call(kernel, outs, scratch, *operands, space=pltpu.VMEM):
+def call(kernel, outs, scratch, *operands, space=pltpu.VMEM, cost=None):
     inside = pl.BlockSpec(memory_space=pltpu.VMEM)
     if space == pltpu.HBM:
         operands = [pltpu.with_memory_space_constraint(x, space) for x in operands]
@@ -508,6 +537,7 @@
         in_specs=[pl.BlockSpec(memory_space=space)] * len(operands),
         out_specs=inside if single else (inside,) * len(outs),
         scratch_shapes=scratch,
+        cost_estimate=cost,
         compiler_params=pltpu.CompilerParams(vmem_limit_bytes=24 << 20),
     )(*operands)
 
@@ -541,7 +571,7 @@
             shape(size, size, count, kind=BF16),
             shape(*coarse_inverse.shape, kind=BF16),
             shape(1, count, kind=jnp.int32),
-            tile, tile, edge, edge, shape(10, size, size), line,
+            tile, tile, edge, edge, shape(22, size, size), line,
         ),
         [
             plain, half, half, half, plain,
@@ -552,9 +582,14 @@
     )
     far = swap(far, 1)
     near = swap(near, 0)
+    trial_partial = call(
+        functools.partial(trial_kernel, group_count), packed, [plain],
+        rhs, trial_twice, diag, coupling, prolong, aggregate,
+        cost=pl.CostEstimate(flops=8 * size**2 * count, bytes_accessed=8 * size**2 * count, transcendentals=0),
+    )
     twice, partial, ghosts = call(
-        functools.partial(second_kernel, group_count), (tile, packed, tile), [plain],
-        rhs, trial, trial_twice, diag, coupling, own, rows, far, near, prolong, aggregate,
+        functools.partial(second_kernel, group_count), (tile, packed, tile), [],
+        trial_partial, trial_twice, own, rows, near, far,
     )
     shares = lax.all_to_all(partial, "row", 0, 0, tiled=True)
     corrected = call(

time: 43.9 us -> 44.2 us (level)
  blocking collectives: 23.7 us -> 27.4 us
  starting transfers between devices: 6.46 us -> 3.69 us
  waiting for transfers between devices: 2.76 us -> 0.71 us
  Pallas kernels: 10.1 us -> 11.5 us
    all_to_all x1, blocking collectives: 13.2 us -> 17.5 us  [local(): shares = lax.all_to_all(partial, 'row', 0, 0, tiled=True)]
    ppermute x2, starting transfers between devices: 6.46 us -> 3.69 us  [swap(): return lax.ppermute(block, BOTH, pairs + [(j, i) for i, j in pairs])]
    ppermute x2, waiting for transfers between devices: 2.76 us -> 0.71 us  [swap(): return lax.ppermute(block, BOTH, pairs + [(j, i) for i, j in pairs])]
    pallas_call x4 -> x5, Pallas kernels: 10.1 us -> 11.5 us  [call(): pl.pallas_call(kernel, out_shape=outs, in_specs=[pl.BlockSpec(memory_spac...]
    all_to_all x1, blocking collectives: 10.5 us -> 9.92 us  [local(): values = lax.all_to_all(corrected, BOTH, 0, 0, tiled=True)]
  transfers between devices with their start and end apart: 2 -> 2, of which waited for: 1 -> 1; matrix products, arithmetic and copies ran while one was open for 0% -> 0% of each run, Pallas kernels for 0% -> 3%
where the time goes in v9:
time: 44.2 us; the launch traced here: 44 us
  blocking collectives  27.4 us (62%)
  Pallas kernels  11.5 us (26%)
  starting transfers between devices  3.69 us (8%)
  waiting for transfers between devices  0.71 us (2%)
  between operations  0.66 us (1%)
    all_to_all x1, blocking collectives, local(): shares = lax.all_to_all(partial, 'row', 0, 0, tiled=True)  17.5 us
    pallas_call x5, Pallas kernels, call(): pl.pallas_call(kernel, out_shape=outs, in_specs=[pl.BlockSpec(memory_spac...  11.5 us
    all_to_all x1, blocking collectives, local(): values = lax.all_to_all(corrected, BOTH, 0, 0, tiled=True)  9.92 us
    ppermute x2, starting transfers between devices, swap(): return lax.ppermute(block, BOTH, pairs + [(j, i) for i, j in pairs])  3.69 us
  transfers between devices with their start and end apart: 2, of which 1 were waited for; matrix products, arithmetic and copies ran while one was open for 0% of the time, Pallas kernels for 3%

profile of v9, /device:TPU:0, one launch (start us, length us, event | category | flops | bytes accessed | tf_op | source)
XLA Modules:
  0.0 44.0 jit_solution(1463103023034838716)
XLA Ops:
  0.6 4.9 %shard_map.95 = (f32[64,128]{1,0:T(8,128)S(1)}, f32[64,64,128]{2,1,0:T(8,128)S(1)}, f32[64,64,128]{2,1,0:T(8,128)S(1)}, f32[64,64,128]{2,1,0:T(8,128)S(1)}, bf16...) custom-call(f32[64,128]{1,0:T(8,128)} %rhs_in.1, ...), custom_call_target="tpu_custom_call" | custom-call | tf_op jit(solution)/shard_map/pallas_call | solution.py:534
  5.5 3.0 %collective-permute-start = (bf16[368,128]{1,0:T(8,128)(2,1)S(1)}, bf16[368,128]{1,0:T(8,128)(2,1)S(1)}, u32[]{:S(2)}, u32[]{:S(2)}) collective-permute-start(bf16[368,128]{1,0:T(8,128)(2,1)S(1)} %get-tuple-element.25), channel_id=1, source_target_pairs={{0,1},{2,3},{4,5},{6,7},{8,9},{10,11},{12,13},{14,15},{16,17},{18,... | collective-permute-start | bytes 282632 | tf_op jit(solution)/shard_map/ppermute | solution.py:23
  8.5 0.7 %collective-permute-start.1 = (bf16[368,128]{1,0:T(8,128)(2,1)S(1)}, bf16[368,128]{1,0:T(8,128)(2,1)S(1)}, u32[]{:S(2)}, u32[]{:S(2)}) collective-permute-start(bf16[368,128]{1,0:T(8,128)(2,1)S(1)} %get-tuple-element.26), channel_id=1, source_target_pairs={{1,2},{3,4},{5,6},{7,8},{9,10},{11,12},{13,14},{15,16},{17,18},{19... | collective-permute-start | bytes 282632 | tf_op jit(solution)/shard_map/ppermute | solution.py:23
  9.2 1.3 %shard_map.96.trial_partial = f32[64,128]{1,0:T(8,128)S(1)} custom-call(f32[64,128]{1,0:T(8,128)S(1)} %get-tuple-element.17.rhs, f32[64,128]{1,0:T(8,128)S(1)} %get-tuple-element.18.trial_twice, f32[64,64,128]{2,1,0:T(8,128)S(1)} %get-tuple-element.19.diag, f32[64,64,128]{2,1,0:T(8,128)S(1)} %get-tuple-element.20.coupling, ...), custom_call_target="tpu_custom_call" | custom-call | flops 4194304 | bytes 4194304 | tf_op jit(solution)/shard_map/pallas_call | solution.py:534
  10.5 0.7 %collective-permute-done.near = bf16[368,128]{1,0:T(8,128)(2,1)S(1)} collective-permute-done((bf16[368,128]{1,0:T(8,128)(2,1)S(1)}, bf16[368,128]{1,0:T(8,128)(2,1)S(1)}, u32[]{:S(2)}, u32[]{:S(2)}) %collective-permute-start) | collective-permute-done | bytes 94240 | tf_op jit(solution)/shard_map/ppermute | solution.py:23
  11.2 0.0 collective-permute-done.1.far
  11.2 1.0 %shard_map.97 = (f32[64,128]{1,0:T(8,128)S(1)}, f32[64,128]{1,0:T(8,128)S(1)}, f32[64,128]{1,0:T(8,128)S(1)}) custom-call(f32[64,128]{1,0:T(8,128)S(1)} %shard_map.96.trial_partial, f32[64,128]{1,0:T(8,128)S(1)} %get-tuple-element.18.trial_twice, f32[22,64,64]{2,1,0:T(8,128)S(1)} %get-tuple-element.23.own, f32[24,64]{1,0:T(8,128)S(1)} %get-tuple-element.24.rows, ...), custom_call_target="tpu_custom_call" | custom-call | tf_op jit(solution)/shard_map/pallas_call | solution.py:534
  12.3 17.5 %all_to_all.22 = f32[8,8,128]{2,1,0:T(8,128)S(1)} all-to-all(f32[8,8,128]{2,1,0:T(8,128)S(1)} %bitcast.9), channel_id=1, replica_groups=mesh['grp'=4,'row'=8] {'row'}, dimensions={0} | all-to-all | bytes 65536 | tf_op jit(solution)/shard_map/all_to_all | solution.py:594
  29.8 0.3 shard_map.98
  30.1 9.9 %all_to_all.23 = f32[32,8,128]{2,1,0:T(8,128)S(1)} all-to-all(f32[32,8,128]{2,1,0:T(8,128)S(1)} %bitcast.7), channel_id=1, replica_groups=mesh['grp'=4,'row'=8] {'grp','row'}, dimensions={0} | all-to-all | bytes 262144 | tf_op jit(solution)/shard_map/all_to_all | solution.py:598
  40.0 4.0 %shard_map.99 = (f32[64,128]{1,0:T(8,128)}, f32[64,128]{1,0:T(8,128)}) custom-call(f32[64,128]{1,0:T(8,128)S(1)} %get-tuple-element.17.rhs, f32[64,128]{1,0:T(8,128)S(1)} %get-tuple-element.27.twice, f32[256,128]{1,0:T(8,128)S(1)} %bitcast.6, f32[64,64,128]{2,1,0:T(8,128)S(1)} %get-tuple-element.19.diag, f32[64,64,128]{2,1,0:T(8,128)S(1)} %get-tuple-element.30.inverse, ...), custom_call_target="tpu_custom_call" | custom-call | tf_op jit(solution)/shard_map/pallas_call | solution.py:534
Async XLA Ops:
  5.5 5.7 %collective-permute-start = (bf16[368,128]{1,0:T(8,128)(2,1)S(1)}, bf16[368,128]{1,0:T(8,128)(2,1)S(1)}, u32[]{:S(2)}, u32[]{:S(2)}) collective-permute-start(bf16[368,128]{1,0:T(8,128)(2,1)S(1)} %get-tuple-element.25), channel_id=1, source_target_pairs={{0,1},{2,3},{4,5},{6,7},{8,9},{10,11},{12,13},{14,15},{16,17},{18,... | collective-permute-start | bytes 282632 | tf_op jit(solution)/shard_map/ppermute | solution.py:23
  8.5 2.7 %collective-permute-start.1 = (bf16[368,128]{1,0:T(8,128)(2,1)S(1)}, bf16[368,128]{1,0:T(8,128)(2,1)S(1)}, u32[]{:S(2)}, u32[]{:S(2)}) collective-permute-start(bf16[368,128]{1,0:T(8,128)(2,1)S(1)} %get-tuple-element.26), channel_id=1, source_target_pairs={{1,2},{3,4},{5,6},{7,8},{9,10},{11,12},{13,14},{15,16},{17,18},{19... | collective-permute-start | bytes 282632 | tf_op jit(solution)/shard_map/ppermute | solution.py:23

commit v10 on v9

--- a/solution.py
+++ b/solution.py
@@ -165,7 +165,7 @@
 def first_kernel(
     rhs_in, guess_in, diag_in, inverse_in, coupling_in, prolong_in, coarse_in, aggregate_in,
     rhs, diag, inverse, coupling, prolong, coarse, aggregate,
-    trial, twice, near, far, own, rows_out,
+    trial, twice, near, far, rows_out,
     guess, diag_half, inverse_half, coupling_half, work, sems,
 ):
     size, count = guess.shape
@@ -264,12 +264,10 @@
     rows = edge_rows(both, [(column, last - k) for column, k in both], count)
     rows_out[...] = rows
     diag_turned = end_blocks_turned(diag_ends, (1, 2, 3, 4))
-    coupling_turned = end_blocks_turned(coupling_ends, (2, 3, 4, 5))
     inverses = end_blocks(inverse_ends, (1, 2, 3, 4))
     couplings = end_blocks(coupling_ends, (1, 2, 3, 4, 5))
     prolongs = end_blocks(prolong_ends, (0, 1, 2, 3, 4, 5))
     turned_diag = [diag_turned[:, k * size : (k + 1) * size] for k in range(4)]
-    turned = [coupling_turned[:, k * size : (k + 1) * size] for k in range(4)]
     lasts = (
         (turned_diag[1], inverses[1]), (couplings[1], couplings[0]), (prolongs[2], prolongs[1]),
         (prolongs[0], couplings[4]), (turned_diag[0], inverses[0]),
@@ -290,12 +288,6 @@
     ).astype(BF16)
     near[TILES * size :] = shares
     far[TILES * size :] = shares
-    blocks = [turned_diag[1], turned_diag[2]] + inverses
-    blocks = blocks + [couplings[1], couplings[2], turned[1], turned[2]]
-    blocks = blocks + [turned_diag[0], turned_diag[3], couplings[0], couplings[3]]
-    for k, block in enumerate(blocks + [turned[0], turned[3]] + prolongs):
-        own[k] = block
-
 
 def beyond_ends(even, near, far, size):
     near, far = near[...].astype(F32), far[...].astype(F32)
@@ -319,7 +311,8 @@
 
 
 def trial_kernel(
-    group_count, rhs, trial_twice, diag, coupling, prolong, aggregate, partial, work,
+    group_count, rhs, trial_twice, diag, coupling, prolong, aggregate, near, far,
+    partial, own, work,
 ):
     work[...] = wrong(rhs, trial_twice, diag, coupling, work)
     pieces = apply_transposed(prolong, work)
@@ -327,6 +320,26 @@
     both = product(jnp.concatenate(picked, axis=0), pieces, ((1,), (1,)))
     rows_out = group_count // 2
     partial[...] = jnp.concatenate([both[:rows_out], both[rows_out:]], axis=1)
+
+    size = rhs.shape[0]
+    even = even_device()
+    near, far = near[: TILES * size].astype(F32), far[: TILES * size].astype(F32)
+    lasts, firsts = (
+        [side[k * size : (k + 1) * size] for k in range(TILES)]
+        for side in (jnp.where(even, near, far), jnp.where(even, far, near))
+    )
+    turned_last, turned_first = jnp.transpose(lasts[1]), jnp.transpose(firsts[1])
+    turned_third = jnp.transpose(firsts[3])[size:]
+    lasts = [(tile[:, :size], tile[:, size:]) for tile in lasts]
+    firsts = [(tile[:, :size], tile[:, size:]) for tile in firsts]
+    blocks = (
+        lasts[0][0], firsts[0][0], lasts[4][1], lasts[0][1], firsts[0][1], firsts[4][1],
+        lasts[1][0], firsts[1][0], turned_first[:size], turned_first[size:],
+        lasts[4][0], firsts[4][0], lasts[1][1], firsts[1][1], turned_last[:size], turned_third,
+        lasts[3][0], lasts[2][1], lasts[2][0], firsts[2][0], firsts[2][1], firsts[3][0],
+    )
+    for k, block in enumerate(blocks):
+        own[k] = block
 
 
 def second_kernel(
@@ -563,7 +576,7 @@
     loads = 2 + 3 * (size // LOAD) + 3
     (
         rhs, diag, inverse, coupling, prolong, coarse_inverse, aggregate,
-        trial, trial_twice, near, far, own, rows,
+        trial, trial_twice, near, far, rows,
     ) = call(
         first_kernel,
         (
@@ -571,7 +584,7 @@
             shape(size, size, count, kind=BF16),
             shape(*coarse_inverse.shape, kind=BF16),
             shape(1, count, kind=jnp.int32),
-            tile, tile, edge, edge, shape(22, size, size), line,
+            tile, tile, edge, edge, line,
         ),
         [
             plain, half, half, half, plain,
@@ -580,13 +593,13 @@
         rhs, guess, diag_blocks, diag_inverse, coupling, prolong, coarse_inverse, aggregate,
         space=pltpu.HBM,
     )
+    trial_partial, own = call(
+        functools.partial(trial_kernel, group_count), (packed, shape(22, size, size)), [plain],
+        rhs, trial_twice, diag, coupling, prolong, aggregate, near, far,
+        cost=pl.CostEstimate(flops=8 * size**2 * count, bytes_accessed=8 * size**2 * count, transcendentals=0),
+    )
     far = swap(far, 1)
     near = swap(near, 0)
-    trial_partial = call(
-        functools.partial(trial_kernel, group_count), packed, [plain],
-        rhs, trial_twice, diag, coupling, prolong, aggregate,
-        cost=pl.CostEstimate(flops=8 * size**2 * count, bytes_accessed=8 * size**2 * count, transcendentals=0),
-    )
     twice, partial, ghosts = call(
         functools.partial(second_kernel, group_count), (tile, packed, tile), [],
         trial_partial, trial_twice, own, rows, near, far,

time: 44.2 us -> 44.1 us (level)
  no operation moved by 1% of the time
where the time goes in v10:
time: 44.1 us; the launch traced here: 43.9 us
  blocking collectives  27.4 us (62%)
  Pallas kernels  11.5 us (26%)
  starting transfers between devices  3.69 us (8%)
  waiting for transfers between devices  0.7 us (2%)
  between operations  0.67 us (2%)
    all_to_all x1, blocking collectives, local(): shares = lax.all_to_all(partial, 'row', 0, 0, tiled=True)  17.5 us
    pallas_call x5, Pallas kernels, call(): pl.pallas_call(kernel, out_shape=outs, in_specs=[pl.BlockSpec(memory_spac...  11.5 us
    all_to_all x1, blocking collectives, local(): values = lax.all_to_all(corrected, BOTH, 0, 0, tiled=True)  9.91 us
    ppermute x2, starting transfers between devices, swap(): return lax.ppermute(block, BOTH, pairs + [(j, i) for i, j in pairs])  3.69 us
  transfers between devices with their start and end apart: 2, of which 1 were waited for; matrix products, arithmetic and copies ran while one was open for 0% of the time, Pallas kernels for 3%

profile of v10, /device:TPU:0, one launch (start us, length us, event | category | flops | bytes accessed | tf_op | source)
XLA Modules:
  0.0 43.9 jit_solution(17529917770537424896)
XLA Ops:
  0.6 4.8 %shard_map.95 = (f32[64,128]{1,0:T(8,128)S(1)}, f32[64,64,128]{2,1,0:T(8,128)S(1)}, f32[64,64,128]{2,1,0:T(8,128)S(1)}, f32[64,64,128]{2,1,0:T(8,128)S(1)}, bf16...) custom-call(f32[64,128]{1,0:T(8,128)} %rhs_in.1, ...), custom_call_target="tpu_custom_call" | custom-call | tf_op jit(solution)/shard_map/pallas_call | solution.py:547
  5.4 3.0 %collective-permute-start = (bf16[368,128]{1,0:T(8,128)(2,1)S(1)}, bf16[368,128]{1,0:T(8,128)(2,1)S(1)}, u32[]{:S(2)}, u32[]{:S(2)}) collective-permute-start(bf16[368,128]{1,0:T(8,128)(2,1)S(1)} %get-tuple-element.24.near), channel_id=1, source_target_pairs={{0,1},{2,3},{4,5},{6,7},{8,9},{10,11},{12,13},{14,15},{16,17},{18,... | collective-permute-start | bytes 282632 | tf_op jit(solution)/shard_map/ppermute | solution.py:23
  8.5 0.7 %collective-permute-start.1 = (bf16[368,128]{1,0:T(8,128)(2,1)S(1)}, bf16[368,128]{1,0:T(8,128)(2,1)S(1)}, u32[]{:S(2)}, u32[]{:S(2)}) collective-permute-start(bf16[368,128]{1,0:T(8,128)(2,1)S(1)} %get-tuple-element.25.far), channel_id=1, source_target_pairs={{1,2},{3,4},{5,6},{7,8},{9,10},{11,12},{13,14},{15,16},{17,18},{19... | collective-permute-start | bytes 282632 | tf_op jit(solution)/shard_map/ppermute | solution.py:23
  9.1 1.3 %shard_map.96 = (f32[64,128]{1,0:T(8,128)S(1)}, f32[22,64,64]{2,1,0:T(8,128)S(1)}) custom-call(f32[64,128]{1,0:T(8,128)S(1)} %get-tuple-element.18.rhs, f32[64,128]{1,0:T(8,128)S(1)} %get-tuple-element.19.trial_twice, f32[64,64,128]{2,1,0:T(8,128)S(1)} %get-tuple-element.20.diag, f32[64,64,128]{2,1,0:T(8,128)S(1)} %get-tuple-element.21.coupling, ...), custom_call_target="tpu_custom_call" | custom-call | flops 4194304 | bytes 4194304 | tf_op jit(solution)/shard_map/pallas_call | solution.py:547
  10.5 0.7 %collective-permute-done.near = bf16[368,128]{1,0:T(8,128)(2,1)S(1)} collective-permute-done((bf16[368,128]{1,0:T(8,128)(2,1)S(1)}, bf16[368,128]{1,0:T(8,128)(2,1)S(1)}, u32[]{:S(2)}, u32[]{:S(2)}) %collective-permute-start) | collective-permute-done | bytes 94240 | tf_op jit(solution)/shard_map/ppermute | solution.py:23
  11.2 0.0 collective-permute-done.1.far
  11.2 1.0 %shard_map.97 = (f32[64,128]{1,0:T(8,128)S(1)}, f32[64,128]{1,0:T(8,128)S(1)}, f32[64,128]{1,0:T(8,128)S(1)}) custom-call(f32[64,128]{1,0:T(8,128)S(1)} %get-tuple-element.26.trial_partial, f32[64,128]{1,0:T(8,128)S(1)} %get-tuple-element.19.trial_twice, f32[22,64,64]{2,1,0:T(8,128)S(1)} %get-tuple-element.27.own, f32[24,64]{1,0:T(8,128)S(1)} %get-tuple-element.28.rows, ...), custom_call_target="tpu_custom_call" | custom-call | tf_op jit(solution)/shard_map/pallas_call | solution.py:547
  12.2 17.5 %all_to_all.22 = f32[8,8,128]{2,1,0:T(8,128)S(1)} all-to-all(f32[8,8,128]{2,1,0:T(8,128)S(1)} %bitcast.9), channel_id=1, replica_groups=mesh['grp'=4,'row'=8] {'row'}, dimensions={0} | all-to-all | bytes 65536 | tf_op jit(solution)/shard_map/all_to_all | solution.py:607
  29.7 0.3 shard_map.98
  30.1 9.9 %all_to_all.23 = f32[32,8,128]{2,1,0:T(8,128)S(1)} all-to-all(f32[32,8,128]{2,1,0:T(8,128)S(1)} %bitcast.7), channel_id=1, replica_groups=mesh['grp'=4,'row'=8] {'grp','row'}, dimensions={0} | all-to-all | bytes 262144 | tf_op jit(solution)/shard_map/all_to_all | solution.py:611
  40.0 4.0 %shard_map.99 = (f32[64,128]{1,0:T(8,128)}, f32[64,128]{1,0:T(8,128)}) custom-call(f32[64,128]{1,0:T(8,128)S(1)} %get-tuple-element.18.rhs, f32[64,128]{1,0:T(8,128)S(1)} %get-tuple-element.29.twice, f32[256,128]{1,0:T(8,128)S(1)} %bitcast.6, f32[64,64,128]{2,1,0:T(8,128)S(1)} %get-tuple-element.20.diag, f32[64,64,128]{2,1,0:T(8,128)S(1)} %get-tuple-element.32.inverse, ...), custom_call_target="tpu_custom_call" | custom-call | tf_op jit(solution)/shard_map/pallas_call | solution.py:547
Async XLA Ops:
  5.4 5.7 %collective-permute-start = (bf16[368,128]{1,0:T(8,128)(2,1)S(1)}, bf16[368,128]{1,0:T(8,128)(2,1)S(1)}, u32[]{:S(2)}, u32[]{:S(2)}) collective-permute-start(bf16[368,128]{1,0:T(8,128)(2,1)S(1)} %get-tuple-element.24.near), channel_id=1, source_target_pairs={{0,1},{2,3},{4,5},{6,7},{8,9},{10,11},{12,13},{14,15},{16,17},{18,... | collective-permute-start | bytes 282632 | tf_op jit(solution)/shard_map/ppermute | solution.py:23
  8.5 2.7 %collective-permute-start.1 = (bf16[368,128]{1,0:T(8,128)(2,1)S(1)}, bf16[368,128]{1,0:T(8,128)(2,1)S(1)}, u32[]{:S(2)}, u32[]{:S(2)}) collective-permute-start(bf16[368,128]{1,0:T(8,128)(2,1)S(1)} %get-tuple-element.25.far), channel_id=1, source_target_pairs={{1,2},{3,4},{5,6},{7,8},{9,10},{11,12},{13,14},{15,16},{17,18},{19... | collective-permute-start | bytes 282632 | tf_op jit(solution)/shard_map/ppermute | solution.py:23

commit v11 on v10

--- a/solution.py
+++ b/solution.py
@@ -165,8 +165,8 @@
 def first_kernel(
     rhs_in, guess_in, diag_in, inverse_in, coupling_in, prolong_in, coarse_in, aggregate_in,
     rhs, diag, inverse, coupling, prolong, coarse, aggregate,
-    trial, twice, near, far, rows_out,
-    guess, diag_half, inverse_half, coupling_half, work, sems,
+    twice, near, far, rows_out,
+    trial, guess, diag_half, inverse_half, coupling_half, work, sems,
 ):
     size, count = guess.shape
     parts = diag_half.shape[0] // LOAD
@@ -576,7 +576,7 @@
     loads = 2 + 3 * (size // LOAD) + 3
     (
         rhs, diag, inverse, coupling, prolong, coarse_inverse, aggregate,
-        trial, trial_twice, near, far, rows,
+        trial_twice, near, far, rows,
     ) = call(
         first_kernel,
         (
@@ -584,10 +584,10 @@
             shape(size, size, count, kind=BF16),
             shape(*coarse_inverse.shape, kind=BF16),
             shape(1, count, kind=jnp.int32),
-            tile, tile, edge, edge, line,
+            tile, edge, edge, line,
         ),
         [
-            plain, half, half, half, plain,
+            plain, plain, half, half, half, plain,
             pltpu.SemaphoreType.DMA((loads,)),
         ],
         rhs, guess, diag_blocks, diag_inverse, coupling, prolong, coarse_inverse, aggregate,

time: 44.1 us -> 43.7 us (level)
  Pallas kernels: 11.5 us -> 11 us
    pallas_call x5, Pallas kernels: 11.5 us -> 11 us  [call(): pl.pallas_call(kernel, out_shape=outs, in_specs=[pl.BlockSpec(memory_spac...]
where the time goes in v11:
time: 43.7 us; the launch traced here: 43.4 us
  blocking collectives  27.4 us (63%)
  Pallas kernels  11 us (25%)
  starting transfers between devices  3.69 us (8%)
  waiting for transfers between devices  0.7 us (2%)
  between operations  0.67 us (2%)
    all_to_all x1, blocking collectives, local(): shares = lax.all_to_all(partial, 'row', 0, 0, tiled=True)  17.5 us
    pallas_call x5, Pallas kernels, call(): pl.pallas_call(kernel, out_shape=outs, in_specs=[pl.BlockSpec(memory_spac...  11 us
    all_to_all x1, blocking collectives, local(): values = lax.all_to_all(corrected, BOTH, 0, 0, tiled=True)  9.91 us
    ppermute x2, starting transfers between devices, swap(): return lax.ppermute(block, BOTH, pairs + [(j, i) for i, j in pairs])  3.69 us
  transfers between devices with their start and end apart: 2, of which 1 were waited for; matrix products, arithmetic and copies ran while one was open for 0% of the time, Pallas kernels for 3%

profile of v11, /device:TPU:0, one launch (start us, length us, event | category | flops | bytes accessed | tf_op | source)
XLA Modules:
  0.0 43.4 jit_solution(4141162935283563956)
XLA Ops:
  0.6 4.3 %shard_map.95 = (f32[64,128]{1,0:T(8,128)S(1)}, f32[64,64,128]{2,1,0:T(8,128)S(1)}, f32[64,64,128]{2,1,0:T(8,128)S(1)}, f32[64,64,128]{2,1,0:T(8,128)S(1)}, bf16...) custom-call(f32[64,128]{1,0:T(8,128)} %rhs_in.1, ...), custom_call_target="tpu_custom_call" | custom-call | tf_op jit(solution)/shard_map/pallas_call | solution.py:547
  4.9 3.0 %collective-permute-start = (bf16[368,128]{1,0:T(8,128)(2,1)S(1)}, bf16[368,128]{1,0:T(8,128)(2,1)S(1)}, u32[]{:S(2)}, u32[]{:S(2)}) collective-permute-start(bf16[368,128]{1,0:T(8,128)(2,1)S(1)} %get-tuple-element.24.near), channel_id=1, source_target_pairs={{0,1},{2,3},{4,5},{6,7},{8,9},{10,11},{12,13},{14,15},{16,17},{18,... | collective-permute-start | bytes 282632 | tf_op jit(solution)/shard_map/ppermute | solution.py:23
  8.0 0.7 %collective-permute-start.1 = (bf16[368,128]{1,0:T(8,128)(2,1)S(1)}, bf16[368,128]{1,0:T(8,128)(2,1)S(1)}, u32[]{:S(2)}, u32[]{:S(2)}) collective-permute-start(bf16[368,128]{1,0:T(8,128)(2,1)S(1)} %get-tuple-element.25.far), channel_id=1, source_target_pairs={{1,2},{3,4},{5,6},{7,8},{9,10},{11,12},{13,14},{15,16},{17,18},{19... | collective-permute-start | bytes 282632 | tf_op jit(solution)/shard_map/ppermute | solution.py:23
  8.6 1.3 %shard_map.96 = (f32[64,128]{1,0:T(8,128)S(1)}, f32[22,64,64]{2,1,0:T(8,128)S(1)}) custom-call(f32[64,128]{1,0:T(8,128)S(1)} %get-tuple-element.18.rhs, f32[64,128]{1,0:T(8,128)S(1)} %get-tuple-element.19.trial_twice, f32[64,64,128]{2,1,0:T(8,128)S(1)} %get-tuple-element.20.diag, f32[64,64,128]{2,1,0:T(8,128)S(1)} %get-tuple-element.21.coupling, ...), custom_call_target="tpu_custom_call" | custom-call | flops 4194304 | bytes 4194304 | tf_op jit(solution)/shard_map/pallas_call | solution.py:547
  10.0 0.7 %collective-permute-done.near = bf16[368,128]{1,0:T(8,128)(2,1)S(1)} collective-permute-done((bf16[368,128]{1,0:T(8,128)(2,1)S(1)}, bf16[368,128]{1,0:T(8,128)(2,1)S(1)}, u32[]{:S(2)}, u32[]{:S(2)}) %collective-permute-start) | collective-permute-done | bytes 94240 | tf_op jit(solution)/shard_map/ppermute | solution.py:23
  10.7 0.0 collective-permute-done.1.far
  10.7 1.0 %shard_map.97 = (f32[64,128]{1,0:T(8,128)S(1)}, f32[64,128]{1,0:T(8,128)S(1)}, f32[64,128]{1,0:T(8,128)S(1)}) custom-call(f32[64,128]{1,0:T(8,128)S(1)} %get-tuple-element.26.trial_partial, f32[64,128]{1,0:T(8,128)S(1)} %get-tuple-element.19.trial_twice, f32[22,64,64]{2,1,0:T(8,128)S(1)} %get-tuple-element.27.own, f32[24,64]{1,0:T(8,128)S(1)} %get-tuple-element.28.rows, ...), custom_call_target="tpu_custom_call" | custom-call | tf_op jit(solution)/shard_map/pallas_call | solution.py:547
  11.7 17.5 %all_to_all.22 = f32[8,8,128]{2,1,0:T(8,128)S(1)} all-to-all(f32[8,8,128]{2,1,0:T(8,128)S(1)} %bitcast.9), channel_id=1, replica_groups=mesh['grp'=4,'row'=8] {'row'}, dimensions={0} | all-to-all | bytes 65536 | tf_op jit(solution)/shard_map/all_to_all | solution.py:607
  29.2 0.3 shard_map.98
  29.6 9.9 %all_to_all.23 = f32[32,8,128]{2,1,0:T(8,128)S(1)} all-to-all(f32[32,8,128]{2,1,0:T(8,128)S(1)} %bitcast.7), channel_id=1, replica_groups=mesh['grp'=4,'row'=8] {'grp','row'}, dimensions={0} | all-to-all | bytes 262144 | tf_op jit(solution)/shard_map/all_to_all | solution.py:611
  39.5 4.0 %shard_map.99 = (f32[64,128]{1,0:T(8,128)}, f32[64,128]{1,0:T(8,128)}) custom-call(f32[64,128]{1,0:T(8,128)S(1)} %get-tuple-element.18.rhs, f32[64,128]{1,0:T(8,128)S(1)} %get-tuple-element.29.twice, f32[256,128]{1,0:T(8,128)S(1)} %bitcast.6, f32[64,64,128]{2,1,0:T(8,128)S(1)} %get-tuple-element.20.diag, f32[64,64,128]{2,1,0:T(8,128)S(1)} %get-tuple-element.32.inverse, ...), custom_call_target="tpu_custom_call" | custom-call | tf_op jit(solution)/shard_map/pallas_call | solution.py:547
Async XLA Ops:
  4.9 5.7 %collective-permute-start = (bf16[368,128]{1,0:T(8,128)(2,1)S(1)}, bf16[368,128]{1,0:T(8,128)(2,1)S(1)}, u32[]{:S(2)}, u32[]{:S(2)}) collective-permute-start(bf16[368,128]{1,0:T(8,128)(2,1)S(1)} %get-tuple-element.24.near), channel_id=1, source_target_pairs={{0,1},{2,3},{4,5},{6,7},{8,9},{10,11},{12,13},{14,15},{16,17},{18,... | collective-permute-start | bytes 282632 | tf_op jit(solution)/shard_map/ppermute | solution.py:23
  8.0 2.7 %collective-permute-start.1 = (bf16[368,128]{1,0:T(8,128)(2,1)S(1)}, bf16[368,128]{1,0:T(8,128)(2,1)S(1)}, u32[]{:S(2)}, u32[]{:S(2)}) collective-permute-start(bf16[368,128]{1,0:T(8,128)(2,1)S(1)} %get-tuple-element.25.far), channel_id=1, source_target_pairs={{1,2},{3,4},{5,6},{7,8},{9,10},{11,12},{13,14},{15,16},{17,18},{19... | collective-permute-start | bytes 282632 | tf_op jit(solution)/shard_map/ppermute | solution.py:23

commit v12 on v11

--- a/solution.py
+++ b/solution.py
@@ -343,7 +343,7 @@
 
 
 def second_kernel(
-    group_count, trial_partial, trial_twice, own, rows, near, far, twice, partial, ghosts,
+    group_count, trial_partial, trial_twice, own, rows, far, near, twice, partial, ghosts,
 ):
     size, count = trial_twice.shape
     sides, (left, right) = beyond_ends(even_device(), near, far, size)
@@ -602,7 +602,7 @@
     near = swap(near, 0)
     twice, partial, ghosts = call(
         functools.partial(second_kernel, group_count), (tile, packed, tile), [],
-        trial_partial, trial_twice, own, rows, near, far,
+        trial_partial, trial_twice, own, rows, far, near,
     )
     shares = lax.all_to_all(partial, "row", 0, 0, tiled=True)
     corrected = call(

time: 43.7 us -> 43.4 us (level)
  blocking collectives: 27.4 us -> 23.7 us
  starting transfers between devices: 3.69 us -> 6.46 us
  waiting for transfers between devices: 0.7 us -> 1.4 us
    all_to_all x1, blocking collectives: 17.5 us -> 13.2 us  [local(): shares = lax.all_to_all(partial, 'row', 0, 0, tiled=True)]
    ppermute x2, starting transfers between devices: 3.69 us -> 6.46 us  [swap(): return lax.ppermute(block, BOTH, pairs + [(j, i) for i, j in pairs])]
    ppermute x2, waiting for transfers between devices: 0.7 us -> 1.4 us  [swap(): return lax.ppermute(block, BOTH, pairs + [(j, i) for i, j in pairs])]
    all_to_all x1, blocking collectives: 9.91 us -> 10.5 us  [local(): values = lax.all_to_all(corrected, BOTH, 0, 0, tiled=True)]
where the time goes in v12:
time: 43.4 us; the launch traced here: 43.2 us
  blocking collectives  23.7 us (55%)
  Pallas kernels  11 us (25%)
  starting transfers between devices  6.46 us (15%)
  waiting for transfers between devices  1.4 us (3%)
  between operations  0.67 us (2%)
    all_to_all x1, blocking collectives, local(): shares = lax.all_to_all(partial, 'row', 0, 0, tiled=True)  13.2 us
    pallas_call x5, Pallas kernels, call(): pl.pallas_call(kernel, out_shape=outs, in_specs=[pl.BlockSpec(memory_spac...  11 us
    all_to_all x1, blocking collectives, local(): values = lax.all_to_all(corrected, BOTH, 0, 0, tiled=True)  10.5 us
    ppermute x2, starting transfers between devices, swap(): return lax.ppermute(block, BOTH, pairs + [(j, i) for i, j in pairs])  6.46 us
    ppermute x2, waiting for transfers between devices, swap(): return lax.ppermute(block, BOTH, pairs + [(j, i) for i, j in pairs])  1.4 us
  transfers between devices with their start and end apart: 2, of which 1 were waited for; matrix products, arithmetic and copies ran while one was open for 0% of the time, Pallas kernels for 3%

profile of v12, /device:TPU:0, one launch (start us, length us, event | category | flops | bytes accessed | tf_op | source)
XLA Modules:
  0.0 43.2 jit_solution(3092687631109795084)
XLA Ops:
  0.6 4.3 %shard_map.95 = (f32[64,128]{1,0:T(8,128)S(1)}, f32[64,64,128]{2,1,0:T(8,128)S(1)}, f32[64,64,128]{2,1,0:T(8,128)S(1)}, f32[64,64,128]{2,1,0:T(8,128)S(1)}, bf16...) custom-call(f32[64,128]{1,0:T(8,128)} %rhs_in.1, ...), custom_call_target="tpu_custom_call" | custom-call | tf_op jit(solution)/shard_map/pallas_call | solution.py:547
  4.9 0.7 %collective-permute-start = (bf16[368,128]{1,0:T(8,128)(2,1)S(1)}, bf16[368,128]{1,0:T(8,128)(2,1)S(1)}, u32[]{:S(2)}, u32[]{:S(2)}) collective-permute-start(bf16[368,128]{1,0:T(8,128)(2,1)S(1)} %get-tuple-element.25.far), channel_id=1, source_target_pairs={{1,2},{3,4},{5,6},{7,8},{9,10},{11,12},{13,14},{15,16},{17,18},{19... | collective-permute-start | bytes 282632 | tf_op jit(solution)/shard_map/ppermute | solution.py:23
  5.6 5.8 %collective-permute-start.1 = (bf16[368,128]{1,0:T(8,128)(2,1)S(1)}, bf16[368,128]{1,0:T(8,128)(2,1)S(1)}, u32[]{:S(2)}, u32[]{:S(2)}) collective-permute-start(bf16[368,128]{1,0:T(8,128)(2,1)S(1)} %get-tuple-element.24.near), channel_id=1, source_target_pairs={{0,1},{2,3},{4,5},{6,7},{8,9},{10,11},{12,13},{14,15},{16,17},{18,... | collective-permute-start | bytes 282632 | tf_op jit(solution)/shard_map/ppermute | solution.py:23
  11.4 1.3 %shard_map.96 = (f32[64,128]{1,0:T(8,128)S(1)}, f32[22,64,64]{2,1,0:T(8,128)S(1)}) custom-call(f32[64,128]{1,0:T(8,128)S(1)} %get-tuple-element.18.rhs, f32[64,128]{1,0:T(8,128)S(1)} %get-tuple-element.19.trial_twice, f32[64,64,128]{2,1,0:T(8,128)S(1)} %get-tuple-element.20.diag, f32[64,64,128]{2,1,0:T(8,128)S(1)} %get-tuple-element.21.coupling, ...), custom_call_target="tpu_custom_call" | custom-call | flops 4194304 | bytes 4194304 | tf_op jit(solution)/shard_map/pallas_call | solution.py:547
  12.8 0.0 collective-permute-done.far
  12.8 1.4 %collective-permute-done.1.near = bf16[368,128]{1,0:T(8,128)(2,1)S(1)} collective-permute-done((bf16[368,128]{1,0:T(8,128)(2,1)S(1)}, bf16[368,128]{1,0:T(8,128)(2,1)S(1)}, u32[]{:S(2)}, u32[]{:S(2)}) %collective-permute-start.1) | collective-permute-done | bytes 94240 | tf_op jit(solution)/shard_map/ppermute | solution.py:23
  14.2 1.0 %shard_map.97 = (f32[64,128]{1,0:T(8,128)S(1)}, f32[64,128]{1,0:T(8,128)S(1)}, f32[64,128]{1,0:T(8,128)S(1)}) custom-call(f32[64,128]{1,0:T(8,128)S(1)} %get-tuple-element.26.trial_partial, f32[64,128]{1,0:T(8,128)S(1)} %get-tuple-element.19.trial_twice, f32[22,64,64]{2,1,0:T(8,128)S(1)} %get-tuple-element.27.own, f32[24,64]{1,0:T(8,128)S(1)} %get-tuple-element.28.rows, ...), custom_call_target="tpu_custom_call" | custom-call | tf_op jit(solution)/shard_map/pallas_call | solution.py:547
  15.2 13.2 %all_to_all.22 = f32[8,8,128]{2,1,0:T(8,128)S(1)} all-to-all(f32[8,8,128]{2,1,0:T(8,128)S(1)} %bitcast.9), channel_id=1, replica_groups=mesh['grp'=4,'row'=8] {'row'}, dimensions={0} | all-to-all | bytes 65536 | tf_op jit(solution)/shard_map/all_to_all | solution.py:607
  28.4 0.3 shard_map.98
  28.7 10.5 %all_to_all.23 = f32[32,8,128]{2,1,0:T(8,128)S(1)} all-to-all(f32[32,8,128]{2,1,0:T(8,128)S(1)} %bitcast.7), channel_id=1, replica_groups=mesh['grp'=4,'row'=8] {'grp','row'}, dimensions={0} | all-to-all | bytes 262144 | tf_op jit(solution)/shard_map/all_to_all | solution.py:611
  39.2 4.0 %shard_map.99 = (f32[64,128]{1,0:T(8,128)}, f32[64,128]{1,0:T(8,128)}) custom-call(f32[64,128]{1,0:T(8,128)S(1)} %get-tuple-element.18.rhs, f32[64,128]{1,0:T(8,128)S(1)} %get-tuple-element.29.twice, f32[256,128]{1,0:T(8,128)S(1)} %bitcast.6, f32[64,64,128]{2,1,0:T(8,128)S(1)} %get-tuple-element.20.diag, f32[64,64,128]{2,1,0:T(8,128)S(1)} %get-tuple-element.32.inverse, ...), custom_call_target="tpu_custom_call" | custom-call | tf_op jit(solution)/shard_map/pallas_call | solution.py:547
Async XLA Ops:
  4.9 7.8 %collective-permute-start = (bf16[368,128]{1,0:T(8,128)(2,1)S(1)}, bf16[368,128]{1,0:T(8,128)(2,1)S(1)}, u32[]{:S(2)}, u32[]{:S(2)}) collective-permute-start(bf16[368,128]{1,0:T(8,128)(2,1)S(1)} %get-tuple-element.25.far), channel_id=1, source_target_pairs={{1,2},{3,4},{5,6},{7,8},{9,10},{11,12},{13,14},{15,16},{17,18},{19... | collective-permute-start | bytes 282632 | tf_op jit(solution)/shard_map/ppermute | solution.py:23
  5.6 8.6 %collective-permute-start.1 = (bf16[368,128]{1,0:T(8,128)(2,1)S(1)}, bf16[368,128]{1,0:T(8,128)(2,1)S(1)}, u32[]{:S(2)}, u32[]{:S(2)}) collective-permute-start(bf16[368,128]{1,0:T(8,128)(2,1)S(1)} %get-tuple-element.24.near), channel_id=1, source_target_pairs={{0,1},{2,3},{4,5},{6,7},{8,9},{10,11},{12,13},{14,15},{16,17},{18,... | collective-permute-start | bytes 282632 | tf_op jit(solution)/shard_map/ppermute | solution.py:23

commit v13 on v12

--- a/solution.py
+++ b/solution.py
@@ -115,7 +115,7 @@
     shape = (tile.shape[0] // ROWS, ROWS, tile.shape[1])
     lane = lax.broadcasted_iota(jnp.int32, (1,) + shape[1:], 2)
     mine = lax.shift_right_logical(lane, 3) == row
-    turned = pltpu.roll(block, 8 * row + 3, 1).reshape(shape)
+    turned = pltpu.roll(block, 8 * row + 4, 1).reshape(shape)
     return jnp.where(mine, turned, tile.reshape(shape)).reshape(tile.shape)
 
 
@@ -165,8 +165,8 @@
 def first_kernel(
     rhs_in, guess_in, diag_in, inverse_in, coupling_in, prolong_in, coarse_in, aggregate_in,
     rhs, diag, inverse, coupling, prolong, coarse, aggregate,
-    twice, near, far, rows_out,
-    trial, guess, diag_half, inverse_half, coupling_half, work, sems,
+    trial, near, far, rows_out,
+    guess, diag_half, inverse_half, coupling_half, work, sems,
 ):
     size, count = guess.shape
     parts = diag_half.shape[0] // LOAD
@@ -210,6 +210,7 @@
             diag[i] = block
             t, row = divmod(i, size // 4)
             diag_ends[t] = place(diag_ends[t], block, row)
+            coupling_ends[t] = place(coupling_ends[t], pair, row)
             sums.append(jnp.sum(block * start + pair * lower, axis=0, keepdims=True))
             upward = upward + pair * guess[i : i + 1, :]
         work[pl.ds(chunk * ROWS, ROWS), :] = jnp.concatenate(sums, axis=0)
@@ -230,51 +231,57 @@
             sums.append(jnp.sum(block * defect, axis=0, keepdims=True))
         trial[rows, :] = guess[rows, :] + jnp.concatenate(sums, axis=0)
 
-    second = trial[...]
-    lower = jnp.where(lane == 0, 0.0, turn(second, 1))
-    upward = jnp.zeros_like(start)
-    for chunk in range(size // ROWS):
-        sums = []
-        for i in range(chunk * ROWS, chunk * ROWS + ROWS):
-            pair = coupling[i]
-            t, row = divmod(i, size // 4)
-            coupling_ends[t] = place(coupling_ends[t], pair, row)
-            sums.append(jnp.sum(diag[i] * second + pair * lower, axis=0, keepdims=True))
-            upward = upward + pair * trial[i : i + 1, :]
-        work[pl.ds(chunk * ROWS, ROWS), :] = jnp.concatenate(sums, axis=0)
-    upper = jnp.where(lane == count - 1, 0.0, turn(upward, -1))
-    defect = rhs[...] - (work[...] + upper)
-
     for copy in copies[-3:]:
         copy.wait()
-    for chunk in range(size // ROWS):
-        rows = pl.ds(chunk * ROWS, ROWS)
-        sums = []
-        for i in range(chunk * ROWS, chunk * ROWS + ROWS):
-            t, row = divmod(i, size // 4)
-            prolong_ends[t] = place(prolong_ends[t], prolong[i].astype(F32), row)
-            sums.append(jnp.sum(inverse[i] * defect, axis=0, keepdims=True))
-        twice[rows, :] = trial[rows, :] + jnp.concatenate(sums, axis=0)
-
+    for i in range(size):
+        t, row = divmod(i, size // 4)
+        prolong_ends[t] = place(prolong_ends[t], prolong[i].astype(F32), row)
+    diag_turned = end_blocks_turned(diag_ends, (1, 2, 3, 4, 5, 6))
+    coupling_turned = end_blocks_turned(coupling_ends, (1, 2, 3, 4, 5, 6))
+    inverses = end_blocks(inverse_ends, (1, 2, 3, 4, 5, 6))
+    couplings = end_blocks(coupling_ends, (2, 3, 4, 5, 6, 7))
+    prolongs = end_blocks(prolong_ends, (1, 2, 3, 4, 5, 6))
+    turned_diag = [diag_turned[:, k * size : (k + 1) * size] for k in range(6)]
+    turned = [coupling_turned[:, k * size : (k + 1) * size] for k in range(6)]
+
+    second = trial[...]
     last = count - 1
     named = jnp.broadcast_to(aggregate[...].astype(F32), (size, count))
-    after = twice[...]
-    both = [(start, 0), (second, 0), (defect, 0), (after, 1), (after, 2), (rhs[...], 0), (rhs[...], 1)]
-    both = both + [(named, 0), (named, 1), (named, 2)]
-    rows = edge_rows(both, [(column, last - k) for column, k in both], count)
+    both = [(start, 0)] + [(second, k) for k in range(3)] + [(rhs[...], k) for k in range(3)]
+    both = both + [(named, k) for k in range(3)]
+    known = edge_rows(both, [(column, last - k) for column, k in both], count)
+    shape = (size, size)
+    unit = lax.broadcasted_iota(jnp.int32, shape, 0) == lax.broadcasted_iota(jnp.int32, shape, 1)
+    defects, after = [], []
+    for k in range(6):
+        own_row = (k - 3) if k > 2 else EDGE_ROWS + (2 - k)
+        lane_of = (k - 3) if k > 2 else last - (2 - k)
+        total = to_row(turned_diag[k], trial[:, lane_of : lane_of + 1])
+        if k != 3:
+            total = total + to_row(turned[k], trial[:, lane_of - 1 : lane_of])
+        if k != 2:
+            total = total + to_row(couplings[k], trial[:, lane_of + 1 : lane_of + 2])
+        defect_row = known[own_row + 4 : own_row + 5] - total
+        step = to_column(inverses[k], defect_row)
+        step = jnp.sum(jnp.where(unit, step, 0.0), axis=0, keepdims=True)
+        defects.append(defect_row)
+        after.append(known[own_row + 1 : own_row + 2] + step)
+    rows = []
+    for base, nearest, next_one, third in ((0, 3, 4, 5), (EDGE_ROWS, 2, 1, 0)):
+        rows = rows + [
+            known[base : base + 2], defects[nearest], after[next_one], after[third],
+            known[base + 4 : base + 6], known[base + 7 : base + 10],
+        ]
+    rows = rows + [jnp.zeros((EDGES - 2 * EDGE_ROWS, size), F32)]
+    rows = jnp.concatenate(rows, axis=0)
     rows_out[...] = rows
-    diag_turned = end_blocks_turned(diag_ends, (1, 2, 3, 4))
-    inverses = end_blocks(inverse_ends, (1, 2, 3, 4))
-    couplings = end_blocks(coupling_ends, (1, 2, 3, 4, 5))
-    prolongs = end_blocks(prolong_ends, (0, 1, 2, 3, 4, 5))
-    turned_diag = [diag_turned[:, k * size : (k + 1) * size] for k in range(4)]
     lasts = (
-        (turned_diag[1], inverses[1]), (couplings[1], couplings[0]), (prolongs[2], prolongs[1]),
-        (prolongs[0], couplings[4]), (turned_diag[0], inverses[0]),
+        (turned_diag[2], inverses[2]), (couplings[1], couplings[0]), (prolongs[2], prolongs[1]),
+        (prolongs[0], couplings[4]), (turned_diag[1], inverses[1]),
     )
     firsts = (
-        (turned_diag[2], inverses[2]), (couplings[2], couplings[3]), (prolongs[3], prolongs[4]),
-        (prolongs[5], couplings[4]), (turned_diag[3], inverses[3]),
+        (turned_diag[3], inverses[3]), (couplings[2], couplings[3]), (prolongs[3], prolongs[4]),
+        (prolongs[5], couplings[4]), (turned_diag[4], inverses[4]),
     )
     even = even_device()
     for k, (one, other) in enumerate(zip(lasts, firsts)):
@@ -311,9 +318,10 @@
 
 
 def trial_kernel(
-    group_count, rhs, trial_twice, diag, coupling, prolong, aggregate, near, far,
-    partial, own, work,
+    group_count, rhs, trial, diag, inverse, coupling, prolong, aggregate, near, far,
+    trial_twice, partial, own, work,
 ):
+    apply_blocks(inverse, wrong(rhs, trial, diag, coupling, work), trial, trial_twice)
     work[...] = wrong(rhs, trial_twice, diag, coupling, work)
     pieces = apply_transposed(prolong, work)
     picked = [chosen(aggregate, group_count, half) for half in (0, 1)]
@@ -576,7 +584,7 @@
     loads = 2 + 3 * (size // LOAD) + 3
     (
         rhs, diag, inverse, coupling, prolong, coarse_inverse, aggregate,
-        trial_twice, near, far, rows,
+        trial, near, far, rows,
     ) = call(
         first_kernel,
         (
@@ -587,15 +595,15 @@
             tile, edge, edge, line,
         ),
         [
-            plain, plain, half, half, half, plain,
+            plain, half, half, half, plain,
             pltpu.SemaphoreType.DMA((loads,)),
         ],
         rhs, guess, diag_blocks, diag_inverse, coupling, prolong, coarse_inverse, aggregate,
         space=pltpu.HBM,
     )
-    trial_partial, own = call(
-        functools.partial(trial_kernel, group_count), (packed, shape(22, size, size)), [plain],
-        rhs, trial_twice, diag, coupling, prolong, aggregate, near, far,
+    trial_twice, trial_partial, own = call(
+        functools.partial(trial_kernel, group_count), (tile, packed, shape(22, size, size)), [plain],
+        rhs, trial, diag, inverse, coupling, prolong, aggregate, near, far,
         cost=pl.CostEstimate(flops=8 * size**2 * count, bytes_accessed=8 * size**2 * count, transcendentals=0),
     )
     far = swap(far, 1)

time: 43.4 us -> 43.2 us (level)
  waiting for transfers between devices: 1.4 us -> 0.37 us
  Pallas kernels: 11 us -> 11.8 us
    ppermute x2, waiting for transfers between devices: 1.4 us -> 0.37 us  [swap(): return lax.ppermute(block, BOTH, pairs + [(j, i) for i, j in pairs])]
    pallas_call x5, Pallas kernels: 11 us -> 11.8 us  [call(): pl.pallas_call(kernel, out_shape=outs, in_specs=[pl.BlockSpec(memory_spac...]
  transfers between devices with their start and end apart: 2 -> 2, of which waited for: 1 -> 1; matrix products, arithmetic and copies ran while one was open for 0% -> 0% of each run, Pallas kernels for 3% -> 6%
where the time goes in v13:
time: 43.2 us; the launch traced here: 43 us
  blocking collectives  23.7 us (55%)
  Pallas kernels  11.8 us (27%)
  starting transfers between devices  6.46 us (15%)
  between operations  0.67 us (2%)
    all_to_all x1, blocking collectives, local(): shares = lax.all_to_all(partial, 'row', 0, 0, tiled=True)  13.2 us
    pallas_call x5, Pallas kernels, call(): pl.pallas_call(kernel, out_shape=outs, in_specs=[pl.BlockSpec(memory_spac...  11.8 us
    all_to_all x1, blocking collectives, local(): values = lax.all_to_all(corrected, BOTH, 0, 0, tiled=True)  10.5 us
    ppermute x2, starting transfers between devices, swap(): return lax.ppermute(block, BOTH, pairs + [(j, i) for i, j in pairs])  6.46 us
  transfers between devices with their start and end apart: 2, of which 1 were waited for; matrix products, arithmetic and copies ran while one was open for 0% of the time, Pallas kernels for 6%

profile of v13, /device:TPU:0, one launch (start us, length us, event | category | flops | bytes accessed | tf_op | source)
XLA Modules:
  0.0 43.0 jit_solution(10322531743896246171)
XLA Ops:
  0.6 4.0 %shard_map.95 = (f32[64,128]{1,0:T(8,128)S(1)}, f32[64,64,128]{2,1,0:T(8,128)S(1)}, f32[64,64,128]{2,1,0:T(8,128)S(1)}, f32[64,64,128]{2,1,0:T(8,128)S(1)}, bf16...) custom-call(f32[64,128]{1,0:T(8,128)} %rhs_in.1, ...), custom_call_target="tpu_custom_call" | custom-call | tf_op jit(solution)/shard_map/pallas_call | solution.py:555
  4.7 0.7 %collective-permute-start = (bf16[368,128]{1,0:T(8,128)(2,1)S(1)}, bf16[368,128]{1,0:T(8,128)(2,1)S(1)}, u32[]{:S(2)}, u32[]{:S(2)}) collective-permute-start(bf16[368,128]{1,0:T(8,128)(2,1)S(1)} %get-tuple-element.27.far), channel_id=1, source_target_pairs={{1,2},{3,4},{5,6},{7,8},{9,10},{11,12},{13,14},{15,16},{17,18},{19... | collective-permute-start | bytes 282632 | tf_op jit(solution)/shard_map/ppermute | solution.py:23
  5.4 5.8 %collective-permute-start.1 = (bf16[368,128]{1,0:T(8,128)(2,1)S(1)}, bf16[368,128]{1,0:T(8,128)(2,1)S(1)}, u32[]{:S(2)}, u32[]{:S(2)}) collective-permute-start(bf16[368,128]{1,0:T(8,128)(2,1)S(1)} %get-tuple-element.26.near), channel_id=1, source_target_pairs={{0,1},{2,3},{4,5},{6,7},{8,9},{10,11},{12,13},{14,15},{16,17},{18,... | collective-permute-start | bytes 282632 | tf_op jit(solution)/shard_map/ppermute | solution.py:23
  11.2 2.4 %shard_map.96 = (f32[64,128]{1,0:T(8,128)S(1)}, f32[64,128]{1,0:T(8,128)S(1)}, f32[22,64,64]{2,1,0:T(8,128)S(1)}) custom-call(f32[64,128]{1,0:T(8,128)S(1)} %get-tuple-element.19.rhs, f32[64,128]{1,0:T(8,128)S(1)} %get-tuple-element.20.trial, f32[64,64,128]{2,1,0:T(8,128)S(1)} %get-tuple-element.21.diag, f32[64,64,128]{2,1,0:T(8,128)S(1)} %get-tuple-element.22.inverse, ...), custom_call_target="tpu_custom_call" | custom-call | flops 4194304 | bytes 4194304 | tf_op jit(solution)/shard_map/pallas_call | solution.py:555
  13.5 0.0 collective-permute-done.far
  13.5 0.4 collective-permute-done.1.near
  13.9 1.0 %shard_map.97 = (f32[64,128]{1,0:T(8,128)S(1)}, f32[64,128]{1,0:T(8,128)S(1)}, f32[64,128]{1,0:T(8,128)S(1)}) custom-call(f32[64,128]{1,0:T(8,128)S(1)} %get-tuple-element.28.trial_partial, f32[64,128]{1,0:T(8,128)S(1)} %get-tuple-element.29.trial_twice, f32[22,64,64]{2,1,0:T(8,128)S(1)} %get-tuple-element.30.own, f32[24,64]{1,0:T(8,128)S(1)} %get-tuple-element.31.rows, ...), custom_call_target="tpu_custom_call" | custom-call | tf_op jit(solution)/shard_map/pallas_call | solution.py:555
  15.0 13.2 %all_to_all.22 = f32[8,8,128]{2,1,0:T(8,128)S(1)} all-to-all(f32[8,8,128]{2,1,0:T(8,128)S(1)} %bitcast.9), channel_id=1, replica_groups=mesh['grp'=4,'row'=8] {'row'}, dimensions={0} | all-to-all | bytes 65536 | tf_op jit(solution)/shard_map/all_to_all | solution.py:615
  28.2 0.3 shard_map.98
  28.5 10.5 %all_to_all.23 = f32[32,8,128]{2,1,0:T(8,128)S(1)} all-to-all(f32[32,8,128]{2,1,0:T(8,128)S(1)} %bitcast.7), channel_id=1, replica_groups=mesh['grp'=4,'row'=8] {'grp','row'}, dimensions={0} | all-to-all | bytes 262144 | tf_op jit(solution)/shard_map/all_to_all | solution.py:619
  38.9 4.0 %shard_map.99 = (f32[64,128]{1,0:T(8,128)}, f32[64,128]{1,0:T(8,128)}) custom-call(f32[64,128]{1,0:T(8,128)S(1)} %get-tuple-element.19.rhs, f32[64,128]{1,0:T(8,128)S(1)} %get-tuple-element.32.twice, f32[256,128]{1,0:T(8,128)S(1)} %bitcast.6, f32[64,64,128]{2,1,0:T(8,128)S(1)} %get-tuple-element.21.diag, f32[64,64,128]{2,1,0:T(8,128)S(1)} %get-tuple-element.22.inverse, ...), custom_call_target="tpu_custom_call" | custom-call | tf_op jit(solution)/shard_map/pallas_call | solution.py:555
Async XLA Ops:
  4.7 8.9 %collective-permute-start = (bf16[368,128]{1,0:T(8,128)(2,1)S(1)}, bf16[368,128]{1,0:T(8,128)(2,1)S(1)}, u32[]{:S(2)}, u32[]{:S(2)}) collective-permute-start(bf16[368,128]{1,0:T(8,128)(2,1)S(1)} %get-tuple-element.27.far), channel_id=1, source_target_pairs={{1,2},{3,4},{5,6},{7,8},{9,10},{11,12},{13,14},{15,16},{17,18},{19... | collective-permute-start | bytes 282632 | tf_op jit(solution)/shard_map/ppermute | solution.py:23
  5.4 8.6 %collective-permute-start.1 = (bf16[368,128]{1,0:T(8,128)(2,1)S(1)}, bf16[368,128]{1,0:T(8,128)(2,1)S(1)}, u32[]{:S(2)}, u32[]{:S(2)}) collective-permute-start(bf16[368,128]{1,0:T(8,128)(2,1)S(1)} %get-tuple-element.26.near), channel_id=1, source_target_pairs={{0,1},{2,3},{4,5},{6,7},{8,9},{10,11},{12,13},{14,15},{16,17},{18,... | collective-permute-start | bytes 282632 | tf_op jit(solution)/shard_map/ppermute | solution.py:23

commit v14 on v13

--- a/solution.py
+++ b/solution.py
@@ -319,7 +319,7 @@
 
 def trial_kernel(
     group_count, rhs, trial, diag, inverse, coupling, prolong, aggregate, near, far,
-    trial_twice, partial, own, work,
+    trial_twice, partial, own, wide, work,
 ):
     apply_blocks(inverse, wrong(rhs, trial, diag, coupling, work), trial, trial_twice)
     work[...] = wrong(rhs, trial_twice, diag, coupling, work)
@@ -348,6 +348,8 @@
     )
     for k, block in enumerate(blocks):
         own[k] = block
+    for i in range(size):
+        wide[i] = prolong[i].astype(F32)
 
 
 def second_kernel(
@@ -601,8 +603,8 @@
         rhs, guess, diag_blocks, diag_inverse, coupling, prolong, coarse_inverse, aggregate,
         space=pltpu.HBM,
     )
-    trial_twice, trial_partial, own = call(
-        functools.partial(trial_kernel, group_count), (tile, packed, shape(22, size, size)), [plain],
+    trial_twice, trial_partial, own, wide = call(
+        functools.partial(trial_kernel, group_count), (tile, packed, shape(22, size, size), blocks), [plain],
         rhs, trial, diag, inverse, coupling, prolong, aggregate, near, far,
         cost=pl.CostEstimate(flops=8 * size**2 * count, bytes_accessed=8 * size**2 * count, transcendentals=0),
     )
@@ -619,7 +621,7 @@
     values = lax.all_to_all(corrected, BOTH, 0, 0, tiled=True)
     return call(
         functools.partial(third_kernel, group_count), (tile, tile), [plain, plain, plain],
-        rhs, twice, values, diag, inverse, coupling, own, near, far, ghosts, prolong, aggregate,
+        rhs, twice, values, diag, inverse, coupling, own, near, far, ghosts, wide, aggregate,
     )
 
 

time: 43.2 us -> 43.1 us (level)
  no operation moved by 1% of the time
where the time goes in v14:
time: 43.1 us; the launch traced here: 42.9 us
  blocking collectives  23.7 us (55%)
  Pallas kernels  11.8 us (27%)
  starting transfers between devices  6.46 us (15%)
  between operations  0.67 us (2%)
    all_to_all x1, blocking collectives, local(): shares = lax.all_to_all(partial, 'row', 0, 0, tiled=True)  13.2 us
    pallas_call x5, Pallas kernels, call(): pl.pallas_call(kernel, out_shape=outs, in_specs=[pl.BlockSpec(memory_spac...  11.8 us
    all_to_all x1, blocking collectives, local(): values = lax.all_to_all(corrected, BOTH, 0, 0, tiled=True)  10.5 us
    ppermute x2, starting transfers between devices, swap(): return lax.ppermute(block, BOTH, pairs + [(j, i) for i, j in pairs])  6.46 us
  transfers between devices with their start and end apart: 2, of which 1 were waited for; matrix products, arithmetic and copies ran while one was open for 0% of the time, Pallas kernels for 6%

profile of v14, /device:TPU:0, one launch (start us, length us, event | category | flops | bytes accessed | tf_op | source)
XLA Modules:
  0.0 42.9 jit_solution(14690656426619402388)
XLA Ops:
  0.6 4.0 %shard_map.95 = (f32[64,128]{1,0:T(8,128)S(1)}, f32[64,64,128]{2,1,0:T(8,128)S(1)}, f32[64,64,128]{2,1,0:T(8,128)S(1)}, f32[64,64,128]{2,1,0:T(8,128)S(1)}, bf16...) custom-call(f32[64,128]{1,0:T(8,128)} %rhs_in.1, ...), custom_call_target="tpu_custom_call" | custom-call | tf_op jit(solution)/shard_map/pallas_call | solution.py:557
  4.7 0.7 %collective-permute-start = (bf16[368,128]{1,0:T(8,128)(2,1)S(1)}, bf16[368,128]{1,0:T(8,128)(2,1)S(1)}, u32[]{:S(2)}, u32[]{:S(2)}) collective-permute-start(bf16[368,128]{1,0:T(8,128)(2,1)S(1)} %get-tuple-element.28.far), channel_id=1, source_target_pairs={{1,2},{3,4},{5,6},{7,8},{9,10},{11,12},{13,14},{15,16},{17,18},{19... | collective-permute-start | bytes 282632 | tf_op jit(solution)/shard_map/ppermute | solution.py:23
  5.3 5.8 %collective-permute-start.1 = (bf16[368,128]{1,0:T(8,128)(2,1)S(1)}, bf16[368,128]{1,0:T(8,128)(2,1)S(1)}, u32[]{:S(2)}, u32[]{:S(2)}) collective-permute-start(bf16[368,128]{1,0:T(8,128)(2,1)S(1)} %get-tuple-element.27.near), channel_id=1, source_target_pairs={{0,1},{2,3},{4,5},{6,7},{8,9},{10,11},{12,13},{14,15},{16,17},{18,... | collective-permute-start | bytes 282632 | tf_op jit(solution)/shard_map/ppermute | solution.py:23
  11.1 2.4 %shard_map.96 = (f32[64,128]{1,0:T(8,128)S(1)}, f32[64,128]{1,0:T(8,128)S(1)}, f32[22,64,64]{2,1,0:T(8,128)S(1)}, f32[64,64,128]{2,1,0:T(8,128)S(1)}) custom-call(f32[64,128]{1,0:T(8,128)S(1)} %get-tuple-element.20.rhs, f32[64,128]{1,0:T(8,128)S(1)} %get-tuple-element.21.trial, f32[64,64,128]{2,1,0:T(8,128)S(1)} %get-tuple-element.22.diag, ...), custom_call_target="tpu_custom_call" | custom-call | flops 4194304 | bytes 4194304 | tf_op jit(solution)/shard_map/pallas_call | solution.py:557
  13.6 0.0 collective-permute-done.far
  13.6 0.3 collective-permute-done.1.near
  13.9 1.0 %shard_map.97 = (f32[64,128]{1,0:T(8,128)S(1)}, f32[64,128]{1,0:T(8,128)S(1)}, f32[64,128]{1,0:T(8,128)S(1)}) custom-call(f32[64,128]{1,0:T(8,128)S(1)} %get-tuple-element.29.trial_partial, f32[64,128]{1,0:T(8,128)S(1)} %get-tuple-element.30.trial_twice, f32[22,64,64]{2,1,0:T(8,128)S(1)} %get-tuple-element.31.own, f32[24,64]{1,0:T(8,128)S(1)} %get-tuple-element.32.rows, ...), custom_call_target="tpu_custom_call" | custom-call | tf_op jit(solution)/shard_map/pallas_call | solution.py:557
  15.0 13.2 %all_to_all.22 = f32[8,8,128]{2,1,0:T(8,128)S(1)} all-to-all(f32[8,8,128]{2,1,0:T(8,128)S(1)} %bitcast.9), channel_id=1, replica_groups=mesh['grp'=4,'row'=8] {'row'}, dimensions={0} | all-to-all | bytes 65536 | tf_op jit(solution)/shard_map/all_to_all | solution.py:617
  28.1 0.3 shard_map.98
  28.5 10.5 %all_to_all.23 = f32[32,8,128]{2,1,0:T(8,128)S(1)} all-to-all(f32[32,8,128]{2,1,0:T(8,128)S(1)} %bitcast.7), channel_id=1, replica_groups=mesh['grp'=4,'row'=8] {'grp','row'}, dimensions={0} | all-to-all | bytes 262144 | tf_op jit(solution)/shard_map/all_to_all | solution.py:621
  38.9 4.0 %shard_map.99 = (f32[64,128]{1,0:T(8,128)}, f32[64,128]{1,0:T(8,128)}) custom-call(f32[64,128]{1,0:T(8,128)S(1)} %get-tuple-element.20.rhs, f32[64,128]{1,0:T(8,128)S(1)} %get-tuple-element.33.twice, f32[256,128]{1,0:T(8,128)S(1)} %bitcast.6, f32[64,64,128]{2,1,0:T(8,128)S(1)} %get-tuple-element.22.diag, f32[64,64,128]{2,1,0:T(8,128)S(1)} %get-tuple-element.23.inverse, ...), custom_call_target="tpu_custom_call" | custom-call | tf_op jit(solution)/shard_map/pallas_call | solution.py:557
Async XLA Ops:
  4.7 8.9 %collective-permute-start = (bf16[368,128]{1,0:T(8,128)(2,1)S(1)}, bf16[368,128]{1,0:T(8,128)(2,1)S(1)}, u32[]{:S(2)}, u32[]{:S(2)}) collective-permute-start(bf16[368,128]{1,0:T(8,128)(2,1)S(1)} %get-tuple-element.28.far), channel_id=1, source_target_pairs={{1,2},{3,4},{5,6},{7,8},{9,10},{11,12},{13,14},{15,16},{17,18},{19... | collective-permute-start | bytes 282632 | tf_op jit(solution)/shard_map/ppermute | solution.py:23
  5.3 8.6 %collective-permute-start.1 = (bf16[368,128]{1,0:T(8,128)(2,1)S(1)}, bf16[368,128]{1,0:T(8,128)(2,1)S(1)}, u32[]{:S(2)}, u32[]{:S(2)}) collective-permute-start(bf16[368,128]{1,0:T(8,128)(2,1)S(1)} %get-tuple-element.27.near), channel_id=1, source_target_pairs={{0,1},{2,3},{4,5},{6,7},{8,9},{10,11},{12,13},{14,15},{16,17},{18,... | collective-permute-start | bytes 282632 | tf_op jit(solution)/shard_map/ppermute | solution.py:23

commit v15 on v13

--- a/solution.py
+++ b/solution.py
@@ -12,7 +12,7 @@
 F32 = jnp.float32
 BF16 = jnp.bfloat16
 ROWS = 8
-LOAD = 16
+LOAD = 32
 EDGES = 24
 EDGE_ROWS = 10
 TILES = 5

time: 43.2 us -> 43.2 us (level)
  no operation moved by 1% of the time
where the time goes in v15:
time: 43.2 us; the launch traced here: 43 us
  blocking collectives  23.7 us (55%)
  Pallas kernels  11.8 us (27%)
  starting transfers between devices  6.46 us (15%)
  between operations  0.67 us (2%)
    all_to_all x1, blocking collectives, local(): shares = lax.all_to_all(partial, 'row', 0, 0, tiled=True)  13.2 us
    pallas_call x5, Pallas kernels, call(): pl.pallas_call(kernel, out_shape=outs, in_specs=[pl.BlockSpec(memory_spac...  11.8 us
    all_to_all x1, blocking collectives, local(): values = lax.all_to_all(corrected, BOTH, 0, 0, tiled=True)  10.5 us
    ppermute x2, starting transfers between devices, swap(): return lax.ppermute(block, BOTH, pairs + [(j, i) for i, j in pairs])  6.46 us
  transfers between devices with their start and end apart: 2, of which 1 were waited for; matrix products, arithmetic and copies ran while one was open for 0% of the time, Pallas kernels for 6%

profile of v15, /device:TPU:0, one launch (start us, length us, event | category | flops | bytes accessed | tf_op | source)
XLA Modules:
  0.0 43.0 jit_solution(185071333963167435)
XLA Ops:
  0.6 4.0 %shard_map.95 = (f32[64,128]{1,0:T(8,128)S(1)}, f32[64,64,128]{2,1,0:T(8,128)S(1)}, f32[64,64,128]{2,1,0:T(8,128)S(1)}, f32[64,64,128]{2,1,0:T(8,128)S(1)}, bf16...) custom-call(f32[64,128]{1,0:T(8,128)} %rhs_in.1, ...), custom_call_target="tpu_custom_call" | custom-call | tf_op jit(solution)/shard_map/pallas_call | solution.py:555
  4.7 0.7 %collective-permute-start = (bf16[368,128]{1,0:T(8,128)(2,1)S(1)}, bf16[368,128]{1,0:T(8,128)(2,1)S(1)}, u32[]{:S(2)}, u32[]{:S(2)}) collective-permute-start(bf16[368,128]{1,0:T(8,128)(2,1)S(1)} %get-tuple-element.27.far), channel_id=1, source_target_pairs={{1,2},{3,4},{5,6},{7,8},{9,10},{11,12},{13,14},{15,16},{17,18},{19... | collective-permute-start | bytes 282632 | tf_op jit(solution)/shard_map/ppermute | solution.py:23
  5.3 5.8 %collective-permute-start.1 = (bf16[368,128]{1,0:T(8,128)(2,1)S(1)}, bf16[368,128]{1,0:T(8,128)(2,1)S(1)}, u32[]{:S(2)}, u32[]{:S(2)}) collective-permute-start(bf16[368,128]{1,0:T(8,128)(2,1)S(1)} %get-tuple-element.26.near), channel_id=1, source_target_pairs={{0,1},{2,3},{4,5},{6,7},{8,9},{10,11},{12,13},{14,15},{16,17},{18,... | collective-permute-start | bytes 282632 | tf_op jit(solution)/shard_map/ppermute | solution.py:23
  11.1 2.4 %shard_map.96 = (f32[64,128]{1,0:T(8,128)S(1)}, f32[64,128]{1,0:T(8,128)S(1)}, f32[22,64,64]{2,1,0:T(8,128)S(1)}) custom-call(f32[64,128]{1,0:T(8,128)S(1)} %get-tuple-element.19.rhs, f32[64,128]{1,0:T(8,128)S(1)} %get-tuple-element.20.trial, f32[64,64,128]{2,1,0:T(8,128)S(1)} %get-tuple-element.21.diag, f32[64,64,128]{2,1,0:T(8,128)S(1)} %get-tuple-element.22.inverse, ...), custom_call_target="tpu_custom_call" | custom-call | flops 4194304 | bytes 4194304 | tf_op jit(solution)/shard_map/pallas_call | solution.py:555
  13.5 0.0 collective-permute-done.far
  13.5 0.3 collective-permute-done.1.near
  13.9 1.0 %shard_map.97 = (f32[64,128]{1,0:T(8,128)S(1)}, f32[64,128]{1,0:T(8,128)S(1)}, f32[64,128]{1,0:T(8,128)S(1)}) custom-call(f32[64,128]{1,0:T(8,128)S(1)} %get-tuple-element.28.trial_partial, f32[64,128]{1,0:T(8,128)S(1)} %get-tuple-element.29.trial_twice, f32[22,64,64]{2,1,0:T(8,128)S(1)} %get-tuple-element.30.own, f32[24,64]{1,0:T(8,128)S(1)} %get-tuple-element.31.rows, ...), custom_call_target="tpu_custom_call" | custom-call | tf_op jit(solution)/shard_map/pallas_call | solution.py:555
  14.9 13.2 %all_to_all.22 = f32[8,8,128]{2,1,0:T(8,128)S(1)} all-to-all(f32[8,8,128]{2,1,0:T(8,128)S(1)} %bitcast.9), channel_id=1, replica_groups=mesh['grp'=4,'row'=8] {'row'}, dimensions={0} | all-to-all | bytes 65536 | tf_op jit(solution)/shard_map/all_to_all | solution.py:615
  28.1 0.3 shard_map.98
  28.5 10.5 %all_to_all.23 = f32[32,8,128]{2,1,0:T(8,128)S(1)} all-to-all(f32[32,8,128]{2,1,0:T(8,128)S(1)} %bitcast.7), channel_id=1, replica_groups=mesh['grp'=4,'row'=8] {'grp','row'}, dimensions={0} | all-to-all | bytes 262144 | tf_op jit(solution)/shard_map/all_to_all | solution.py:619
  38.9 4.0 %shard_map.99 = (f32[64,128]{1,0:T(8,128)}, f32[64,128]{1,0:T(8,128)}) custom-call(f32[64,128]{1,0:T(8,128)S(1)} %get-tuple-element.19.rhs, f32[64,128]{1,0:T(8,128)S(1)} %get-tuple-element.32.twice, f32[256,128]{1,0:T(8,128)S(1)} %bitcast.6, f32[64,64,128]{2,1,0:T(8,128)S(1)} %get-tuple-element.21.diag, f32[64,64,128]{2,1,0:T(8,128)S(1)} %get-tuple-element.22.inverse, ...), custom_call_target="tpu_custom_call" | custom-call | tf_op jit(solution)/shard_map/pallas_call | solution.py:555
Async XLA Ops:
  4.7 8.9 %collective-permute-start = (bf16[368,128]{1,0:T(8,128)(2,1)S(1)}, bf16[368,128]{1,0:T(8,128)(2,1)S(1)}, u32[]{:S(2)}, u32[]{:S(2)}) collective-permute-start(bf16[368,128]{1,0:T(8,128)(2,1)S(1)} %get-tuple-element.27.far), channel_id=1, source_target_pairs={{1,2},{3,4},{5,6},{7,8},{9,10},{11,12},{13,14},{15,16},{17,18},{19... | collective-permute-start | bytes 282632 | tf_op jit(solution)/shard_map/ppermute | solution.py:23
  5.3 8.5 %collective-permute-start.1 = (bf16[368,128]{1,0:T(8,128)(2,1)S(1)}, bf16[368,128]{1,0:T(8,128)(2,1)S(1)}, u32[]{:S(2)}, u32[]{:S(2)}) collective-permute-start(bf16[368,128]{1,0:T(8,128)(2,1)S(1)} %get-tuple-element.26.near), channel_id=1, source_target_pairs={{0,1},{2,3},{4,5},{6,7},{8,9},{10,11},{12,13},{14,15},{16,17},{18,... | collective-permute-start | bytes 282632 | tf_op jit(solution)/shard_map/ppermute | solution.py:23
